TPU v7x, 512 devices: a whole 4x4x16 slice. The times are simulated.
512 devices in a mesh: pencil: 32 (over z, core), gz: 4 (over x), coarse: 4 (over y).
Axes of the slice: x: 4, y: 4, z: 16, core: 2. Of those that a mesh axis runs over, the one named last changes fastest.
Arguments:
- right_side: float32 [256, 64, 1024], P('pencil', 'coarse', 'gz'), may hold values from -6 to 6
- conductivity: float32 [256, 64, 1024], P('pencil', 'coarse', 'gz'), may hold values from 0.2 to 5
- guess: float32 [256, 64, 1024], P('pencil', 'coarse', 'gz'), may hold values from -4 to 4
Outputs:
- updated: float32 [256, 64, 1024], P('pencil', 'coarse', 'gz')
- smoothed_residual: float32 [256, 64, 1024], P('pencil', 'coarse', 'gz')
All inputs are finite; a program needn't handle non-finite values.
Results may differ from a plain program's by a relative error of at most 0.00002.
Values sent between devices are 32-bit elements; how exact they have to be, the bound alone decides.
No kernel may reach another device: no remote copies, remote signals or barrier semaphores. Data moves between devices by JAX's collectives and lax.ppermute only.
A program may use at most 64 MiB of HBM per device.

v0:
```python
import jax
import jax.numpy as jnp
from jax import lax
from jax.sharding import PartitionSpec as P

KSWEEP = 4


def padded_2(cells, sides, width):
    for axis, dim in sides:
        count = lax.axis_size(axis)
        ends = count - 1
        head = lax.slice_in_dim(cells, 0, width, axis=dim)
        tail = lax.slice_in_dim(cells, cells.shape[dim] - width, cells.shape[dim], axis=dim)
        cells = jnp.concatenate(
            [
                lax.ppermute(tail, axis, [(i, (i + 1) % count) for i in range(ends)]),
                cells,
                lax.ppermute(head, axis, [((i + 1) % count, i) for i in range(ends)]),
            ],
            axis=dim,
        )
    return cells


def face_terms(padded_k, scale):
    k = padded_k[1:-1, 1:-1, 1:-1]
    return [
        scale * 0.5 * (k + padded_k[:-2, 1:-1, 1:-1]),
        scale * 0.5 * (k + padded_k[2:, 1:-1, 1:-1]),
        scale * 0.5 * (k + padded_k[1:-1, :-2, 1:-1]),
        scale * 0.5 * (k + padded_k[1:-1, 2:, 1:-1]),
        scale * 0.5 * (k + padded_k[1:-1, 1:-1, :-2]),
        scale * 0.5 * (k + padded_k[1:-1, 1:-1, 2:]),
    ]


def diagonal_of(terms):
    return terms[0] + terms[1] + terms[2] + terms[3] + terms[4] + terms[5]


def operate(padded_v, terms, diag):
    v = padded_v[1:-1, 1:-1, 1:-1]
    out = diag * v - terms[0] * padded_v[:-2, 1:-1, 1:-1] - terms[1] * padded_v[2:, 1:-1, 1:-1]
    out = out - terms[2] * padded_v[1:-1, :-2, 1:-1] - terms[3] * padded_v[1:-1, 2:, 1:-1]
    return out - terms[4] * padded_v[1:-1, 1:-1, :-2] - terms[5] * padded_v[1:-1, 1:-1, 2:]


def restrict(field):
    a, b, c = field.shape
    return field.reshape(a // 2, 2, b // 2, 2, c // 2, 2).mean(axis=(1, 3, 5))


def extend_faces(stacked):
    return padded_2(stacked, (("pencil", 1), ("gz", 3), ("coarse", 2)), 1)


def extend_blocked(stacked):
    return padded_2(stacked, (("pencil", 1), ("gz", 3), ("coarse", 2)), 1)


def coarse_solve(coarse_r, coarse_k, extend):
    cterms = face_terms(extend(coarse_k[None])[0], 0.25)
    dcoarse = diagonal_of(cterms)
    correction = 0.8 * coarse_r / dcoarse
    for sweep in range(KSWEEP - 1):
        padded = extend(correction[None])[0]
        correction = correction + 0.8 * (coarse_r - operate(padded, cterms, dcoarse)) / dcoarse
    return correction


def on_device(right_side, conductivity, guess):
    theta = 1.1
    delta = 0.8
    sigma = theta / delta
    rho0 = 1.0 / sigma
    rho1 = 1.0 / (2.0 * sigma - rho0)
    first = extend_faces(jnp.stack([guess, conductivity]))
    terms = face_terms(first[1], 1.0)
    dfine = diagonal_of(terms)
    r0 = right_side - operate(first[0], terms, dfine)
    d0 = r0 / (theta * dfine)
    r1 = r0 - operate(extend_faces(d0[None])[0], terms, dfine)
    d1 = rho1 * rho0 * d0 + 2.0 * rho1 / delta * r1 / dfine
    smoothed = r1 - operate(extend_faces(d1[None])[0], terms, dfine)
    coarse_r = restrict(r0)
    coarse_k = restrict(conductivity)
    correction = coarse_solve(coarse_r, coarse_k, extend_blocked)
    lifted = jnp.repeat(jnp.repeat(jnp.repeat(correction, 2, axis=0), 2, axis=1), 2, axis=2)
    updated = guess + d0 + d1 + lifted
    return (updated, smoothed)


def solution(mesh):
    return jax.shard_map(
        on_device,
        mesh=mesh,
        in_specs=(
            P("pencil", "coarse", "gz"),
            P("pencil", "coarse", "gz"),
            P("pencil", "coarse", "gz"),
        ),
        out_specs=(P("pencil", "coarse", "gz"), P("pencil", "coarse", "gz")),
        check_vma=False,
    )
```

profile of v0, /device:TPU:128, one launch (start us, length us, event | category | flops | bytes accessed | tf_op | source)
XLA Modules:
  0.0 187.2 jit_solution(6826554219576936224)
XLA Ops:
  0.6 10.6 %reshape.29 = f32[4,2,8,2,128,2]{5,4,3,2,1,0:T(8,128)} reshape(f32[8,16,256]{2,1,0:T(8,128)} %param.4) | data formatting | bytes 262144 | tf_op jit(solution)/shard_map/reshape | solution.py:51
  11.2 4.1 %reduce_sum.19 = f32[4,8,128]{2,1,0:T(8,128)S(1)} reduce(f32[4,2,8,2,128,2]{5,4,3,2,1,0:T(8,128)} %reshape.29, f32[]{:T(128)} %constant.7.clone.1), dimensions={1,3,5}, to_apply=%region_1.0 | reduce | flops 28672 | bytes 147460 | tf_op jit(solution)/shard_map/reduce_sum | solution.py:51
  15.3 1.9 %collective-permute-start.12 = (f32[1,1,8,128]{3,2,1,0:T(8,128)S(1)}, f32[1,1,8,128]{3,2,1,0:T(8,128)S(1)}, u32[]{:S(2)}, u32[]{:S(2)}) collective-permute-start(f32[1,1,8,128]{3,2,1,0:T(8,128)S(1)} %get-tuple-element.72), channel_id=1, source_target_pairs={{0,16},{16,32},{32,48},{48,64},{64,80},{80,96},{96,112},{112,128},... | collective-permute-start | bytes 12296 | tf_op jit(solution)/shard_map/ppermute | solution.py:17
  17.2 4.9 %collective-permute-start.13 = (f32[1,1,8,128]{3,2,1,0:T(8,128)S(1)}, f32[1,1,8,128]{3,2,1,0:T(8,128)S(1)}, u32[]{:S(2)}, u32[]{:S(2)}) collective-permute-start(f32[1,1,8,128]{3,2,1,0:T(8,128)S(1)} %get-tuple-element.73), channel_id=1, source_target_pairs={{16,0},{32,16},{48,32},{64,48},{80,64},{96,80},{112,96},{128,112},... | collective-permute-start | bytes 12296 | tf_op jit(solution)/shard_map/ppermute | solution.py:19
  22.1 1.9 %collective-permute-start = (f32[2,1,16,256]{3,2,1,0:T(8,128)S(1)}, f32[2,1,16,256]{3,2,1,0:T(8,128)S(1)}, u32[]{:S(2)}, u32[]{:S(2)}) collective-permute-start(f32[2,1,16,256]{3,2,1,0:T(8,128)S(1)} %get-tuple-element.40), channel_id=1, source_target_pairs={{0,16},{16,32},{32,48},{48,64},{64,80},{80,96},{96,112},{112,128},... | collective-permute-start | bytes 98312 | tf_op jit(solution)/shard_map/ppermute | solution.py:17
  24.0 4.9 %collective-permute-start.1 = (f32[2,1,16,256]{3,2,1,0:T(8,128)S(1)}, f32[2,1,16,256]{3,2,1,0:T(8,128)S(1)}, u32[]{:S(2)}, u32[]{:S(2)}) collective-permute-start(f32[2,1,16,256]{3,2,1,0:T(8,128)S(1)} %get-tuple-element.41), channel_id=1, source_target_pairs={{16,0},{32,16},{48,32},{64,48},{80,64},{96,80},{112,96},{128,112},... | collective-permute-start | bytes 98312 | tf_op jit(solution)/shard_map/ppermute | solution.py:19
  29.0 3.4 %collective-permute-start.14 = (f32[1,6,8,1]{3,2,1,0:T(8,128)S(1)}, f32[1,6,8,1]{3,2,1,0:T(8,128)S(1)}, u32[]{:S(2)}, u32[]{:S(2)}) collective-permute-start(f32[1,6,8,1]{3,2,1,0:T(8,128)S(1)} %get-tuple-element.64), channel_id=1, source_target_pairs={{0,4},{4,8},{8,12},{1,5},{5,9},{9,13},{2,6},{6,10},{10,14},{3,7},{... | collective-permute-start | bytes 584 | tf_op jit(solution)/shard_map/ppermute | solution.py:17
  32.4 1.3 collective-permute-start.15
  33.9 4.6 %collective-permute-start.2 = (f32[2,10,16,1]{3,2,1,0:T(8,128)S(1)}, f32[2,10,16,1]{3,2,1,0:T(8,128)S(1)}, u32[]{:S(2)}, u32[]{:S(2)}) collective-permute-start(f32[2,10,16,1]{3,2,1,0:T(8,128)S(1)} %get-tuple-element.36), channel_id=1, source_target_pairs={{0,4},{4,8},{8,12},{1,5},{5,9},{9,13},{2,6},{6,10},{10,14},{3,7},{... | collective-permute-start | bytes 3848 | tf_op jit(solution)/shard_map/ppermute | solution.py:17
  38.4 1.3 collective-permute-start.3
  39.9 3.5 %collective-permute-start.16 = (f32[1,6,1,130]{3,2,1,0:T(1,128)S(1)}, f32[1,6,1,130]{3,2,1,0:T(1,128)S(1)}, u32[]{:S(2)}, u32[]{:S(2)}) collective-permute-start(f32[1,6,1,130]{3,2,1,0:T(1,128)S(1)} %get-tuple-element.56), channel_id=1, source_target_pairs={{0,1},{1,2},{2,3},{4,5},{5,6},{6,7},{8,9},{9,10},{10,11},{12,13},{... | collective-permute-start | bytes 9368 | tf_op jit(solution)/shard_map/ppermute | solution.py:17
  43.4 1.3 collective-permute-start.17
  45.9 3.6 %collective-permute-start.4 = (f32[2,10,1,258]{3,0,2,1:T(2,128)S(1)}, f32[2,10,1,258]{3,0,2,1:T(2,128)S(1)}, u32[]{:S(2)}, u32[]{:S(2)}) collective-permute-start(f32[2,10,1,258]{3,0,2,1:T(2,128)S(1)} %copy.77), channel_id=1, source_target_pairs={{0,1},{1,2},{2,3},{4,5},{5,6},{6,7},{8,9},{9,10},{10,11},{12,13},{... | collective-permute-start | bytes 61928 | tf_op jit(solution)/shard_map/ppermute | solution.py:17
  49.5 1.3 collective-permute-start.5
  51.1 4.2 %collective-permute-done.5 = f32[2,10,1,258]{3,0,2,1:T(2,128)S(1)} collective-permute-done((f32[2,10,1,258]{3,0,2,1:T(2,128)S(1)}, f32[2,10,1,258]{3,0,2,1:T(2,128)S(1)}, u32[]{:S(2)}, u32[]{:S(2)}) %collective-permute-start.5) | collective-permute-done | bytes 20672 | tf_op jit(solution)/shard_map/ppermute | solution.py:19
  56.2 9.8 %reshape.28 = f32[4,2,8,2,128,2]{5,4,3,2,1,0:T(8,128)} reshape(f32[8,16,256]{2,1,0:T(8,128)S(1)} %get-tuple-element.13) | data formatting | bytes 262144 | tf_op jit(solution)/shard_map/reshape | solution.py:51
  66.0 4.0 %reduce_sum.18 = f32[4,8,128]{2,1,0:T(8,128)S(1)} reduce(f32[4,2,8,2,128,2]{5,4,3,2,1,0:T(8,128)} %reshape.28, f32[]{:T(128)} %constant.7.clone.1), dimensions={1,3,5}, to_apply=%region_0.0 | reduce | flops 28672 | bytes 147460 | tf_op jit(solution)/shard_map/reduce_sum | solution.py:51
  70.2 1.9 %collective-permute-start.18 = (f32[1,1,8,128]{3,2,1,0:T(8,128)S(1)}, f32[1,1,8,128]{3,2,1,0:T(8,128)S(1)}, u32[]{:S(2)}, u32[]{:S(2)}) collective-permute-start(f32[1,1,8,128]{3,2,1,0:T(8,128)S(1)} %get-tuple-element.70), channel_id=1, source_target_pairs={{0,16},{16,32},{32,48},{48,64},{64,80},{80,96},{96,112},{112,128},... | collective-permute-start | bytes 12296 | tf_op jit(solution)/shard_map/ppermute | solution.py:17
  72.1 4.9 %collective-permute-start.19 = (f32[1,1,8,128]{3,2,1,0:T(8,128)S(1)}, f32[1,1,8,128]{3,2,1,0:T(8,128)S(1)}, u32[]{:S(2)}, u32[]{:S(2)}) collective-permute-start(f32[1,1,8,128]{3,2,1,0:T(8,128)S(1)} %get-tuple-element.71), channel_id=1, source_target_pairs={{16,0},{32,16},{48,32},{64,48},{80,64},{96,80},{112,96},{128,112},... | collective-permute-start | bytes 12296 | tf_op jit(solution)/shard_map/ppermute | solution.py:19
  77.0 1.3 collective-permute-done.19
  78.3 4.5 %collective-permute-start.20 = (f32[1,6,8,1]{3,2,1,0:T(8,128)S(1)}, f32[1,6,8,1]{3,2,1,0:T(8,128)S(1)}, u32[]{:S(2)}, u32[]{:S(2)}) collective-permute-start(f32[1,6,8,1]{3,2,1,0:T(8,128)S(1)} %get-tuple-element.62), channel_id=1, source_target_pairs={{0,4},{4,8},{8,12},{1,5},{5,9},{9,13},{2,6},{6,10},{10,14},{3,7},{... | collective-permute-start | bytes 584 | tf_op jit(solution)/shard_map/ppermute | solution.py:17
  84.4 4.2 %collective-permute-done.21 = f32[1,6,8,1]{3,2,1,0:T(8,128)S(1)} collective-permute-done((f32[1,6,8,1]{3,2,1,0:T(8,128)S(1)}, f32[1,6,8,1]{3,2,1,0:T(8,128)S(1)}, u32[]{:S(2)}, u32[]{:S(2)}) %collective-permute-start.21) | collective-permute-done | bytes 224 | tf_op jit(solution)/shard_map/ppermute | solution.py:19
  88.7 3.5 %collective-permute-start.22 = (f32[1,6,1,130]{3,2,1,0:T(1,128)S(1)}, f32[1,6,1,130]{3,2,1,0:T(1,128)S(1)}, u32[]{:S(2)}, u32[]{:S(2)}) collective-permute-start(f32[1,6,1,130]{3,2,1,0:T(1,128)S(1)} %get-tuple-element.54), channel_id=1, source_target_pairs={{0,1},{1,2},{2,3},{4,5},{5,6},{6,7},{8,9},{9,10},{10,11},{12,13},{... | collective-permute-start | bytes 9368 | tf_op jit(solution)/shard_map/ppermute | solution.py:17
  93.5 4.2 %collective-permute-done.23 = f32[1,6,1,130]{3,2,1,0:T(1,128)S(1)} collective-permute-done((f32[1,6,1,130]{3,2,1,0:T(1,128)S(1)}, f32[1,6,1,130]{3,2,1,0:T(1,128)S(1)}, u32[]{:S(2)}, u32[]{:S(2)}) %collective-permute-start.23) | collective-permute-done | bytes 3152 | tf_op jit(solution)/shard_map/ppermute | solution.py:19
  98.0 1.9 %collective-permute-start.24 = (f32[1,1,8,128]{3,2,1,0:T(8,128)S(1)}, f32[1,1,8,128]{3,2,1,0:T(8,128)S(1)}, u32[]{:S(2)}, u32[]{:S(2)}) collective-permute-start(f32[1,1,8,128]{3,2,1,0:T(8,128)S(1)} %get-tuple-element.68), channel_id=1, source_target_pairs={{0,16},{16,32},{32,48},{48,64},{64,80},{80,96},{96,112},{112,128},... | collective-permute-start | bytes 12296 | tf_op jit(solution)/shard_map/ppermute | solution.py:17
  99.9 4.9 %collective-permute-start.25 = (f32[1,1,8,128]{3,2,1,0:T(8,128)S(1)}, f32[1,1,8,128]{3,2,1,0:T(8,128)S(1)}, u32[]{:S(2)}, u32[]{:S(2)}) collective-permute-start(f32[1,1,8,128]{3,2,1,0:T(8,128)S(1)} %get-tuple-element.69), channel_id=1, source_target_pairs={{16,0},{32,16},{48,32},{64,48},{80,64},{96,80},{112,96},{128,112},... | collective-permute-start | bytes 12296 | tf_op jit(solution)/shard_map/ppermute | solution.py:19
  104.8 1.3 collective-permute-done.25
  106.1 3.4 %collective-permute-start.26 = (f32[1,6,8,1]{3,2,1,0:T(8,128)S(1)}, f32[1,6,8,1]{3,2,1,0:T(8,128)S(1)}, u32[]{:S(2)}, u32[]{:S(2)}) collective-permute-start(f32[1,6,8,1]{3,2,1,0:T(8,128)S(1)} %get-tuple-element.60), channel_id=1, source_target_pairs={{0,4},{4,8},{8,12},{1,5},{5,9},{9,13},{2,6},{6,10},{10,14},{3,7},{... | collective-permute-start | bytes 584 | tf_op jit(solution)/shard_map/ppermute | solution.py:17
  111.0 4.2 %collective-permute-done.27 = f32[1,6,8,1]{3,2,1,0:T(8,128)S(1)} collective-permute-done((f32[1,6,8,1]{3,2,1,0:T(8,128)S(1)}, f32[1,6,8,1]{3,2,1,0:T(8,128)S(1)}, u32[]{:S(2)}, u32[]{:S(2)}) %collective-permute-start.27) | collective-permute-done | bytes 224 | tf_op jit(solution)/shard_map/ppermute | solution.py:19
  115.4 3.2 %collective-permute-start.28 = (f32[1,6,1,130]{3,2,1,0:T(1,128)S(1)}, f32[1,6,1,130]{3,2,1,0:T(1,128)S(1)}, u32[]{:S(2)}, u32[]{:S(2)}) collective-permute-start(f32[1,6,1,130]{3,2,1,0:T(1,128)S(1)} %get-tuple-element.52), channel_id=1, source_target_pairs={{0,1},{1,2},{2,3},{4,5},{5,6},{6,7},{8,9},{9,10},{10,11},{12,13},{... | collective-permute-start | bytes 9368 | tf_op jit(solution)/shard_map/ppermute | solution.py:17
  118.6 1.3 collective-permute-start.29
  119.9 1.9 %collective-permute-start.6 = (f32[1,1,16,256]{3,2,1,0:T(8,128)S(1)}, f32[1,1,16,256]{3,2,1,0:T(8,128)S(1)}, u32[]{:S(2)}, u32[]{:S(2)}) collective-permute-start(f32[1,1,16,256]{3,2,1,0:T(8,128)S(1)} %get-tuple-element.48), channel_id=1, source_target_pairs={{0,16},{16,32},{32,48},{48,64},{64,80},{80,96},{96,112},{112,128},... | collective-permute-start | bytes 49160 | tf_op jit(solution)/shard_map/ppermute | solution.py:17
  121.8 4.9 %collective-permute-start.7 = (f32[1,1,16,256]{3,2,1,0:T(8,128)S(1)}, f32[1,1,16,256]{3,2,1,0:T(8,128)S(1)}, u32[]{:S(2)}, u32[]{:S(2)}) collective-permute-start(f32[1,1,16,256]{3,2,1,0:T(8,128)S(1)} %get-tuple-element.49), channel_id=1, source_target_pairs={{16,0},{32,16},{48,32},{64,48},{80,64},{96,80},{112,96},{128,112},... | collective-permute-start | bytes 49160 | tf_op jit(solution)/shard_map/ppermute | solution.py:19
  128.2 3.1 %collective-permute-start.8 = (f32[1,10,16,1]{3,2,1,0:T(8,128)S(1)}, f32[1,10,16,1]{3,2,1,0:T(8,128)S(1)}, u32[]{:S(2)}, u32[]{:S(2)}) collective-permute-start(f32[1,10,16,1]{3,2,1,0:T(8,128)S(1)} %get-tuple-element.44), channel_id=1, source_target_pairs={{0,4},{4,8},{8,12},{1,5},{5,9},{9,13},{2,6},{6,10},{10,14},{3,7},{... | collective-permute-start | bytes 1928 | tf_op jit(solution)/shard_map/ppermute | solution.py:17
  131.3 1.3 collective-permute-start.9
  132.6 1.9 %collective-permute-start.30 = (f32[1,1,8,128]{3,2,1,0:T(8,128)S(1)}, f32[1,1,8,128]{3,2,1,0:T(8,128)S(1)}, u32[]{:S(2)}, u32[]{:S(2)}) collective-permute-start(f32[1,1,8,128]{3,2,1,0:T(8,128)S(1)} %get-tuple-element.66), channel_id=1, source_target_pairs={{0,16},{16,32},{32,48},{48,64},{64,80},{80,96},{96,112},{112,128},... | collective-permute-start | bytes 12296 | tf_op jit(solution)/shard_map/ppermute | solution.py:17
  134.5 4.9 %collective-permute-start.31 = (f32[1,1,8,128]{3,2,1,0:T(8,128)S(1)}, f32[1,1,8,128]{3,2,1,0:T(8,128)S(1)}, u32[]{:S(2)}, u32[]{:S(2)}) collective-permute-start(f32[1,1,8,128]{3,2,1,0:T(8,128)S(1)} %get-tuple-element.67), channel_id=1, source_target_pairs={{16,0},{32,16},{48,32},{64,48},{80,64},{96,80},{112,96},{128,112},... | collective-permute-start | bytes 12296 | tf_op jit(solution)/shard_map/ppermute | solution.py:19
  139.6 4.5 %collective-permute-start.10 = (f32[1,10,1,258]{3,2,1,0:T(1,128)S(1)}, f32[1,10,1,258]{3,2,1,0:T(1,128)S(1)}, u32[]{:S(2)}, u32[]{:S(2)}) collective-permute-start(f32[1,10,1,258]{3,2,1,0:T(1,128)S(1)} %get-tuple-element.34), channel_id=1, source_target_pairs={{0,1},{1,2},{2,3},{4,5},{5,6},{6,7},{8,9},{9,10},{10,11},{12,13},{... | collective-permute-start | bytes 30968 | tf_op jit(solution)/shard_map/ppermute | solution.py:17
  145.5 4.5 %collective-permute-start.32 = (f32[1,6,8,1]{3,2,1,0:T(8,128)S(1)}, f32[1,6,8,1]{3,2,1,0:T(8,128)S(1)}, u32[]{:S(2)}, u32[]{:S(2)}) collective-permute-start(f32[1,6,8,1]{3,2,1,0:T(8,128)S(1)} %get-tuple-element.58), channel_id=1, source_target_pairs={{0,4},{4,8},{8,12},{1,5},{5,9},{9,13},{2,6},{6,10},{10,14},{3,7},{... | collective-permute-start | bytes 584 | tf_op jit(solution)/shard_map/ppermute | solution.py:17
  150.1 1.3 collective-permute-start.33
  151.9 1.9 %collective-permute-start.36 = (f32[1,1,16,256]{3,2,1,0:T(8,128)S(1)}, f32[1,1,16,256]{3,2,1,0:T(8,128)S(1)}, u32[]{:S(2)}, u32[]{:S(2)}) collective-permute-start(f32[1,1,16,256]{3,2,1,0:T(8,128)S(1)} %get-tuple-element.46), channel_id=1, source_target_pairs={{0,16},{16,32},{32,48},{48,64},{64,80},{80,96},{96,112},{112,128},... | collective-permute-start | bytes 49160 | tf_op jit(solution)/shard_map/ppermute | solution.py:17
  153.8 4.9 %collective-permute-start.37 = (f32[1,1,16,256]{3,2,1,0:T(8,128)S(1)}, f32[1,1,16,256]{3,2,1,0:T(8,128)S(1)}, u32[]{:S(2)}, u32[]{:S(2)}) collective-permute-start(f32[1,1,16,256]{3,2,1,0:T(8,128)S(1)} %get-tuple-element.47), channel_id=1, source_target_pairs={{16,0},{32,16},{48,32},{64,48},{80,64},{96,80},{112,96},{128,112},... | collective-permute-start | bytes 49160 | tf_op jit(solution)/shard_map/ppermute | solution.py:19
  158.8 4.5 %collective-permute-start.34 = (f32[1,6,1,130]{3,2,1,0:T(1,128)S(1)}, f32[1,6,1,130]{3,2,1,0:T(1,128)S(1)}, u32[]{:S(2)}, u32[]{:S(2)}) collective-permute-start(f32[1,6,1,130]{3,2,1,0:T(1,128)S(1)} %get-tuple-element.50), channel_id=1, source_target_pairs={{0,1},{1,2},{2,3},{4,5},{5,6},{6,7},{8,9},{9,10},{10,11},{12,13},{... | collective-permute-start | bytes 9368 | tf_op jit(solution)/shard_map/ppermute | solution.py:17
  163.4 1.3 collective-permute-start.35
  164.8 4.6 %collective-permute-start.38 = (f32[1,10,16,1]{3,2,1,0:T(8,128)S(1)}, f32[1,10,16,1]{3,2,1,0:T(8,128)S(1)}, u32[]{:S(2)}, u32[]{:S(2)}) collective-permute-start(f32[1,10,16,1]{3,2,1,0:T(8,128)S(1)} %get-tuple-element.42), channel_id=1, source_target_pairs={{0,4},{4,8},{8,12},{1,5},{5,9},{9,13},{2,6},{6,10},{10,14},{3,7},{... | collective-permute-start | bytes 1928 | tf_op jit(solution)/shard_map/ppermute | solution.py:17
  171.4 4.3 %collective-permute-done.39 = f32[1,10,16,1]{3,2,1,0:T(8,128)S(1)} collective-permute-done((f32[1,10,16,1]{3,2,1,0:T(8,128)S(1)}, f32[1,10,16,1]{3,2,1,0:T(8,128)S(1)}, u32[]{:S(2)}, u32[]{:S(2)}) %collective-permute-start.39) | collective-permute-done | bytes 672 | tf_op jit(solution)/shard_map/ppermute | solution.py:19
  175.9 4.5 %collective-permute-start.40 = (f32[1,10,1,258]{3,2,1,0:T(1,128)S(1)}, f32[1,10,1,258]{3,2,1,0:T(1,128)S(1)}, u32[]{:S(2)}, u32[]{:S(2)}) collective-permute-start(f32[1,10,1,258]{3,2,1,0:T(1,128)S(1)} %get-tuple-element.32), channel_id=1, source_target_pairs={{0,1},{1,2},{2,3},{4,5},{5,6},{6,7},{8,9},{9,10},{10,11},{12,13},{... | collective-permute-start | bytes 30968 | tf_op jit(solution)/shard_map/ppermute | solution.py:17
  182.6 3.5 %collective-permute-done.41 = f32[1,10,1,258]{3,2,1,0:T(1,128)S(1)} collective-permute-done((f32[1,10,1,258]{3,2,1,0:T(1,128)S(1)}, f32[1,10,1,258]{3,2,1,0:T(1,128)S(1)}, u32[]{:S(2)}, u32[]{:S(2)}) %collective-permute-start.41) | collective-permute-done | bytes 10352 | tf_op jit(solution)/shard_map/ppermute | solution.py:19
  (100 shorter events, 16.9 us)
Async XLA Ops:
  0.6 21.5 %copy-start = (f32[8,16,256]{2,1,0:T(8,128)S(1)}, f32[8,16,256]{2,1,0:T(8,128)}, u32[]{:S(2)}) copy-start(f32[8,16,256]{2,1,0:T(8,128)} %param.4) | copy-start | bytes 393220
  0.6 21.5 %copy-start.1 = (f32[8,16,256]{2,1,0:T(8,128)S(1)}, f32[8,16,256]{2,1,0:T(8,128)}, u32[]{:S(2)}) copy-start(f32[8,16,256]{2,1,0:T(8,128)} %param.5) | copy-start | bytes 393220
  11.2 44.5 %copy-start.2 = (f32[8,16,256]{2,1,0:T(8,128)S(1)}, f32[8,16,256]{2,1,0:T(8,128)}, u32[]{:S(2)}) copy-start(f32[8,16,256]{2,1,0:T(8,128)} %param.3) | copy-start | bytes 393220
  15.3 13.6 %collective-permute-start.12 = (f32[1,1,8,128]{3,2,1,0:T(8,128)S(1)}, f32[1,1,8,128]{3,2,1,0:T(8,128)S(1)}, u32[]{:S(2)}, u32[]{:S(2)}) collective-permute-start(f32[1,1,8,128]{3,2,1,0:T(8,128)S(1)} %get-tuple-element.72), channel_id=1, source_target_pairs={{0,16},{16,32},{32,48},{48,64},{64,80},{80,96},{96,112},{112,128},... | collective-permute-start | bytes 12296 | tf_op jit(solution)/shard_map/ppermute | solution.py:17
  17.2 11.7 %collective-permute-start.13 = (f32[1,1,8,128]{3,2,1,0:T(8,128)S(1)}, f32[1,1,8,128]{3,2,1,0:T(8,128)S(1)}, u32[]{:S(2)}, u32[]{:S(2)}) collective-permute-start(f32[1,1,8,128]{3,2,1,0:T(8,128)S(1)} %get-tuple-element.73), channel_id=1, source_target_pairs={{16,0},{32,16},{48,32},{64,48},{80,64},{96,80},{112,96},{128,112},... | collective-permute-start | bytes 12296 | tf_op jit(solution)/shard_map/ppermute | solution.py:19
  22.1 11.6 %collective-permute-start = (f32[2,1,16,256]{3,2,1,0:T(8,128)S(1)}, f32[2,1,16,256]{3,2,1,0:T(8,128)S(1)}, u32[]{:S(2)}, u32[]{:S(2)}) collective-permute-start(f32[2,1,16,256]{3,2,1,0:T(8,128)S(1)} %get-tuple-element.40), channel_id=1, source_target_pairs={{0,16},{16,32},{32,48},{48,64},{64,80},{80,96},{96,112},{112,128},... | collective-permute-start | bytes 98312 | tf_op jit(solution)/shard_map/ppermute | solution.py:17
  24.0 9.7 %collective-permute-start.1 = (f32[2,1,16,256]{3,2,1,0:T(8,128)S(1)}, f32[2,1,16,256]{3,2,1,0:T(8,128)S(1)}, u32[]{:S(2)}, u32[]{:S(2)}) collective-permute-start(f32[2,1,16,256]{3,2,1,0:T(8,128)S(1)} %get-tuple-element.41), channel_id=1, source_target_pairs={{16,0},{32,16},{48,32},{64,48},{80,64},{96,80},{112,96},{128,112},... | collective-permute-start | bytes 98312 | tf_op jit(solution)/shard_map/ppermute | solution.py:19
  29.0 10.7 %collective-permute-start.14 = (f32[1,6,8,1]{3,2,1,0:T(8,128)S(1)}, f32[1,6,8,1]{3,2,1,0:T(8,128)S(1)}, u32[]{:S(2)}, u32[]{:S(2)}) collective-permute-start(f32[1,6,8,1]{3,2,1,0:T(8,128)S(1)} %get-tuple-element.64), channel_id=1, source_target_pairs={{0,4},{4,8},{8,12},{1,5},{5,9},{9,13},{2,6},{6,10},{10,14},{3,7},{... | collective-permute-start | bytes 584 | tf_op jit(solution)/shard_map/ppermute | solution.py:17
  32.4 7.3 %collective-permute-start.15 = (f32[1,6,8,1]{3,2,1,0:T(8,128)S(1)}, f32[1,6,8,1]{3,2,1,0:T(8,128)S(1)}, u32[]{:S(2)}, u32[]{:S(2)}) collective-permute-start(f32[1,6,8,1]{3,2,1,0:T(8,128)S(1)} %get-tuple-element.65), channel_id=1, source_target_pairs={{4,0},{8,4},{12,8},{5,1},{9,5},{13,9},{6,2},{10,6},{14,10},{7,3},{... | collective-permute-start | bytes 584 | tf_op jit(solution)/shard_map/ppermute | solution.py:19
  33.9 10.8 %collective-permute-start.2 = (f32[2,10,16,1]{3,2,1,0:T(8,128)S(1)}, f32[2,10,16,1]{3,2,1,0:T(8,128)S(1)}, u32[]{:S(2)}, u32[]{:S(2)}) collective-permute-start(f32[2,10,16,1]{3,2,1,0:T(8,128)S(1)} %get-tuple-element.36), channel_id=1, source_target_pairs={{0,4},{4,8},{8,12},{1,5},{5,9},{9,13},{2,6},{6,10},{10,14},{3,7},{... | collective-permute-start | bytes 3848 | tf_op jit(solution)/shard_map/ppermute | solution.py:17
  38.4 7.2 %collective-permute-start.3 = (f32[2,10,16,1]{3,2,1,0:T(8,128)S(1)}, f32[2,10,16,1]{3,2,1,0:T(8,128)S(1)}, u32[]{:S(2)}, u32[]{:S(2)}) collective-permute-start(f32[2,10,16,1]{3,2,1,0:T(8,128)S(1)} %get-tuple-element.37), channel_id=1, source_target_pairs={{4,0},{8,4},{12,8},{5,1},{9,5},{13,9},{6,2},{10,6},{14,10},{7,3},{... | collective-permute-start | bytes 3848 | tf_op jit(solution)/shard_map/ppermute | solution.py:19
  39.9 11.0 %collective-permute-start.16 = (f32[1,6,1,130]{3,2,1,0:T(1,128)S(1)}, f32[1,6,1,130]{3,2,1,0:T(1,128)S(1)}, u32[]{:S(2)}, u32[]{:S(2)}) collective-permute-start(f32[1,6,1,130]{3,2,1,0:T(1,128)S(1)} %get-tuple-element.56), channel_id=1, source_target_pairs={{0,1},{1,2},{2,3},{4,5},{5,6},{6,7},{8,9},{9,10},{10,11},{12,13},{... | collective-permute-start | bytes 9368 | tf_op jit(solution)/shard_map/ppermute | solution.py:17
  43.4 7.5 %collective-permute-start.17 = (f32[1,6,1,130]{3,2,1,0:T(1,128)S(1)}, f32[1,6,1,130]{3,2,1,0:T(1,128)S(1)}, u32[]{:S(2)}, u32[]{:S(2)}) collective-permute-start(f32[1,6,1,130]{3,2,1,0:T(1,128)S(1)} %get-tuple-element.57), channel_id=1, source_target_pairs={{1,0},{2,1},{3,2},{5,4},{6,5},{7,6},{9,8},{10,9},{11,10},{13,12},{... | collective-permute-start | bytes 9368 | tf_op jit(solution)/shard_map/ppermute | solution.py:19
  45.9 5.1 %collective-permute-start.4 = (f32[2,10,1,258]{3,0,2,1:T(2,128)S(1)}, f32[2,10,1,258]{3,0,2,1:T(2,128)S(1)}, u32[]{:S(2)}, u32[]{:S(2)}) collective-permute-start(f32[2,10,1,258]{3,0,2,1:T(2,128)S(1)} %copy.77), channel_id=1, source_target_pairs={{0,1},{1,2},{2,3},{4,5},{5,6},{6,7},{8,9},{9,10},{10,11},{12,13},{... | collective-permute-start | bytes 61928 | tf_op jit(solution)/shard_map/ppermute | solution.py:17
  49.5 5.8 %collective-permute-start.5 = (f32[2,10,1,258]{3,0,2,1:T(2,128)S(1)}, f32[2,10,1,258]{3,0,2,1:T(2,128)S(1)}, u32[]{:S(2)}, u32[]{:S(2)}) collective-permute-start(f32[2,10,1,258]{3,0,2,1:T(2,128)S(1)} %copy.78), channel_id=1, source_target_pairs={{1,0},{2,1},{3,2},{5,4},{6,5},{7,6},{9,8},{10,9},{11,10},{13,12},{... | collective-permute-start | bytes 61928 | tf_op jit(solution)/shard_map/ppermute | solution.py:19
  70.2 6.8 %collective-permute-start.18 = (f32[1,1,8,128]{3,2,1,0:T(8,128)S(1)}, f32[1,1,8,128]{3,2,1,0:T(8,128)S(1)}, u32[]{:S(2)}, u32[]{:S(2)}) collective-permute-start(f32[1,1,8,128]{3,2,1,0:T(8,128)S(1)} %get-tuple-element.70), channel_id=1, source_target_pairs={{0,16},{16,32},{32,48},{48,64},{64,80},{80,96},{96,112},{112,128},... | collective-permute-start | bytes 12296 | tf_op jit(solution)/shard_map/ppermute | solution.py:17
  72.1 6.2 %collective-permute-start.19 = (f32[1,1,8,128]{3,2,1,0:T(8,128)S(1)}, f32[1,1,8,128]{3,2,1,0:T(8,128)S(1)}, u32[]{:S(2)}, u32[]{:S(2)}) collective-permute-start(f32[1,1,8,128]{3,2,1,0:T(8,128)S(1)} %get-tuple-element.71), channel_id=1, source_target_pairs={{16,0},{32,16},{48,32},{64,48},{80,64},{96,80},{112,96},{128,112},... | collective-permute-start | bytes 12296 | tf_op jit(solution)/shard_map/ppermute | solution.py:19
  78.3 6.0 %collective-permute-start.20 = (f32[1,6,8,1]{3,2,1,0:T(8,128)S(1)}, f32[1,6,8,1]{3,2,1,0:T(8,128)S(1)}, u32[]{:S(2)}, u32[]{:S(2)}) collective-permute-start(f32[1,6,8,1]{3,2,1,0:T(8,128)S(1)} %get-tuple-element.62), channel_id=1, source_target_pairs={{0,4},{4,8},{8,12},{1,5},{5,9},{9,13},{2,6},{6,10},{10,14},{3,7},{... | collective-permute-start | bytes 584 | tf_op jit(solution)/shard_map/ppermute | solution.py:17
  82.9 5.7 %collective-permute-start.21 = (f32[1,6,8,1]{3,2,1,0:T(8,128)S(1)}, f32[1,6,8,1]{3,2,1,0:T(8,128)S(1)}, u32[]{:S(2)}, u32[]{:S(2)}) collective-permute-start(f32[1,6,8,1]{3,2,1,0:T(8,128)S(1)} %get-tuple-element.63), channel_id=1, source_target_pairs={{4,0},{8,4},{12,8},{5,1},{9,5},{13,9},{6,2},{10,6},{14,10},{7,3},{... | collective-permute-start | bytes 584 | tf_op jit(solution)/shard_map/ppermute | solution.py:19
  88.7 4.8 %collective-permute-start.22 = (f32[1,6,1,130]{3,2,1,0:T(1,128)S(1)}, f32[1,6,1,130]{3,2,1,0:T(1,128)S(1)}, u32[]{:S(2)}, u32[]{:S(2)}) collective-permute-start(f32[1,6,1,130]{3,2,1,0:T(1,128)S(1)} %get-tuple-element.54), channel_id=1, source_target_pairs={{0,1},{1,2},{2,3},{4,5},{5,6},{6,7},{8,9},{9,10},{10,11},{12,13},{... | collective-permute-start | bytes 9368 | tf_op jit(solution)/shard_map/ppermute | solution.py:17
  92.2 5.5 %collective-permute-start.23 = (f32[1,6,1,130]{3,2,1,0:T(1,128)S(1)}, f32[1,6,1,130]{3,2,1,0:T(1,128)S(1)}, u32[]{:S(2)}, u32[]{:S(2)}) collective-permute-start(f32[1,6,1,130]{3,2,1,0:T(1,128)S(1)} %get-tuple-element.55), channel_id=1, source_target_pairs={{1,0},{2,1},{3,2},{5,4},{6,5},{7,6},{9,8},{10,9},{11,10},{13,12},{... | collective-permute-start | bytes 9368 | tf_op jit(solution)/shard_map/ppermute | solution.py:19
  98.0 6.8 %collective-permute-start.24 = (f32[1,1,8,128]{3,2,1,0:T(8,128)S(1)}, f32[1,1,8,128]{3,2,1,0:T(8,128)S(1)}, u32[]{:S(2)}, u32[]{:S(2)}) collective-permute-start(f32[1,1,8,128]{3,2,1,0:T(8,128)S(1)} %get-tuple-element.68), channel_id=1, source_target_pairs={{0,16},{16,32},{32,48},{48,64},{64,80},{80,96},{96,112},{112,128},... | collective-permute-start | bytes 12296 | tf_op jit(solution)/shard_map/ppermute | solution.py:17
  99.9 6.2 %collective-permute-start.25 = (f32[1,1,8,128]{3,2,1,0:T(8,128)S(1)}, f32[1,1,8,128]{3,2,1,0:T(8,128)S(1)}, u32[]{:S(2)}, u32[]{:S(2)}) collective-permute-start(f32[1,1,8,128]{3,2,1,0:T(8,128)S(1)} %get-tuple-element.69), channel_id=1, source_target_pairs={{16,0},{32,16},{48,32},{64,48},{80,64},{96,80},{112,96},{128,112},... | collective-permute-start | bytes 12296 | tf_op jit(solution)/shard_map/ppermute | solution.py:19
  106.1 4.9 %collective-permute-start.26 = (f32[1,6,8,1]{3,2,1,0:T(8,128)S(1)}, f32[1,6,8,1]{3,2,1,0:T(8,128)S(1)}, u32[]{:S(2)}, u32[]{:S(2)}) collective-permute-start(f32[1,6,8,1]{3,2,1,0:T(8,128)S(1)} %get-tuple-element.60), channel_id=1, source_target_pairs={{0,4},{4,8},{8,12},{1,5},{5,9},{9,13},{2,6},{6,10},{10,14},{3,7},{... | collective-permute-start | bytes 584 | tf_op jit(solution)/shard_map/ppermute | solution.py:17
  109.5 5.7 %collective-permute-start.27 = (f32[1,6,8,1]{3,2,1,0:T(8,128)S(1)}, f32[1,6,8,1]{3,2,1,0:T(8,128)S(1)}, u32[]{:S(2)}, u32[]{:S(2)}) collective-permute-start(f32[1,6,8,1]{3,2,1,0:T(8,128)S(1)} %get-tuple-element.61), channel_id=1, source_target_pairs={{4,0},{8,4},{12,8},{5,1},{9,5},{13,9},{6,2},{10,6},{14,10},{7,3},{... | collective-permute-start | bytes 584 | tf_op jit(solution)/shard_map/ppermute | solution.py:19
  115.4 11.3 %collective-permute-start.28 = (f32[1,6,1,130]{3,2,1,0:T(1,128)S(1)}, f32[1,6,1,130]{3,2,1,0:T(1,128)S(1)}, u32[]{:S(2)}, u32[]{:S(2)}) collective-permute-start(f32[1,6,1,130]{3,2,1,0:T(1,128)S(1)} %get-tuple-element.52), channel_id=1, source_target_pairs={{0,1},{1,2},{2,3},{4,5},{5,6},{6,7},{8,9},{9,10},{10,11},{12,13},{... | collective-permute-start | bytes 9368 | tf_op jit(solution)/shard_map/ppermute | solution.py:17
  118.6 8.1 %collective-permute-start.29 = (f32[1,6,1,130]{3,2,1,0:T(1,128)S(1)}, f32[1,6,1,130]{3,2,1,0:T(1,128)S(1)}, u32[]{:S(2)}, u32[]{:S(2)}) collective-permute-start(f32[1,6,1,130]{3,2,1,0:T(1,128)S(1)} %get-tuple-element.53), channel_id=1, source_target_pairs={{1,0},{2,1},{3,2},{5,4},{6,5},{7,6},{9,8},{10,9},{11,10},{13,12},{... | collective-permute-start | bytes 9368 | tf_op jit(solution)/shard_map/ppermute | solution.py:19
  119.9 7.0 %collective-permute-start.6 = (f32[1,1,16,256]{3,2,1,0:T(8,128)S(1)}, f32[1,1,16,256]{3,2,1,0:T(8,128)S(1)}, u32[]{:S(2)}, u32[]{:S(2)}) collective-permute-start(f32[1,1,16,256]{3,2,1,0:T(8,128)S(1)} %get-tuple-element.48), channel_id=1, source_target_pairs={{0,16},{16,32},{32,48},{48,64},{64,80},{80,96},{96,112},{112,128},... | collective-permute-start | bytes 49160 | tf_op jit(solution)/shard_map/ppermute | solution.py:17
  121.8 6.3 %collective-permute-start.7 = (f32[1,1,16,256]{3,2,1,0:T(8,128)S(1)}, f32[1,1,16,256]{3,2,1,0:T(8,128)S(1)}, u32[]{:S(2)}, u32[]{:S(2)}) collective-permute-start(f32[1,1,16,256]{3,2,1,0:T(8,128)S(1)} %get-tuple-element.49), channel_id=1, source_target_pairs={{16,0},{32,16},{48,32},{64,48},{80,64},{96,80},{112,96},{128,112},... | collective-permute-start | bytes 49160 | tf_op jit(solution)/shard_map/ppermute | solution.py:19
  128.2 11.2 %collective-permute-start.8 = (f32[1,10,16,1]{3,2,1,0:T(8,128)S(1)}, f32[1,10,16,1]{3,2,1,0:T(8,128)S(1)}, u32[]{:S(2)}, u32[]{:S(2)}) collective-permute-start(f32[1,10,16,1]{3,2,1,0:T(8,128)S(1)} %get-tuple-element.44), channel_id=1, source_target_pairs={{0,4},{4,8},{8,12},{1,5},{5,9},{9,13},{2,6},{6,10},{10,14},{3,7},{... | collective-permute-start | bytes 1928 | tf_op jit(solution)/shard_map/ppermute | solution.py:17
  131.3 8.1 %collective-permute-start.9 = (f32[1,10,16,1]{3,2,1,0:T(8,128)S(1)}, f32[1,10,16,1]{3,2,1,0:T(8,128)S(1)}, u32[]{:S(2)}, u32[]{:S(2)}) collective-permute-start(f32[1,10,16,1]{3,2,1,0:T(8,128)S(1)} %get-tuple-element.45), channel_id=1, source_target_pairs={{4,0},{8,4},{12,8},{5,1},{9,5},{13,9},{6,2},{10,6},{14,10},{7,3},{... | collective-permute-start | bytes 1928 | tf_op jit(solution)/shard_map/ppermute | solution.py:19
  132.6 12.8 %collective-permute-start.30 = (f32[1,1,8,128]{3,2,1,0:T(8,128)S(1)}, f32[1,1,8,128]{3,2,1,0:T(8,128)S(1)}, u32[]{:S(2)}, u32[]{:S(2)}) collective-permute-start(f32[1,1,8,128]{3,2,1,0:T(8,128)S(1)} %get-tuple-element.66), channel_id=1, source_target_pairs={{0,16},{16,32},{32,48},{48,64},{64,80},{80,96},{96,112},{112,128},... | collective-permute-start | bytes 12296 | tf_op jit(solution)/shard_map/ppermute | solution.py:17
  134.5 10.9 %collective-permute-start.31 = (f32[1,1,8,128]{3,2,1,0:T(8,128)S(1)}, f32[1,1,8,128]{3,2,1,0:T(8,128)S(1)}, u32[]{:S(2)}, u32[]{:S(2)}) collective-permute-start(f32[1,1,8,128]{3,2,1,0:T(8,128)S(1)} %get-tuple-element.67), channel_id=1, source_target_pairs={{16,0},{32,16},{48,32},{64,48},{80,64},{96,80},{112,96},{128,112},... | collective-permute-start | bytes 12296 | tf_op jit(solution)/shard_map/ppermute | solution.py:19
  139.6 11.8 %collective-permute-start.10 = (f32[1,10,1,258]{3,2,1,0:T(1,128)S(1)}, f32[1,10,1,258]{3,2,1,0:T(1,128)S(1)}, u32[]{:S(2)}, u32[]{:S(2)}) collective-permute-start(f32[1,10,1,258]{3,2,1,0:T(1,128)S(1)} %get-tuple-element.34), channel_id=1, source_target_pairs={{0,1},{1,2},{2,3},{4,5},{5,6},{6,7},{8,9},{9,10},{10,11},{12,13},{... | collective-permute-start | bytes 30968 | tf_op jit(solution)/shard_map/ppermute | solution.py:17
  144.1 7.3 %collective-permute-start.11 = (f32[1,10,1,258]{3,2,1,0:T(1,128)S(1)}, f32[1,10,1,258]{3,2,1,0:T(1,128)S(1)}, u32[]{:S(2)}, u32[]{:S(2)}) collective-permute-start(f32[1,10,1,258]{3,2,1,0:T(1,128)S(1)} %get-tuple-element.35), channel_id=1, source_target_pairs={{1,0},{2,1},{3,2},{5,4},{6,5},{7,6},{9,8},{10,9},{11,10},{13,12},{... | collective-permute-start | bytes 30968 | tf_op jit(solution)/shard_map/ppermute | solution.py:19
  145.5 13.2 %collective-permute-start.32 = (f32[1,6,8,1]{3,2,1,0:T(8,128)S(1)}, f32[1,6,8,1]{3,2,1,0:T(8,128)S(1)}, u32[]{:S(2)}, u32[]{:S(2)}) collective-permute-start(f32[1,6,8,1]{3,2,1,0:T(8,128)S(1)} %get-tuple-element.58), channel_id=1, source_target_pairs={{0,4},{4,8},{8,12},{1,5},{5,9},{9,13},{2,6},{6,10},{10,14},{3,7},{... | collective-permute-start | bytes 584 | tf_op jit(solution)/shard_map/ppermute | solution.py:17
  150.1 8.6 %collective-permute-start.33 = (f32[1,6,8,1]{3,2,1,0:T(8,128)S(1)}, f32[1,6,8,1]{3,2,1,0:T(8,128)S(1)}, u32[]{:S(2)}, u32[]{:S(2)}) collective-permute-start(f32[1,6,8,1]{3,2,1,0:T(8,128)S(1)} %get-tuple-element.59), channel_id=1, source_target_pairs={{4,0},{8,4},{12,8},{5,1},{9,5},{13,9},{6,2},{10,6},{14,10},{7,3},{... | collective-permute-start | bytes 584 | tf_op jit(solution)/shard_map/ppermute | solution.py:19
  151.9 12.8 %collective-permute-start.36 = (f32[1,1,16,256]{3,2,1,0:T(8,128)S(1)}, f32[1,1,16,256]{3,2,1,0:T(8,128)S(1)}, u32[]{:S(2)}, u32[]{:S(2)}) collective-permute-start(f32[1,1,16,256]{3,2,1,0:T(8,128)S(1)} %get-tuple-element.46), channel_id=1, source_target_pairs={{0,16},{16,32},{32,48},{48,64},{64,80},{80,96},{96,112},{112,128},... | collective-permute-start | bytes 49160 | tf_op jit(solution)/shard_map/ppermute | solution.py:17
  153.8 10.9 %collective-permute-start.37 = (f32[1,1,16,256]{3,2,1,0:T(8,128)S(1)}, f32[1,1,16,256]{3,2,1,0:T(8,128)S(1)}, u32[]{:S(2)}, u32[]{:S(2)}) collective-permute-start(f32[1,1,16,256]{3,2,1,0:T(8,128)S(1)} %get-tuple-element.47), channel_id=1, source_target_pairs={{16,0},{32,16},{48,32},{64,48},{80,64},{96,80},{112,96},{128,112},... | collective-permute-start | bytes 49160 | tf_op jit(solution)/shard_map/ppermute | solution.py:19
  158.8 11.8 %collective-permute-start.34 = (f32[1,6,1,130]{3,2,1,0:T(1,128)S(1)}, f32[1,6,1,130]{3,2,1,0:T(1,128)S(1)}, u32[]{:S(2)}, u32[]{:S(2)}) collective-permute-start(f32[1,6,1,130]{3,2,1,0:T(1,128)S(1)} %get-tuple-element.50), channel_id=1, source_target_pairs={{0,1},{1,2},{2,3},{4,5},{5,6},{6,7},{8,9},{9,10},{10,11},{12,13},{... | collective-permute-start | bytes 9368 | tf_op jit(solution)/shard_map/ppermute | solution.py:17
  163.4 7.3 %collective-permute-start.35 = (f32[1,6,1,130]{3,2,1,0:T(1,128)S(1)}, f32[1,6,1,130]{3,2,1,0:T(1,128)S(1)}, u32[]{:S(2)}, u32[]{:S(2)}) collective-permute-start(f32[1,6,1,130]{3,2,1,0:T(1,128)S(1)} %get-tuple-element.51), channel_id=1, source_target_pairs={{1,0},{2,1},{3,2},{5,4},{6,5},{7,6},{9,8},{10,9},{11,10},{13,12},{... | collective-permute-start | bytes 9368 | tf_op jit(solution)/shard_map/ppermute | solution.py:19
  164.8 6.6 %collective-permute-start.38 = (f32[1,10,16,1]{3,2,1,0:T(8,128)S(1)}, f32[1,10,16,1]{3,2,1,0:T(8,128)S(1)}, u32[]{:S(2)}, u32[]{:S(2)}) collective-permute-start(f32[1,10,16,1]{3,2,1,0:T(8,128)S(1)} %get-tuple-element.42), channel_id=1, source_target_pairs={{0,4},{4,8},{8,12},{1,5},{5,9},{9,13},{2,6},{6,10},{10,14},{3,7},{... | collective-permute-start | bytes 1928 | tf_op jit(solution)/shard_map/ppermute | solution.py:17
  169.4 6.3 %collective-permute-start.39 = (f32[1,10,16,1]{3,2,1,0:T(8,128)S(1)}, f32[1,10,16,1]{3,2,1,0:T(8,128)S(1)}, u32[]{:S(2)}, u32[]{:S(2)}) collective-permute-start(f32[1,10,16,1]{3,2,1,0:T(8,128)S(1)} %get-tuple-element.43), channel_id=1, source_target_pairs={{4,0},{8,4},{12,8},{5,1},{9,5},{13,9},{6,2},{10,6},{14,10},{7,3},{... | collective-permute-start | bytes 1928 | tf_op jit(solution)/shard_map/ppermute | solution.py:19
  175.9 6.7 %collective-permute-start.40 = (f32[1,10,1,258]{3,2,1,0:T(1,128)S(1)}, f32[1,10,1,258]{3,2,1,0:T(1,128)S(1)}, u32[]{:S(2)}, u32[]{:S(2)}) collective-permute-start(f32[1,10,1,258]{3,2,1,0:T(1,128)S(1)} %get-tuple-element.32), channel_id=1, source_target_pairs={{0,1},{1,2},{2,3},{4,5},{5,6},{6,7},{8,9},{9,10},{10,11},{12,13},{... | collective-permute-start | bytes 30968 | tf_op jit(solution)/shard_map/ppermute | solution.py:17
  180.4 5.6 %collective-permute-start.41 = (f32[1,10,1,258]{3,2,1,0:T(1,128)S(1)}, f32[1,10,1,258]{3,2,1,0:T(1,128)S(1)}, u32[]{:S(2)}, u32[]{:S(2)}) collective-permute-start(f32[1,10,1,258]{3,2,1,0:T(1,128)S(1)} %get-tuple-element.33), channel_id=1, source_target_pairs={{1,0},{2,1},{3,2},{5,4},{6,5},{7,6},{9,8},{10,9},{11,10},{13,12},{... | collective-permute-start | bytes 30968 | tf_op jit(solution)/shard_map/ppermute | solution.py:19
where the time goes:
time: 188 us; the launch traced here: 187 us
  starting transfers between devices  121 us (64%)
  waiting for transfers between devices  30.6 us (16%)
  local copies, waits for them, and re-layouts  21.8 us (12%)
  other arithmetic  12.4 us (7%)
    ppermute x21, starting transfers between devices, padded_2(): lax.ppermute(tail, axis, [(i, (i + 1) % count) for i in range(ends)])  68.9 us
    ppermute x21, starting transfers between devices, padded_2(): lax.ppermute(head, axis, [((i + 1) % count, i) for i in range(ends)])  52.1 us
    ppermute x21, waiting for transfers between devices, padded_2(): lax.ppermute(head, axis, [((i + 1) % count, i) for i in range(ends)])  29.4 us
    reshape x2, local copies, waits for them, and re-layouts, restrict(): return field.reshape(a // 2, 2, b // 2, 2, c // 2, 2).mean(axis=(1, 3, 5))  20.3 us
    reduce_sum x2, other arithmetic, restrict(): return field.reshape(a // 2, 2, b // 2, 2, c // 2, 2).mean(axis=(1, 3, 5))  8.07 us
  transfers between devices with their start and end apart: 42, of which 14 were waited for; matrix products, arithmetic and copies ran while one was open for 1% of the time, Pallas kernels for 0%

commit v1 on v0

v1 whole, which is shorter than its diff:
```python
import functools

import jax
import jax.numpy as jnp
from jax import lax
from jax.experimental import pallas as pl
from jax.experimental.pallas import tpu as pltpu
from jax.sharding import PartitionSpec as P

KSWEEP = 4
THETA = 1.1
DELTA = 0.8
SIGMA = THETA / DELTA
RHO0 = 1.0 / SIGMA
RHO1 = 1.0 / (2.0 * SIGMA - RHO0)

NX, NY, NZ = 8, 16, 256
H = 8
RE = NY + 2 * H
RF = NY + H
ZE = NZ + 128
CX, CY = NX // 2, NY // 2
CE = RE // 2
GROUPS = 3 * NX
f32 = jnp.float32


def up(v, axis, by=1):
    return pltpu.roll(v, v.shape[axis] - by, axis)


def down(v, axis, by=1):
    return pltpu.roll(v, by, axis)


def lanes(shape):
    return lax.broadcasted_iota(jnp.int32, shape, len(shape) - 1)


def pack_kernel(where_ref, u_ref, k_ref, f_ref, up_ref, down_ref, z_ref):
    gz, cy = where_ref[0], where_ref[1]
    fields = (u_ref, k_ref, f_ref)
    for i, field in enumerate(fields):
        for p in range(NX):
            up_ref[i * NX + p] = field[p, NY - H :, :]
            down_ref[i * NX + p] = field[p, :H, :]
    group = lanes((NY, 128)) // H
    ends = []
    for first, start in ((NZ - 128, H), (0, 0)):
        tiles = []
        for t in range(2):
            tile = jnp.zeros((NY, 128), f32)
            for q in range(16):
                g = t * 16 + q
                if g < GROUPS:
                    cells = fields[g // NX][g % NX, :, first : first + 128]
                    shift = (H * q + start) % 128
                    moved = pltpu.roll(cells, shift, 1) if shift else cells
                    tile = jnp.where(group == q, moved, tile)
            tiles.append(tile)
        ends.append(jnp.concatenate(tiles, axis=1))
    z_ref[...] = jnp.zeros(z_ref.shape, f32)
    for end, to_z in zip(ends, (1, 3)):
        z = lax.rem(gz + to_z, 4) * 4
        z_ref[z + cy] = end
        z_ref[z + lax.rem(cy + 1, 4), :H] = end[NY - H :]
        z_ref[z + lax.rem(cy + 3, 4), :H] = end[:H]


def restrict_plane(plane, scratch_ref, even):
    pairs = plane + jnp.where(even, up(plane, 1), down(plane, 1))
    cols = []
    for t in range(ZE // 128):
        scratch_ref[t] = pairs[:, t * 128 : (t + 1) * 128]
        tile = scratch_ref.at[t]
        cols.append(tile[pl.ds(0, CE, stride=2), :] + tile[pl.ds(1, CE, stride=2), :])
    return 0.125 * jnp.concatenate(cols, axis=1)


def inner_rows(plane):
    row = lax.broadcasted_iota(jnp.int32, (H, ZE), 0)
    return jnp.concatenate(
        [plane[:NY], jnp.where(row < H // 2, plane[NY : NY + H], plane[NY + H :])], axis=0
    )


X_U, X_K, X_KI, X_R, X_C = 0, RE, 2 * RE, 2 * RE + 2 * RF, 2 * RE + 4 * RF
X_ROWS = X_C + 4 * CE


def block_kernel(
    where_ref, u_ref, k_ref, f_ref, up_ref, down_ref, z_ref,
    uo_ref, ko_ref, k_in_ref, r_in_ref, rc_ref, kc_ref, chip_ref, link_ref,
    ue_ref, ke_ref, fe_ref, tmp_ref,
):
    gz, cy, core = where_ref[0], where_ref[1], where_ref[2]
    lane = lanes((RE, 128))
    sides = []
    for from_z, inside in ((3, gz > 0), (1, gz < 3)):
        z = lax.rem(gz + from_z, 4) * 4
        rows = [
            z_ref[z + cy],
            jnp.where(cy < 3, z_ref[z + lax.rem(cy + 1, 4), :H], 0.0),
            jnp.where(cy > 0, z_ref[z + lax.rem(cy + 3, 4), :H], 0.0),
        ]
        sides.append(jnp.where(inside, jnp.concatenate(rows, axis=0), 0.0))
    for i, (own, ext) in enumerate(((u_ref, ue_ref), (k_ref, ke_ref), (f_ref, fe_ref))):
        for p in range(NX):
            g = i * NX + p
            t, q = divmod(g, 16)
            at = slice(t * 128, t * 128 + 128)
            before = pltpu.roll(sides[0][:, at], (120 - H * q) % 128, 1) if (120 - H * q) % 128 else sides[0][:, at]
            after = pltpu.roll(sides[1][:, at], (128 - H * q) % 128, 1) if q else sides[1][:, at]
            ext[p, :NY, :NZ] = own[p]
            ext[p, NY : NY + H, :NZ] = down_ref[g]
            ext[p, NY + H :, :NZ] = up_ref[g]
            ext[p, :, NZ:] = jnp.where(lane < H, after, jnp.where(lane >= 120, before, 0.0))
    even = lanes((RE, ZE)) % 2 == 0
    flux_x = None
    r_pair = k_pair = None
    for p in range(NX):
        k, u = ke_ref[p], ue_ref[p]
        flux = 0.5 * (k + up(k, 1)) * (u - up(u, 1))
        out = flux - down(flux, 1)
        flux = 0.5 * (k + up(k, 0)) * (u - up(u, 0))
        out = out + (flux - down(flux, 0))
        if flux_x is not None:
            out = out - flux_x
        if p < NX - 1:
            flux_x = 0.5 * (k + ke_ref[p + 1]) * (u - ue_ref[p + 1])
            out = out + flux_x
        r = fe_ref[p] - out
        r_in_ref[p] = inner_rows(r)
        k_in_ref[p] = inner_rows(k)
        if p % 2 == 0:
            r_pair, k_pair = r, k
        else:
            rc_ref[p // 2] = restrict_plane(r_pair + r, tmp_ref, even)
            kc_ref[p // 2] = restrict_plane(k_pair + k, tmp_ref, even)
    uo_ref[0], uo_ref[1] = ue_ref[0], ue_ref[NX - 1]
    ko_ref[0], ko_ref[1] = ke_ref[0], ke_ref[NX - 1]
    even_c = lanes((CE, ZE)) % 2 == 0
    for ref, last in ((chip_ref, core == 0), (link_ref, core == 1)):
        end = last.astype(jnp.int32)
        at, step = end * (NX - 1), 1 - 2 * end
        ref[X_U : X_U + RE] = ue_ref[at]
        ref[X_K : X_K + RE] = ke_ref[at]
        for d in range(2):
            ref[X_KI + d * RF : X_KI + (d + 1) * RF] = k_in_ref[at + (d + 1) * step]
            ref[X_R + d * RF : X_R + (d + 1) * RF] = r_in_ref[at + d * step]
        for d in range(CX):
            c = end * (CX - 1) + d * step
            ref[X_C + d * CE : X_C + (d + 1) * CE] = jnp.where(even_c, rc_ref[c], kc_ref[c])


def apply_faces(v, kx0, kx1, ky, kz, before, after, by=1):
    flux = kz * (v - up(v, 1, by))
    out = flux - down(flux, 1, by)
    flux = ky * (v - up(v, 0))
    out = out + (flux - down(flux, 0))
    return out + kx0 * (v - before) + kx1 * (v - after)


def final_kernel(
    where_ref, guess_ref, uo_ref, ko_ref, k_in_ref, r_in_ref, rc_ref, kc_ref, chip_ref, link_ref,
    new_ref, smooth_ref,
    k_ref, r_ref, inv_ref, d0_ref, d1_ref, ky_ref, kz_ref,
    q_ref, s_ref, cinv_ref, ec_ref, ed_ref, cy_ref, cz_ref, tmp_ref, lift_ref,
):
    core = where_ref[2]
    even = lanes((RE, ZE)) % 2 == 0
    even_c = lanes((CE, ZE)) % 2 == 0
    KO, RO, QO = 3, 2, 4
    for p in range(NX):
        k_ref[KO + p] = k_in_ref[p]
        r_ref[RO + p] = r_in_ref[p]
    for c in range(CX):
        q_ref[QO + c] = kc_ref[c]
        s_ref[QO + c] = rc_ref[c]
    for ref, last in ((chip_ref, core == 0), (link_ref, core == 1)):
        end = last.astype(jnp.int32)
        at, step = end * (NX - 1), 2 * end - 1
        un, kn = ref[X_U : X_U + RE], ref[X_K : X_K + RE]
        flux = 0.5 * (ko_ref[end] + kn) * (uo_ref[end] - un)
        inner = inner_rows(flux)
        r_ref[RO + at] = r_ref[RO + at] - inner
        k_ref[KO + at + step] = inner_rows(kn)
        r_ref[RO + at + step] = ref[X_R : X_R + RF] + inner
        r_ref[RO + at + 2 * step] = ref[X_R + RF : X_R + 2 * RF]
        for d in range(2):
            k_ref[KO + at + (d + 2) * step] = ref[X_KI + d * RF : X_KI + (d + 1) * RF]
        coarse = restrict_plane(flux, tmp_ref, even)
        ct = end * (CX - 1)
        s_ref[QO + ct] = s_ref[QO + ct] - coarse
        for d in range(CX):
            both = ref[X_C + d * CE : X_C + (d + 1) * CE]
            rc = jnp.where(even_c, both, down(both, 1))
            if d == 0:
                rc = rc + coarse
            s_ref[QO + ct + (d + 1) * step] = rc
            q_ref[QO + ct + (d + 1) * step] = jnp.where(even_c, up(both, 1), both)

    for p in range(-2, NX + 2):
        k = k_ref[KO + p]
        kx0 = 0.5 * (k + k_ref[KO + p - 1])
        kx1 = 0.5 * (k + k_ref[KO + p + 1])
        ky = 0.5 * (k + up(k, 0))
        kz = 0.5 * (k + up(k, 1))
        diag = kx0 + kx1 + (ky + down(ky, 0)) + (kz + down(kz, 1))
        inside = k > 0.0
        inv = jnp.where(inside, 1.0 / jnp.where(inside, diag, 1.0), 0.0)
        ky_ref[RO + p], kz_ref[RO + p], inv_ref[RO + p] = ky, kz, inv
        d0_ref[RO + p] = r_ref[RO + p] * inv * (1.0 / THETA)
    for p in range(-1, NX + 1):
        at = RO + p
        k = k_ref[KO + p]
        d0 = d0_ref[at]
        r1 = r_ref[at] - apply_faces(
            d0, 0.5 * (k + k_ref[KO + p - 1]), 0.5 * (k + k_ref[KO + p + 1]),
            ky_ref[at], kz_ref[at], d0_ref[at - 1], d0_ref[at + 1],
        )
        r_ref[at] = r1
        d1_ref[at] = RHO1 * RHO0 * d0 + (2.0 * RHO1 / DELTA) * r1 * inv_ref[at]
    for p in range(NX):
        at = RO + p
        k = k_ref[KO + p]
        d1 = d1_ref[at]
        out = r_ref[at] - apply_faces(
            d1, 0.5 * (k + k_ref[KO + p - 1]), 0.5 * (k + k_ref[KO + p + 1]),
            ky_ref[at], kz_ref[at], d1_ref[at - 1], d1_ref[at + 1],
        )
        smooth_ref[p] = out[:NY, :NZ]

    for c in range(-3, CX + 3):
        at = QO + c
        k = q_ref[at]
        cy = 0.125 * (k + up(k, 0))
        cz = 0.125 * (k + up(k, 1, 2))
        diag = 0.125 * (k + q_ref[at - 1]) + 0.125 * (k + q_ref[at + 1])
        diag = diag + (cy + down(cy, 0)) + (cz + down(cz, 1, 2))
        inside = k > 0.0
        inv = jnp.where(inside, 0.8 / jnp.where(inside, diag, 1.0), 0.0)
        cy_ref[at], cz_ref[at], cinv_ref[at] = cy, cz, inv
        ec_ref[at] = s_ref[at] * inv
    now, then = ec_ref, ed_ref
    for sweep in range(KSWEEP - 1):
        wide = KSWEEP - 2 - sweep
        for c in range(-wide, CX + wide):
            at = QO + c
            k = q_ref[at]
            e = now[at]
            res = s_ref[at] - apply_faces(
                e, 0.125 * (k + q_ref[at - 1]), 0.125 * (k + q_ref[at + 1]),
                cy_ref[at], cz_ref[at], now[at - 1], now[at + 1], 2,
            )
            then[at] = e + cinv_ref[at] * res
        now, then = then, now
    for c in range(CX):
        e = now[QO + c][:CY, :NZ]
        cols = []
        for t in range(NZ // 128):
            part = e[:, t * 128 : (t + 1) * 128]
            tile = lift_ref.at[t]
            tile[pl.ds(0, CY, stride=2), :] = part
            tile[pl.ds(1, CY, stride=2), :] = part
            cols.append(tile[...])
        lifted = jnp.concatenate(cols, axis=1)
        for p in (2 * c, 2 * c + 1):
            step = d0_ref[RO + p][:NY, :NZ] + d1_ref[RO + p][:NY, :NZ]
            new_ref[p] = guess_ref[p] + step + lifted


def call(kernel, outs, n_in, scratch, name, bytes_accessed, flops):
    vmem = pl.BlockSpec(memory_space=pltpu.VMEM)
    return pl.pallas_call(
        kernel,
        out_shape=[jax.ShapeDtypeStruct(s, f32) for s in outs],
        in_specs=[pl.BlockSpec(memory_space=pltpu.SMEM)] + [vmem] * (n_in - 1),
        out_specs=[vmem] * len(outs),
        scratch_shapes=[pltpu.VMEM(s, f32) for s in scratch],
        name=name,
        cost_estimate=pl.CostEstimate(flops=flops, bytes_accessed=bytes_accessed, transcendentals=0),
    )


def shifted(cells, axis, by):
    count = lax.axis_size(axis)
    return lax.ppermute(cells, axis, [(i, i + by) for i in range(count) if 0 <= i + by < count])


def swapped(cells, axis, first):
    count = lax.axis_size(axis)
    pairs = []
    for i in range(first, count - 1, 2):
        pairs += [(i, i + 1), (i + 1, i)]
    return lax.ppermute(cells, axis, pairs)


def on_device(right_side, conductivity, guess):
    where = jnp.stack(
        [lax.axis_index("gz"), lax.axis_index("coarse"), lax.axis_index("pencil") % 2]
    ).astype(jnp.int32)
    fields = (guess, conductivity, right_side)
    upward, downward, ends = call(
        pack_kernel,
        [(GROUPS, H, NZ), (GROUPS, H, NZ), (16, NY, 256)],
        4, [], "pack", 1 << 20, 1 << 18,
    )(where, *fields)
    ends = lax.all_to_all(ends, ("gz", "coarse"), 0, 0)
    upward = shifted(upward, "coarse", 1)
    downward = shifted(downward, "coarse", -1)
    kept = call(
        block_kernel,
        [
            (2, RE, ZE), (2, RE, ZE), (NX, RF, ZE), (NX, RF, ZE), (CX, CE, ZE), (CX, CE, ZE),
            (X_ROWS, ZE), (X_ROWS, ZE),
        ],
        7, [(NX, RE, ZE)] * 3 + [(ZE // 128, RE, 128)], "block", 3 << 20, 1 << 22,
    )(where, *fields, upward, downward, ends)
    chip = swapped(kept[6], "pencil", 0)
    link = swapped(kept[7], "pencil", 1)
    fine, wide = (NX + 4, RF, ZE), (NX + 6, RF, ZE)
    coarse = (CX + 8, CE, ZE)
    return tuple(
        call(
            final_kernel,
            [(NX, NY, NZ), (NX, NY, NZ)],
            10,
            [wide] + [fine] * 6 + [coarse] * 7 + [(ZE // 128, RE, 128), (NZ // 128, NY, 128)],
            "final", 4 << 20, 1 << 23,
        )(where, guess, *kept[:6], chip, link)
    )


def solution(mesh):
    spec = P("pencil", "coarse", "gz")
    return jax.shard_map(
        on_device,
        mesh=mesh,
        in_specs=(spec, spec, spec),
        out_specs=(spec, spec),
        check_vma=False,
    )
```

time: 188 us -> 47.7 us (0.25)
  the two profiles are of different devices: /device:TPU:128 before, /device:TPU:1 now
where the time goes in v1:
time: 47.7 us; the launch traced here: 47.3 us
  starting transfers between devices  19.5 us (41%)
  waiting for transfers between devices  12.9 us (27%)
  Pallas kernels  11.4 us (24%)
  local copies, waits for them, and re-layouts  2.11 us (4%)
  between operations  0.72 us (2%)
  other arithmetic  0.6 us (1%)
    all_to_all x1, starting transfers between devices, on_device(): ends = lax.all_to_all(ends, ('gz', 'coarse'), 0, 0)  7.7 us
    ppermute x2, starting transfers between devices, swapped(): return lax.ppermute(cells, axis, pairs)  7.22 us
    ppermute x2, waiting for transfers between devices, swapped(): return lax.ppermute(cells, axis, pairs)  6.83 us
    ppermute x2, waiting for transfers between devices, shifted(): lax.ppermute(cells, axis, [(i, i + by) for i in range(count) if 0 <= i +...  6.1 us
    pallas_call x1, Pallas kernels, on_device(): call(final_kernel, [(NX, NY, NZ), (NX, NY, NZ)], 10, [wide] + [fine] * 6...  5.48 us
    ppermute x2, starting transfers between devices, shifted(): lax.ppermute(cells, axis, [(i, i + by) for i in range(count) if 0 <= i +...  4.57 us
    pallas_call x1, Pallas kernels, on_device(): call(block_kernel, [(2, RE, ZE), (2, RE, ZE), (NX, RF, ZE), (NX, RF, ZE),...  3.95 us
    unnamed x14, local copies, waits for them, and re-layouts  2.11 us
  transfers between devices with their start and end apart: 5, of which 3 were waited for; matrix products, arithmetic and copies ran while one was open for 0% of the time, Pallas kernels for 0%

profile of v1, /device:TPU:1, one launch (start us, length us, event | category | flops | bytes accessed | tf_op | source)
XLA Modules:
  0.0 47.3 jit_solution(13242078502332135910)
XLA Ops:
  0.6 0.6 %pad_add_fusion.where_ref = s32[3]{0:T(128)} fusion(s32[1]{0:T(128)} %bitcast.2, s32[1]{0:T(128)} %bitcast.1, s32[1]{0:T(128)} %bitcast), kind=kLoop, calls=%fused_computation | loop fusion | flops 6 | bytes 24 | tf_op jit(solution)/shard_map/stack | solution.py:300
  1.2 2.0 %pack.1 = (f32[24,8,256]{2,1,0:T(8,128)}, f32[24,8,256]{2,1,0:T(8,128)}, f32[16,16,256]{2,1,0:T(8,128)}) custom-call(s32[3]{0:T(128)} %pad_add_fusion.where_ref, f32[8,16,256]{2,1,0:T(8,128)} %guess_ref.1, f32[8,16,256]{2,1,0:T(8,128)} %k_ref.3, f32[8,16,256]{2,1,0:T(8,128)} %f_ref.3), custom_call_target="tpu_custom_call" | custom-call | flops 262144 | bytes 1048576 | tf_op jit(solution)/shard_map/pack/pallas_call | solution.py:304
  3.3 0.0 copy-start.6
  3.3 0.0 copy-start.5
  3.3 7.7 %all-to-all-start = ((f32[16,16,256]{2,1,0:T(8,128)}), f32[16,16,256]{2,1,0:T(8,128)S(1)}, u32[]{:S(2)}, u32[]{:S(2)}) async-start(f32[16,16,256]{2,1,0:T(8,128)} %get-tuple-element.15), calls=%async_computation | async-start | bytes 524288 | tf_op jit(solution)/shard_map/all_to_all | solution.py:309
  11.0 0.0 copy-done.6
  11.0 3.3 %collective-permute-start = (f32[24,8,256]{2,1,0:T(8,128)S(1)}, f32[24,8,256]{2,1,0:T(8,128)S(1)}, u32[]{:S(2)}, u32[]{:S(2)}) collective-permute-start(f32[24,8,256]{2,1,0:T(8,128)S(1)} %copy-done.6), channel_id=1, source_target_pairs={{0,1},{1,2},{2,3},{4,5},{5,6},{6,7},{8,9},{9,10},{10,11},{12,13},{... | collective-permute-start | bytes 589832 | tf_op jit(solution)/shard_map/ppermute | solution.py:288
  14.3 0.0 copy-done.5
  14.3 1.3 %collective-permute-start.1 = (f32[24,8,256]{2,1,0:T(8,128)S(1)}, f32[24,8,256]{2,1,0:T(8,128)S(1)}, u32[]{:S(2)}, u32[]{:S(2)}) collective-permute-start(f32[24,8,256]{2,1,0:T(8,128)S(1)} %copy-done.5), channel_id=1, source_target_pairs={{1,0},{2,1},{3,2},{5,4},{6,5},{7,6},{9,8},{10,9},{11,10},{13,12},{... | collective-permute-start | bytes 589832 | tf_op jit(solution)/shard_map/ppermute | solution.py:288
  15.6 2.5 %collective-permute-done.up_ref = f32[24,8,256]{2,1,0:T(8,128)S(1)} collective-permute-done((f32[24,8,256]{2,1,0:T(8,128)S(1)}, f32[24,8,256]{2,1,0:T(8,128)S(1)}, u32[]{:S(2)}, u32[]{:S(2)}) %collective-permute-start) | collective-permute-done | bytes 196640 | tf_op jit(solution)/shard_map/ppermute | solution.py:288
  18.1 0.0 copy-start.3
  18.1 3.6 %collective-permute-done.1.down_ref = f32[24,8,256]{2,1,0:T(8,128)S(1)} collective-permute-done((f32[24,8,256]{2,1,0:T(8,128)S(1)}, f32[24,8,256]{2,1,0:T(8,128)S(1)}, u32[]{:S(2)}, u32[]{:S(2)}) %collective-permute-start.1) | collective-permute-done | bytes 196640 | tf_op jit(solution)/shard_map/ppermute | solution.py:288
  21.7 0.0 copy-start.4
  21.7 0.0 all-to-all-done.z_ref
  21.7 0.0 copy-done.3
  21.7 0.7 %copy-done.4 = f32[24,8,256]{2,1,0:T(8,128)} copy-done((f32[24,8,256]{2,1,0:T(8,128)}, f32[24,8,256]{2,1,0:T(8,128)S(1)}, u32[]{:S(2)}) %copy-start.4) | copy-done | bytes 196632
  22.4 0.0 copy-start
  22.4 0.7 %copy-done = f32[16,16,256]{2,1,0:T(8,128)} copy-done((f32[16,16,256]{2,1,0:T(8,128)}, f32[16,16,256]{2,1,0:T(8,128)S(1)}, u32[]{:S(2)}) %copy-start) | copy-done | bytes 262168
  23.1 3.9 %block.1 = (f32[2,32,384]{2,1,0:T(8,128)}, f32[2,32,384]{2,1,0:T(8,128)}, f32[8,24,384]{2,1,0:T(8,128)}, f32[8,24,384]{2,1,0:T(8,128)}, f32[4,16,384]{2,1,0:T(8,...) custom-call(s32[3]{0:T(128)} %pad_add_fusion.where_ref, f32[8,16,256]{2,1,0:T(8,128)} %guess_ref.1, ...), custom_call_target="tpu_custom_call" | custom-call | flops 4194304 | bytes 3145728 | tf_op jit(solution)/shard_map/block/pallas_call | solution.py:312
  27.0 5.3 %collective-permute-start.2 = (f32[224,384]{1,0:T(8,128)}, f32[224,384]{1,0:T(8,128)S(1)}, u32[]{:S(2)}, u32[]{:S(2)}) collective-permute-start(f32[224,384]{1,0:T(8,128)} %get-tuple-element.22), channel_id=1, source_target_pairs={{0,16},{16,0},{32,48},{48,32},{64,80},{80,64},{96,112},{112,96},{1... | collective-permute-start | bytes 1032200 | tf_op jit(solution)/shard_map/ppermute | solution.py:296
  32.3 1.9 %collective-permute-start.3 = (f32[224,384]{1,0:T(8,128)}, f32[224,384]{1,0:T(8,128)S(1)}, u32[]{:S(2)}, u32[]{:S(2)}) collective-permute-start(f32[224,384]{1,0:T(8,128)} %get-tuple-element.23), channel_id=1, source_target_pairs={{16,32},{32,16},{48,64},{64,48},{80,96},{96,80},{112,128},{128,112... | collective-permute-start | bytes 1032200 | tf_op jit(solution)/shard_map/ppermute | solution.py:296
  34.2 0.0 collective-permute-done.2.chip_ref
  34.3 0.0 copy-start.1
  34.3 6.8 %collective-permute-done.3.link_ref = f32[224,384]{1,0:T(8,128)S(1)} collective-permute-done((f32[224,384]{1,0:T(8,128)}, f32[224,384]{1,0:T(8,128)S(1)}, u32[]{:S(2)}, u32[]{:S(2)}) %collective-permute-start.3) | collective-permute-done | bytes 344096 | tf_op jit(solution)/shard_map/ppermute | solution.py:296
  41.1 0.0 copy-start.2
  41.1 0.0 copy-done.1
  41.1 0.7 %copy-done.2 = f32[224,384]{1,0:T(8,128)} copy-done((f32[224,384]{1,0:T(8,128)}, f32[224,384]{1,0:T(8,128)S(1)}, u32[]{:S(2)}) %copy-start.2) | copy-done | bytes 344088
  41.8 5.5 %final.1 = (f32[8,16,256]{2,1,0:T(8,128)}, f32[8,16,256]{2,1,0:T(8,128)}) custom-call(s32[3]{0:T(128)} %pad_add_fusion.where_ref, f32[8,16,256]{2,1,0:T(8,128)} %guess_ref.1, f32[2,32,384]{2,1,0:T(8,128)} %get-tuple-element.16.uo_ref, f32[2,32,384]{2,1,0:T(8,128)} %get-tuple-element.17.ko_ref, f32[8,24,384]{2,1,0:T(8,128)} %get-tuple-element.18.k_in_ref, ...), custom_call_target="tpu_custom_call" | custom-call | flops 8388608 | bytes 4194304 | tf_op jit(solution)/shard_map/final/pallas_call | solution.py:325
Async XLA Ops:
  3.3 7.7 %copy-start.6 = (f32[24,8,256]{2,1,0:T(8,128)S(1)}, f32[24,8,256]{2,1,0:T(8,128)}, u32[]{:S(2)}) copy-start(f32[24,8,256]{2,1,0:T(8,128)} %get-tuple-element.13) | copy-start | bytes 589828
  3.3 11.0 %copy-start.5 = (f32[24,8,256]{2,1,0:T(8,128)S(1)}, f32[24,8,256]{2,1,0:T(8,128)}, u32[]{:S(2)}) copy-start(f32[24,8,256]{2,1,0:T(8,128)} %get-tuple-element.14) | copy-start | bytes 589828
  3.3 18.4 %all-to-all-start = ((f32[16,16,256]{2,1,0:T(8,128)}), f32[16,16,256]{2,1,0:T(8,128)S(1)}, u32[]{:S(2)}, u32[]{:S(2)}) async-start(f32[16,16,256]{2,1,0:T(8,128)} %get-tuple-element.15), calls=%async_computation | async-start | bytes 524288 | tf_op jit(solution)/shard_map/all_to_all | solution.py:309
  11.0 7.1 %collective-permute-start = (f32[24,8,256]{2,1,0:T(8,128)S(1)}, f32[24,8,256]{2,1,0:T(8,128)S(1)}, u32[]{:S(2)}, u32[]{:S(2)}) collective-permute-start(f32[24,8,256]{2,1,0:T(8,128)S(1)} %copy-done.6), channel_id=1, source_target_pairs={{0,1},{1,2},{2,3},{4,5},{5,6},{6,7},{8,9},{9,10},{10,11},{12,13},{... | collective-permute-start | bytes 589832 | tf_op jit(solution)/shard_map/ppermute | solution.py:288
  14.3 7.4 %collective-permute-start.1 = (f32[24,8,256]{2,1,0:T(8,128)S(1)}, f32[24,8,256]{2,1,0:T(8,128)S(1)}, u32[]{:S(2)}, u32[]{:S(2)}) collective-permute-start(f32[24,8,256]{2,1,0:T(8,128)S(1)} %copy-done.5), channel_id=1, source_target_pairs={{1,0},{2,1},{3,2},{5,4},{6,5},{7,6},{9,8},{10,9},{11,10},{13,12},{... | collective-permute-start | bytes 589832 | tf_op jit(solution)/shard_map/ppermute | solution.py:288
  18.1 3.6 %copy-start.3 = (f32[24,8,256]{2,1,0:T(8,128)}, f32[24,8,256]{2,1,0:T(8,128)S(1)}, u32[]{:S(2)}) copy-start(f32[24,8,256]{2,1,0:T(8,128)S(1)} %collective-permute-done.up_ref) | copy-start | bytes 589828
  21.7 0.7 %copy-start.4 = (f32[24,8,256]{2,1,0:T(8,128)}, f32[24,8,256]{2,1,0:T(8,128)S(1)}, u32[]{:S(2)}) copy-start(f32[24,8,256]{2,1,0:T(8,128)S(1)} %collective-permute-done.1.down_ref) | copy-start | bytes 589828
  22.4 0.7 %copy-start = (f32[16,16,256]{2,1,0:T(8,128)}, f32[16,16,256]{2,1,0:T(8,128)S(1)}, u32[]{:S(2)}) copy-start(f32[16,16,256]{2,1,0:T(8,128)S(1)} %all-to-all-done.z_ref) | copy-start | bytes 786436
  27.0 7.2 %collective-permute-start.2 = (f32[224,384]{1,0:T(8,128)}, f32[224,384]{1,0:T(8,128)S(1)}, u32[]{:S(2)}, u32[]{:S(2)}) collective-permute-start(f32[224,384]{1,0:T(8,128)} %get-tuple-element.22), channel_id=1, source_target_pairs={{0,16},{16,0},{32,48},{48,32},{64,80},{80,64},{96,112},{112,96},{1... | collective-permute-start | bytes 1032200 | tf_op jit(solution)/shard_map/ppermute | solution.py:296
  32.3 8.8 %collective-permute-start.3 = (f32[224,384]{1,0:T(8,128)}, f32[224,384]{1,0:T(8,128)S(1)}, u32[]{:S(2)}, u32[]{:S(2)}) collective-permute-start(f32[224,384]{1,0:T(8,128)} %get-tuple-element.23), channel_id=1, source_target_pairs={{16,32},{32,16},{48,64},{64,48},{80,96},{96,80},{112,128},{128,112... | collective-permute-start | bytes 1032200 | tf_op jit(solution)/shard_map/ppermute | solution.py:296
  34.3 6.8 %copy-start.1 = (f32[224,384]{1,0:T(8,128)}, f32[224,384]{1,0:T(8,128)S(1)}, u32[]{:S(2)}) copy-start(f32[224,384]{1,0:T(8,128)S(1)} %collective-permute-done.2.chip_ref) | copy-start | bytes 1032196
  41.1 0.7 %copy-start.2 = (f32[224,384]{1,0:T(8,128)}, f32[224,384]{1,0:T(8,128)S(1)}, u32[]{:S(2)}) copy-start(f32[224,384]{1,0:T(8,128)S(1)} %collective-permute-done.3.link_ref) | copy-start | bytes 1032196

commit v2 on v0

v2 whole, which is shorter than its diff:
```python
import jax
import jax.numpy as jnp
from jax import lax
from jax.experimental import pallas as pl
from jax.experimental.pallas import tpu as pltpu
from jax.sharding import PartitionSpec as P


THETA = 1.1
DELTA = 0.8
SIGMA = THETA / DELTA
RHO0 = 1.0 / SIGMA
RHO1 = 1.0 / (2.0 * SIGMA - RHO0)

NX, NY, NZ = 8, 16, 256
H = 8
RE = NY + 2 * H
RF = NY + H
ZE = NZ + 128
CX, CY = NX // 2, NY // 2
CE = RE // 2
GROUPS = 3 * NX
f32 = jnp.float32


def up(v, axis, by=1):
    return pltpu.roll(v, v.shape[axis] - by, axis)


def down(v, axis, by=1):
    return pltpu.roll(v, by, axis)


def lanes(shape):
    return lax.broadcasted_iota(jnp.int32, shape, len(shape) - 1)


def pack_kernel(
    u_hbm, k_hbm, f_hbm,
    u_ref, k_ref, f_ref, up_ref, down_ref, z_hbm,
    end_ref, own_sem, end_sem,
):
    gz, cy = lax.axis_index("gz"), lax.axis_index("coarse")
    fields = (u_ref, k_ref, f_ref)
    copies = []
    for i, (far, near) in enumerate(zip((u_hbm, k_hbm, f_hbm), fields)):
        for half in range(2):
            at = pl.ds(half * NX // 2, NX // 2)
            copies.append(pltpu.make_async_copy(far.at[at], near.at[at], own_sem.at[2 * i + half]))
            copies[-1].start()
    for copy in copies:
        copy.wait()
    group = lanes((NY, 128)) // H
    sends = []
    for side, (first, start, to_z) in enumerate(((NZ - 128, H, 1), (0, 0, 3))):
        for t in range(2):
            tile = jnp.zeros((NY, 128), f32)
            for q in range(16):
                g = t * 16 + q
                if g < GROUPS:
                    cells = fields[g // NX][g % NX, :, first : first + 128]
                    shift = (H * q + start) % 128
                    moved = pltpu.roll(cells, shift, 1) if shift else cells
                    tile = jnp.where(group == q, moved, tile)
            end_ref[side, :, t * 128 : (t + 1) * 128] = tile
        z = lax.rem(gz + to_z, 4) * 4
        end = end_ref.at[side]
        for j, (src, dst) in enumerate((
            (end, z_hbm.at[z + cy]),
            (end.at[pl.ds(NY - H, H)], z_hbm.at[z + lax.rem(cy + 1, 4), pl.ds(0, H)]),
            (end.at[pl.ds(0, H)], z_hbm.at[z + lax.rem(cy + 3, 4), pl.ds(0, H)]),
        )):
            sends.append(pltpu.make_async_copy(src, dst, end_sem.at[3 * side + j]))
            sends[-1].start()
    for i, field in enumerate(fields):
        for p in range(NX):
            up_ref[i * NX + p] = field[p, NY - H :, :]
            down_ref[i * NX + p] = field[p, :H, :]
    for copy in sends:
        copy.wait()


def restrict_plane(plane, scratch_ref, even, scale):
    pairs = plane + jnp.where(even, up(plane, 1), down(plane, 1))
    cols = []
    for t in range(ZE // 128):
        scratch_ref[t] = pairs[:, t * 128 : (t + 1) * 128]
        tile = scratch_ref.at[t]
        cols.append(tile[pl.ds(0, CE, stride=2), :] + tile[pl.ds(1, CE, stride=2), :])
    return scale * jnp.concatenate(cols, axis=1)


def place(core, p, count):
    return core * (count - 1) + (1 - 2 * core) * p


def inner_rows(plane):
    row = lax.broadcasted_iota(jnp.int32, (H, ZE), 0)
    return jnp.concatenate(
        [plane[:NY], jnp.where(row < H // 2, plane[NY : NY + H], plane[NY + H :])], axis=0
    )


X_U, X_K, X_K2, X_K3, X_R1, X_R2, X_C = 0, 4, 8, 11, 13, 16, 18
X_GROUPS = X_C + 3 * 2 + 1
X_TAIL = X_GROUPS


def send_rows(ref, tails, first, plane):
    for j in range(plane.shape[0] // 8):
        rows = plane[j * 8 : (j + 1) * 8]
        ref[first + j] = rows[:, :NZ]
        tails[first + j] = rows[:, NZ:]


def send_tails(ref, tails):
    lane = lanes((8, 128)) // 16
    for half in range(4):
        tile = jnp.zeros((8, 128), f32)
        for j in range(8):
            g = half * 8 + j
            if g < X_GROUPS:
                shift = (16 * j + 8) % 128
                tile = jnp.where(lane == j, pltpu.roll(tails[g], shift, 1), tile)
        ref[X_TAIL + half // 2, :, (half % 2) * 128 : (half % 2) * 128 + 128] = tile


def received_rows(ref, first, groups):
    rows = []
    for g in range(first, first + groups):
        half, j = divmod(g, 8)
        tile = ref[X_TAIL + half // 2, :, (half % 2) * 128 : (half % 2) * 128 + 128]
        rows.append(jnp.concatenate([ref[g], pltpu.roll(tile, (120 - 16 * j) % 128, 1)], axis=1) if (120 - 16 * j) % 128 else jnp.concatenate([ref[g], tile], axis=1))
    return jnp.concatenate(rows, axis=0)


def block_kernel(
    u_ref, k_ref, f_ref, up_ref, down_ref, z_ref,
    uo_ref, ko_ref, k_in_ref, r_in_ref, rc_ref, kc_ref, chip_ref, link_ref,
    ue_ref, ke_ref, fe_ref, tmp_ref,
):
    gz, cy, core = lax.axis_index("gz"), lax.axis_index("coarse"), lax.rem(lax.axis_index("pencil"), 2)
    lane = lanes((RE, 128))
    sides = []
    for from_z, inside in ((3, gz > 0), (1, gz < 3)):
        z = lax.rem(gz + from_z, 4) * 4
        rows = [
            z_ref[z + cy],
            jnp.where(cy < 3, z_ref[z + lax.rem(cy + 1, 4), :H], 0.0),
            jnp.where(cy > 0, z_ref[z + lax.rem(cy + 3, 4), :H], 0.0),
        ]
        sides.append(jnp.where(inside, jnp.concatenate(rows, axis=0), 0.0))
    for i, (own, ext) in enumerate(((u_ref, ue_ref), (k_ref, ke_ref), (f_ref, fe_ref))):
        scale = (lambda v: 0.5 * v) if i == 1 else (lambda v: v)
        for p in range(NX):
            g = i * NX + p
            t, q = divmod(g, 16)
            before, after = (side[:, t * 128 : t * 128 + 128] for side in sides)
            if (120 - H * q) % 128:
                before = pltpu.roll(before, (120 - H * q) % 128, 1)
            if q:
                after = pltpu.roll(after, 128 - H * q, 1)
            ext[p, :NY, :NZ] = scale(own[p])
            ext[p, NY : NY + H, :NZ] = scale(down_ref[g])
            ext[p, NY + H :, :NZ] = scale(up_ref[g])
            ext[p, :, NZ:] = scale(jnp.where(lane < H, after, jnp.where(lane >= 120, before, 0.0)))
    even = lanes((RE, ZE)) % 2 == 0
    flux_x = None
    r_pair = k_pair = None
    for p in range(NX):
        k, u = ke_ref[p], ue_ref[p]
        flux = (k + up(k, 1)) * (u - up(u, 1))
        out = flux - down(flux, 1)
        flux = (k + up(k, 0)) * (u - up(u, 0))
        out = out + (flux - down(flux, 0))
        if flux_x is not None:
            out = out - flux_x
        if p < NX - 1:
            flux_x = (k + ke_ref[p + 1]) * (u - ue_ref[p + 1])
            out = out + flux_x
        r = fe_ref[p] - out
        q = place(core, p, NX)
        r_in_ref[q] = inner_rows(r)
        k_in_ref[q] = inner_rows(k)
        if p % 2 == 0:
            r_pair, k_pair = r, k
        else:
            c = place(core, p // 2, CX)
            rc_ref[c] = restrict_plane(r_pair + r, tmp_ref, even, 0.125)
            kc_ref[c] = restrict_plane(k_pair + k, tmp_ref, even, 0.03125)
    for i in range(2):
        end = place(core, i * (NX - 1), NX)
        uo_ref[i], ko_ref[i] = ue_ref[end], ke_ref[end]
    even_c = lanes((CE, ZE)) % 2 == 0
    for i, ref in enumerate((link_ref, chip_ref)):
        at, step, c = i * (NX - 1), 1 - 2 * i, i * (CX - 1)
        tails = {}
        send_rows(ref, tails, X_U, uo_ref[i])
        send_rows(ref, tails, X_K, ko_ref[i])
        send_rows(ref, tails, X_K2, k_in_ref[at + step])
        send_rows(ref, tails, X_K3, k_in_ref[at + 2 * step, :NY])
        send_rows(ref, tails, X_R1, r_in_ref[at])
        send_rows(ref, tails, X_R2, r_in_ref[at + step, :NY])
        for d in range(CX):
            both = jnp.where(even_c, rc_ref[c + d * step], kc_ref[c + d * step])
            send_rows(ref, tails, X_C + 2 * d, both if d < 3 else both[:CY])
        send_tails(ref, tails)


def faces_yz(k, by=1):
    ky, kz = k + up(k, 0), k + up(k, 1, by)
    return ky, kz, (ky + down(ky, 0)) + (kz + down(kz, 1, by))


def flux_yz(v, ky, kz, by=1):
    flux = kz * (v - up(v, 1, by))
    out = flux - down(flux, 1, by)
    flux = ky * (v - up(v, 0))
    return out + (flux - down(flux, 0))


def inverse(k, diag, scale=1.0):
    return jnp.where(k > 0.0, scale / diag, 0.0)


def step_d1(r1, d0, inv):
    return (RHO1 * RHO0) * d0 + (2.0 * RHO1 / DELTA) * (r1 * inv)


def main(v):
    return v[:NY, :NZ]


def open_message(msg, u_end, k_end, r_end, rc_end, tmp_ref):
    even, even_c = lanes((RE, ZE)) % 2 == 0, lanes((CE, ZE)) % 2 == 0
    none = jnp.zeros((RF - NY, ZE), f32)
    un, kn = received_rows(msg, X_U, 4), received_rows(msg, X_K, 4)
    flux = (k_end + kn) * (u_end - un)
    inner = inner_rows(flux)
    coarse = restrict_plane(flux, tmp_ref, even, 0.125)
    ks = [inner_rows(kn), received_rows(msg, X_K2, 3)]
    ks.append(jnp.concatenate([received_rows(msg, X_K3, 2), none], axis=0))
    rs = [received_rows(msg, X_R1, 3) + inner]
    rs.append(jnp.concatenate([received_rows(msg, X_R2, 2), none], axis=0))
    kcs, rcs = [], []
    for d in range(CX):
        if d < 3:
            both = received_rows(msg, X_C + 2 * d, 2)
            rc = jnp.where(even_c, both, down(both, 1))
            rcs.append(rc + coarse if d == 0 else rc)
        else:
            both = jnp.concatenate([received_rows(msg, X_C + 2 * d, 1), none], axis=0)
        kcs.append(jnp.where(even_c, up(both, 1), both))
    return r_end - inner, ks, rs, rc_end - coarse, kcs, rcs


def chip_kernel(
    u_ref, uo_ref, ko_ref, k_ref, r_ref, rc_ref, kc_ref, msg_ref,
    ky_ref, kz_ref, inv_ref, d0_ref, r1_ref, d1_ref, sum_ref, smooth_ref,
    q_ref, s_ref, cy_ref, cz_ref, cinv_ref, e0_ref, e1_ref, e2_ref,
    kx_ref, rx_ref, tmp_ref,
):
    core = lax.rem(lax.axis_index("pencil"), 2)
    r_end, ks, rs, rc_end, kcs, rcs = open_message(
        msg_ref, uo_ref[1], ko_ref[1], r_ref[NX - 1], rc_ref[CX - 1], tmp_ref
    )
    for d, k in enumerate(ks):
        kx_ref[d] = k
    for d, r in enumerate([r_end] + rs):
        rx_ref[d] = r
    for c in range(CX):
        q_ref[c], q_ref[CX + c] = kc_ref[c], kcs[c]
        s_ref[c] = rc_ref[c] if c < CX - 1 else rc_end
        if c < 3:
            s_ref[CX + c] = rcs[c]

    def k_at(p):
        return k_ref[p] if p < NX else kx_ref[p - NX]

    def r_at(p):
        return r_ref[p] if p < NX - 1 else rx_ref[p - NX + 1]

    kx = None
    for p in range(NX + 2):
        k = k_at(p)
        ky_ref[p], kz_ref[p], diag = faces_yz(k)
        before, kx = kx, k + k_at(p + 1)
        if p == 0:
            inv_ref[p] = diag + kx
        else:
            inv = inverse(k, diag + before + kx)
            inv_ref[p] = inv
            d0_ref[p] = r_at(p) * inv * (1.0 / THETA)
    flux_x = (k_at(1) + k_at(2)) * (d0_ref[1] - d0_ref[2])
    for p in range(2, NX + 1):
        d0 = d0_ref[p]
        out = flux_yz(d0, ky_ref[p], kz_ref[p]) - flux_x
        flux_x = (k_at(p) + k_at(p + 1)) * (d0 - d0_ref[p + 1])
        r1 = r_at(p) - (out + flux_x)
        d1 = step_d1(r1, d0, inv_ref[p])
        r1_ref[p], d1_ref[p] = r1, d1
        if p < NX:
            sum_ref[p] = u_ref[place(core, p, NX)] + main(d0) + main(d1)
    flux_x = main((k_at(2) + k_at(3)) * (d1_ref[2] - d1_ref[3]))
    for p in range(3, NX):
        d1 = d1_ref[p]
        out = main(flux_yz(d1, ky_ref[p], kz_ref[p])) - flux_x
        flux_x = main((k_at(p) + k_at(p + 1)) * (d1 - d1_ref[p + 1]))
        smooth_ref[p] = main(r1_ref[p]) - (out + flux_x)

    kx = None
    for c in range(CX + 3):
        k = q_ref[c]
        cy_ref[c], cz_ref[c], diag = faces_yz(k, 2)
        before, kx = kx, k + q_ref[c + 1]
        if c == 0:
            cinv_ref[c] = diag + kx
        else:
            inv = inverse(k, diag + before + kx, 0.8)
            cinv_ref[c] = inv
            e0_ref[c] = s_ref[c] * inv
    for now, then, first, last in ((e0_ref, e1_ref, 2, CX + 1), (e1_ref, e2_ref, 3, CX)):
        flux_x = (q_ref[first - 1] + q_ref[first]) * (now[first - 1] - now[first])
        for c in range(first, last + 1):
            e = now[c]
            out = flux_yz(e, cy_ref[c], cz_ref[c], 2) - flux_x
            flux_x = (q_ref[c] + q_ref[c + 1]) * (e - now[c + 1])
            then[c] = e + cinv_ref[c] * (s_ref[c] - (out + flux_x))


def final_kernel(
    u_ref, uo_ref, ko_ref, k_ref, r_ref,
    ky_ref, kz_ref, inv_ref, d0_ref, r1_ref, d1_ref, sum_ref, smooth_ref,
    q_ref, s_ref, cy_ref, cz_ref, cinv_ref, e0_ref, e1_ref, e2_ref, msg_ref,
    new_hbm, smooth_hbm,
    k_x, r_x, ky_x, kz_x, inv_x, d0_x, d1_x, q_x, s_x, cy_x, cz_x, cinv_x, e0_x, e1_x, e2_x,
    tmp_ref, lift_ref, new_ref, out_ref, new_sem, smooth_sem,
):
    core = lax.rem(lax.axis_index("pencil"), 2)
    copies = []

    def put(src, dst, sem, p):
        copies.append(pltpu.make_async_copy(src, dst.at[place(core, p, NX)], sem.at[p]))
        copies[-1].start()

    for p in range(3, NX):
        put(smooth_ref.at[p], smooth_hbm, smooth_sem, p)
    OFF, COFF = 3, 4
    r_end, ks, rs, rc_end, kcs, rcs = open_message(
        msg_ref, uo_ref[0], ko_ref[0], r_ref[0], s_ref[0], tmp_ref
    )
    for d, k in enumerate(ks):
        k_x[OFF - 1 - d] = k
    for d, r in enumerate([r_end] + rs):
        r_x[OFF - d] = r
    for d, k in enumerate(kcs):
        q_x[COFF - 1 - d] = k
    for d, r in enumerate([rc_end] + rcs):
        s_x[COFF - d] = r

    def at(near, own, p, first=0, off=OFF):
        return own[p] if p >= first else near[off + p]

    def k_at(p):
        return at(k_x, k_ref, p)

    def d0_at(p):
        return at(d0_x, d0_ref, p, 1)

    def d1_at(p):
        return at(d1_x, d1_ref, p, 2)

    kx = k_at(-3) + k_at(-2)
    for p in range(-2, 1):
        k = k_at(p)
        before, kx = kx, k + k_at(p + 1)
        if p < 0:
            ky_x[OFF + p], kz_x[OFF + p], diag = faces_yz(k)
            diag = diag + before + kx
        else:
            diag = inv_ref[p] + before
        inv = inverse(k, diag)
        inv_x[OFF + p] = inv
        d0_x[OFF + p] = r_x[OFF + p] * inv * (1.0 / THETA)
    flux_x = (k_at(-2) + k_at(-1)) * (d0_at(-2) - d0_at(-1))
    for p in range(-1, 2):
        d0 = d0_at(p)
        out = flux_yz(d0, at(ky_x, ky_ref, p), at(kz_x, kz_ref, p)) - flux_x
        flux_x = (k_at(p) + k_at(p + 1)) * (d0 - d0_at(p + 1))
        r1 = at(r_x, r_ref, p, 1) - (out + flux_x)
        r_x[OFF + p] = r1
        d1_x[OFF + p] = step_d1(r1, d0, at(inv_x, inv_ref, p, 1))
    flux_x = main((k_at(-1) + k_at(0)) * (d1_at(-1) - d1_at(0)))
    for p in range(3):
        d1 = d1_at(p)
        out = main(flux_yz(d1, ky_ref[p], kz_ref[p])) - flux_x
        flux_x = main((k_at(p) + k_at(p + 1)) * (d1 - d1_at(p + 1)))
        out_ref[p] = main(at(r_x, r1_ref, p, 2)) - (out + flux_x)
        put(out_ref.at[p], smooth_hbm, smooth_sem, p)

    def q_at(c):
        return at(q_x, q_ref, c, 0, COFF)

    kx = q_at(-4) + q_at(-3)
    for c in range(-3, 1):
        k = q_at(c)
        before, kx = kx, k + q_at(c + 1)
        if c < 0:
            cy_x[COFF + c], cz_x[COFF + c], diag = faces_yz(k, 2)
            diag = diag + before + kx
        else:
            diag = cinv_ref[c] + before
        inv = inverse(k, diag, 0.8)
        cinv_x[COFF + c] = inv
        e0_x[COFF + c] = s_x[COFF + c] * inv
    for (near, own, known), store, first in (
        ((e0_x, e0_ref, 1), e1_x, -2), ((e1_x, e1_ref, 2), e2_x, -1), ((e2_x, e2_ref, 3), None, 0)
    ):
        def e_at(c):
            return at(near, own, c, known, COFF)

        flux_x = (q_at(first - 1) + q_at(first)) * (e_at(first - 1) - e_at(first))
        for c in range(first, first + 4):
            e = e_at(c)
            cy, cz = at(cy_x, cy_ref, c, 0, COFF), at(cz_x, cz_ref, c, 0, COFF)
            out = flux_yz(e, cy, cz, 2) - flux_x
            flux_x = (q_at(c) + q_at(c + 1)) * (e - e_at(c + 1))
            rest = at(s_x, s_ref, c, 1, COFF) - (out + flux_x)
            e = e + at(cinv_x, cinv_ref, c, 1, COFF) * rest
            if store is not None:
                store[COFF + c] = e
                continue
            cols = []
            for t in range(NZ // 128):
                part = e[:CY, t * 128 : (t + 1) * 128]
                tile = lift_ref.at[t]
                tile[pl.ds(0, CY, stride=2), :] = part
                tile[pl.ds(1, CY, stride=2), :] = part
                cols.append(tile[...])
            lifted = jnp.concatenate(cols, axis=1)
            for p in (2 * c, 2 * c + 1):
                if p < 2:
                    done = u_ref[place(core, p, NX)] + main(d0_at(p)) + main(d1_at(p))
                else:
                    done = sum_ref[p]
                new_ref[p] = done + lifted
                put(new_ref.at[p], new_hbm, new_sem, p)
    for copy in copies:
        copy.wait()


def call(kernel, outs, specs, scratch, bytes_accessed, flops):
    spaces = {"s": pltpu.SMEM, "v": pltpu.VMEM, "h": pltpu.HBM}
    return pl.pallas_call(
        kernel,
        out_shape=[jax.ShapeDtypeStruct(tuple(s), f32) for s in outs],
        in_specs=[pl.BlockSpec(memory_space=spaces[s]) for s in specs],
        out_specs=[
            pl.BlockSpec(memory_space=pl.ANY if isinstance(s, list) else pltpu.VMEM) for s in outs
        ],
        scratch_shapes=[pltpu.VMEM(s, f32) if isinstance(s, tuple) else s for s in scratch],
        compiler_params=pltpu.CompilerParams(vmem_limit_bytes=16 << 20),
        cost_estimate=pl.CostEstimate(flops=flops, bytes_accessed=bytes_accessed, transcendentals=0),
    )


def shifted(cells, axis, by):
    count = lax.axis_size(axis)
    return lax.ppermute(cells, axis, [(i, i + by) for i in range(count) if 0 <= i + by < count])


def swapped(cells, axis, first):
    count = lax.axis_size(axis)
    pairs = []
    for i in range(first, count - 1, 2):
        pairs += [(i, i + 1), (i + 1, i)]
    return lax.ppermute(cells, axis, pairs)


def on_device(right_side, conductivity, guess):
    own = (NX, NY, NZ)
    dma = pltpu.SemaphoreType.DMA
    u, k, f, upward, downward, ends = call(
        pack_kernel,
        [own, own, own, (GROUPS, H, NZ), (GROUPS, H, NZ), [16, NY, 256]],
        "hhh", [(2, NY, 256), dma((6,)), dma((6,))], 1 << 20, 1 << 18,
    )(*(pltpu.with_memory_space_constraint(a, pltpu.HBM) for a in (guess, conductivity, right_side)))
    upward = shifted(upward, "coarse", 1)
    downward = shifted(downward, "coarse", -1)
    ends = lax.all_to_all(ends, ("gz", "coarse"), 0, 0)

    def fine(n):
        return (n, RF, ZE)

    def coarse(n):
        return (n, CE, ZE)

    message = (X_GROUPS + 2, 8, NZ)
    uo, ko, k_in, r_in, rc, kc, chip, link = call(
        block_kernel,
        [(2, RE, ZE), (2, RE, ZE), fine(NX), fine(NX), coarse(CX), coarse(CX), message, message],
        "vvvvvv", [(NX, RE, ZE)] * 3 + [(ZE // 128, RE, 128)], 3 << 20, 1 << 22,
    )(u, k, f, upward, downward, ends)
    chip = swapped(chip, "pencil", 0)
    link = swapped(link, "pencil", 1)
    half = call(
        chip_kernel,
        [fine(NX + 2)] * 4 + [fine(NX + 1)] * 2 + [own, own]
        + [coarse(2 * CX)] + [coarse(CX + 3)] * 7,
        "vvvvvvvv", [fine(3), fine(3), (ZE // 128, RE, 128)], 4 << 20, 1 << 22,
    )(u, uo, ko, k_in, r_in, rc, kc, chip)
    return tuple(
        call(
            final_kernel, [list(own), list(own)], "v" * 22,
            [fine(3), fine(5)] + [fine(5)] * 5 + [coarse(4)] + [coarse(8)] * 7
            + [(ZE // 128, RE, 128), (NZ // 128, NY, 128), own, (3, NY, NZ), dma((NX,)), dma((NX,))],
            4 << 20, 1 << 22,
        )(u, uo, ko, k_in, r_in, *half, link)
    )


def solution(mesh):
    spec = P("pencil", "coarse", "gz")
    return jax.shard_map(
        on_device,
        mesh=mesh,
        in_specs=(spec, spec, spec),
        out_specs=(spec, spec),
        check_vma=False,
    )
```

time: 188 us -> 37 us (0.20)
  the two profiles are of different devices: /device:TPU:128 before, /device:TPU:1 now
where the time goes in v2:
time: 37 us; the launch traced here: 36.7 us
  starting transfers between devices  19.3 us (52%)
  waiting for transfers between devices  9.08 us (25%)
  Pallas kernels  7.6 us (21%)
  between operations  0.7 us (2%)
    all_to_all x1, starting transfers between devices, on_device(): ends = lax.all_to_all(ends, ('gz', 'coarse'), 0, 0)  7.59 us
    ppermute x2, starting transfers between devices, swapped(): return lax.ppermute(cells, axis, pairs)  7.19 us
    ppermute x2, waiting for transfers between devices, shifted(): lax.ppermute(cells, axis, [(i, i + by) for i in range(count) if 0 <= i +...  6.12 us
    ppermute x2, starting transfers between devices, shifted(): lax.ppermute(cells, axis, [(i, i + by) for i in range(count) if 0 <= i +...  4.56 us
    ppermute x2, waiting for transfers between devices, swapped(): return lax.ppermute(cells, axis, pairs)  2.95 us
    pallas_call x1, Pallas kernels, on_device(): call(chip_kernel, [fine(NX + 2)] * 4 + [fine(NX + 1)] * 2 + [own, own] +...  2.36 us
    pallas_call x1, Pallas kernels, on_device(): call(pack_kernel, [own, own, own, (GROUPS, H, NZ), (GROUPS, H, NZ), [16,...  1.89 us
    pallas_call x1, Pallas kernels, on_device(): call(final_kernel, [list(own), list(own)], 'v' * 22, [fine(3), fine(5)] +...  1.71 us
  transfers between devices with their start and end apart: 5, of which 3 were waited for; matrix products, arithmetic and copies ran while one was open for 0% of the time, Pallas kernels for 6%

profile of v2, /device:TPU:1, one launch (start us, length us, event | category | flops | bytes accessed | tf_op | source)
XLA Modules:
  0.0 36.7 jit_solution(694046443403780101)
XLA Ops:
  0.6 1.9 %shard_map.50 = (f32[8,16,256]{2,1,0:T(8,128)S(1)}, f32[8,16,256]{2,1,0:T(8,128)S(1)}, f32[8,16,256]{2,1,0:T(8,128)S(1)}, f32[24,8,256]{2,1,0:T(8,128)S(1)}, f32...) custom-call(f32[8,16,256]{2,1,0:T(8,128)} %u_hbm.1, f32[8,16,256]{2,1,0:T(8,128)} %k_hbm.1, f32[8,16,256]{2,1,0:T(8,128)} %f_hbm.1), custom_call_target="tpu_custom_call" | custom-call | flops 262144 | bytes 1048576 | tf_op jit(solution)/shard_map/pallas_call | solution.py:483
  2.5 7.6 %all-to-all-start = ((f32[16,16,256]{2,1,0:T(8,128)}), f32[16,16,256]{2,1,0:T(8,128)S(1)}, u32[]{:S(2)}, u32[]{:S(2)}) async-start(f32[16,16,256]{2,1,0:T(8,128)} %get-tuple-element.37), calls=%async_computation | async-start | bytes 524288 | tf_op jit(solution)/shard_map/all_to_all | solution.py:490
  10.1 3.3 %collective-permute-start = (f32[24,8,256]{2,1,0:T(8,128)S(1)}, f32[24,8,256]{2,1,0:T(8,128)S(1)}, u32[]{:S(2)}, u32[]{:S(2)}) collective-permute-start(f32[24,8,256]{2,1,0:T(8,128)S(1)} %get-tuple-element.35), channel_id=1, source_target_pairs={{0,1},{1,2},{2,3},{4,5},{5,6},{6,7},{8,9},{9,10},{10,11},{12,13},{... | collective-permute-start | bytes 589832 | tf_op jit(solution)/shard_map/ppermute | solution.py:469
  13.4 1.3 %collective-permute-start.1 = (f32[24,8,256]{2,1,0:T(8,128)S(1)}, f32[24,8,256]{2,1,0:T(8,128)S(1)}, u32[]{:S(2)}, u32[]{:S(2)}) collective-permute-start(f32[24,8,256]{2,1,0:T(8,128)S(1)} %get-tuple-element.36), channel_id=1, source_target_pairs={{1,0},{2,1},{3,2},{5,4},{6,5},{7,6},{9,8},{10,9},{11,10},{13,12},{... | collective-permute-start | bytes 589832 | tf_op jit(solution)/shard_map/ppermute | solution.py:469
  14.7 2.6 %collective-permute-done.up_ref = f32[24,8,256]{2,1,0:T(8,128)S(1)} collective-permute-done((f32[24,8,256]{2,1,0:T(8,128)S(1)}, f32[24,8,256]{2,1,0:T(8,128)S(1)}, u32[]{:S(2)}, u32[]{:S(2)}) %collective-permute-start) | collective-permute-done | bytes 196640 | tf_op jit(solution)/shard_map/ppermute | solution.py:469
  17.3 3.6 %collective-permute-done.1.down_ref = f32[24,8,256]{2,1,0:T(8,128)S(1)} collective-permute-done((f32[24,8,256]{2,1,0:T(8,128)S(1)}, f32[24,8,256]{2,1,0:T(8,128)S(1)}, u32[]{:S(2)}, u32[]{:S(2)}) %collective-permute-start.1) | collective-permute-done | bytes 196640 | tf_op jit(solution)/shard_map/ppermute | solution.py:469
  20.8 0.0 all-to-all-done.z_ref
  20.8 1.6 %shard_map.51 = (f32[2,32,384]{2,1,0:T(8,128)S(1)}, f32[2,32,384]{2,1,0:T(8,128)S(1)}, f32[8,24,384]{2,1,0:T(8,128)S(1)}, f32[8,24,384]{2,1,0:T(8,128)S(1)}, f32...) custom-call(f32[8,16,256]{2,1,0:T(8,128)S(1)} %get-tuple-element.32.u, ...), custom_call_target="tpu_custom_call" | custom-call | flops 4194304 | bytes 3145728 | tf_op jit(solution)/shard_map/pallas_call | solution.py:499
  22.5 5.3 %collective-permute-start.2 = (f32[27,8,256]{2,1,0:T(8,128)S(1)}, f32[27,8,256]{2,1,0:T(8,128)S(1)}, u32[]{:S(2)}, u32[]{:S(2)}) collective-permute-start(f32[27,8,256]{2,1,0:T(8,128)S(1)} %get-tuple-element.44), channel_id=1, source_target_pairs={{0,16},{16,0},{32,48},{48,32},{64,80},{80,64},{96,112},{112,96},{1... | collective-permute-start | bytes 663560 | tf_op jit(solution)/shard_map/ppermute | solution.py:477
  27.8 1.9 %collective-permute-start.3 = (f32[27,8,256]{2,1,0:T(8,128)S(1)}, f32[27,8,256]{2,1,0:T(8,128)S(1)}, u32[]{:S(2)}, u32[]{:S(2)}) collective-permute-start(f32[27,8,256]{2,1,0:T(8,128)S(1)} %get-tuple-element.61), channel_id=1, source_target_pairs={{16,32},{32,16},{48,64},{64,48},{80,96},{96,80},{112,128},{128,112... | collective-permute-start | bytes 663560 | tf_op jit(solution)/shard_map/ppermute | solution.py:477
  29.7 0.0 collective-permute-done.2.msg_ref
  29.7 2.4 %shard_map.52 = (f32[10,24,384]{2,1,0:T(8,128)S(1)}, f32[10,24,384]{2,1,0:T(8,128)S(1)}, f32[10,24,384]{2,1,0:T(8,128)S(1)}, f32[10,24,384]{2,1,0:T(8,128)S(1)},...) custom-call(f32[8,16,256]{2,1,0:T(8,128)S(1)} %get-tuple-element.32., ...), custom_call_target="tpu_custom_call" | custom-call | flops 4194304 | bytes 4194304 | tf_op jit(solution)/shard_map/pallas_call | solution.py:506
  32.1 2.9 %collective-permute-done.3.msg_ref = f32[27,8,256]{2,1,0:T(8,128)S(1)} collective-permute-done((f32[27,8,256]{2,1,0:T(8,128)S(1)}, f32[27,8,256]{2,1,0:T(8,128)S(1)}, u32[]{:S(2)}, u32[]{:S(2)}) %collective-permute-start.3) | collective-permute-done | bytes 221216 | tf_op jit(solution)/shard_map/ppermute | solution.py:477
  35.0 1.7 %shard_map.53 = (f32[8,16,256]{2,1,0:T(8,128)}, f32[8,16,256]{2,1,0:T(8,128)}) custom-call(f32[8,16,256]{2,1,0:T(8,128)S(1)} %get-tuple-element.32.u_ref, f32[2,32,384]{2,1,0:T(8,128)S(1)} %get-tuple-element.38.uo_ref, f32[2,32,384]{2,1,0:T(8,128)S(1)} %get-tuple-element.39.ko_ref, f32[8,24,384]{2,1,0:T(8,128)S(1)} %get-tuple-element.40.k_ref, ...), custom_call_target="tpu_custom_call" | custom-call | flops 4194304 | bytes 4194304 | tf_op jit(solution)/shard_map/pallas_call | solution.py:513
Async XLA Ops:
  2.5 18.3 %all-to-all-start = ((f32[16,16,256]{2,1,0:T(8,128)}), f32[16,16,256]{2,1,0:T(8,128)S(1)}, u32[]{:S(2)}, u32[]{:S(2)}) async-start(f32[16,16,256]{2,1,0:T(8,128)} %get-tuple-element.37), calls=%async_computation | async-start | bytes 524288 | tf_op jit(solution)/shard_map/all_to_all | solution.py:490
  10.1 7.1 %collective-permute-start = (f32[24,8,256]{2,1,0:T(8,128)S(1)}, f32[24,8,256]{2,1,0:T(8,128)S(1)}, u32[]{:S(2)}, u32[]{:S(2)}) collective-permute-start(f32[24,8,256]{2,1,0:T(8,128)S(1)} %get-tuple-element.35), channel_id=1, source_target_pairs={{0,1},{1,2},{2,3},{4,5},{5,6},{6,7},{8,9},{9,10},{10,11},{12,13},{... | collective-permute-start | bytes 589832 | tf_op jit(solution)/shard_map/ppermute | solution.py:469
  13.4 7.4 %collective-permute-start.1 = (f32[24,8,256]{2,1,0:T(8,128)S(1)}, f32[24,8,256]{2,1,0:T(8,128)S(1)}, u32[]{:S(2)}, u32[]{:S(2)}) collective-permute-start(f32[24,8,256]{2,1,0:T(8,128)S(1)} %get-tuple-element.36), channel_id=1, source_target_pairs={{1,0},{2,1},{3,2},{5,4},{6,5},{7,6},{9,8},{10,9},{11,10},{13,12},{... | collective-permute-start | bytes 589832 | tf_op jit(solution)/shard_map/ppermute | solution.py:469
  22.5 7.2 %collective-permute-start.2 = (f32[27,8,256]{2,1,0:T(8,128)S(1)}, f32[27,8,256]{2,1,0:T(8,128)S(1)}, u32[]{:S(2)}, u32[]{:S(2)}) collective-permute-start(f32[27,8,256]{2,1,0:T(8,128)S(1)} %get-tuple-element.44), channel_id=1, source_target_pairs={{0,16},{16,0},{32,48},{48,32},{64,80},{80,64},{96,112},{112,96},{1... | collective-permute-start | bytes 663560 | tf_op jit(solution)/shard_map/ppermute | solution.py:477
  27.8 7.3 %collective-permute-start.3 = (f32[27,8,256]{2,1,0:T(8,128)S(1)}, f32[27,8,256]{2,1,0:T(8,128)S(1)}, u32[]{:S(2)}, u32[]{:S(2)}) collective-permute-start(f32[27,8,256]{2,1,0:T(8,128)S(1)} %get-tuple-element.61), channel_id=1, source_target_pairs={{16,32},{32,16},{48,64},{64,48},{80,96},{96,80},{112,128},{128,112... | collective-permute-start | bytes 663560 | tf_op jit(solution)/shard_map/ppermute | solution.py:477

commit v3 on v2

--- a/solution.py
+++ b/solution.py
@@ -186,8 +186,8 @@
             r_pair, k_pair = r, k
         else:
             c = place(core, p // 2, CX)
-            rc_ref[c] = restrict_plane(r_pair + r, tmp_ref, even, 0.125)
-            kc_ref[c] = restrict_plane(k_pair + k, tmp_ref, even, 0.03125)
+            rc_ref[c] = restrict_plane(r_pair + r, tmp_ref.at[p - 1], even, 0.125)
+            kc_ref[c] = restrict_plane(k_pair + k, tmp_ref.at[p], even, 0.03125)
     for i in range(2):
         end = place(core, i * (NX - 1), NX)
         uo_ref[i], ko_ref[i] = ue_ref[end], ke_ref[end]
@@ -254,84 +254,195 @@
     return r_end - inner, ks, rs, rc_end - coarse, kcs, rcs
 
 
-def chip_kernel(
-    u_ref, uo_ref, ko_ref, k_ref, r_ref, rc_ref, kc_ref, msg_ref,
+OFF, COFF = 3, 4
+
+
+def at(near, own, s, first, inward, off=OFF):
+    return own[inward(s)] if s >= first else near[off + s]
+
+
+def fine_side(opened, inward, own, near, emit):
+    r_end, ks, rs = opened[:3]
+    k, r, ky, kz, inv, d0, r1, d1 = own
+    k_x, r_x, ky_x, kz_x, inv_x, d0_x, d1_x = near
+    for d, plane in enumerate(ks):
+        k_x[OFF - 1 - d] = plane
+    for d, plane in enumerate([r_end] + rs):
+        r_x[OFF - d] = plane
+
+    def k_at(s):
+        return at(k_x, k, s, 0, inward)
+
+    def d0_at(s):
+        return at(d0_x, d0, s, 1, inward)
+
+    def d1_at(s):
+        return at(d1_x, d1, s, 2, inward)
+
+    def faces_at(s):
+        return at(ky_x, ky, s, 0, inward), at(kz_x, kz, s, 0, inward)
+
+    kx = k_at(-3) + k_at(-2)
+    for s in range(-2, 1):
+        kv = k_at(s)
+        before, kx = kx, kv + k_at(s + 1)
+        if s < 0:
+            ky_x[OFF + s], kz_x[OFF + s], diag = faces_yz(kv)
+            diag = diag + before + kx
+        else:
+            diag = inv[inward(0)] + before
+        scale = inverse(kv, diag)
+        inv_x[OFF + s] = scale
+        d0_x[OFF + s] = r_x[OFF + s] * scale * (1.0 / THETA)
+    flux_x = (k_at(-2) + k_at(-1)) * (d0_at(-2) - d0_at(-1))
+    for s in range(-1, 2):
+        v = d0_at(s)
+        out = flux_yz(v, *faces_at(s)) - flux_x
+        flux_x = (k_at(s) + k_at(s + 1)) * (v - d0_at(s + 1))
+        rv = at(r_x, r, s, 1, inward) - (out + flux_x)
+        r_x[OFF + s] = rv
+        d1_x[OFF + s] = step_d1(rv, v, at(inv_x, inv, s, 1, inward))
+    flux_x = main((k_at(-1) + k_at(0)) * (d1_at(-1) - d1_at(0)))
+    for s in range(3):
+        v = d1_at(s)
+        out = main(flux_yz(v, *faces_at(s))) - flux_x
+        flux_x = main((k_at(s) + k_at(s + 1)) * (v - d1_at(s + 1)))
+        rest = main(at(r_x, r1, s, 2, inward)) - (out + flux_x)
+        emit(s, rest, main(d0_at(s)) + main(v) if s < 2 else None)
+
+
+def coarse_side(opened, inward, kc, cinv, near):
+    rc_end, kcs, rcs = opened[3:]
+    q_x, s_x, cy_x, cz_x, cinv_x, e0_x = near
+    for d, plane in enumerate(kcs):
+        q_x[COFF - 1 - d] = plane
+    for d, plane in enumerate([rc_end] + rcs):
+        s_x[COFF - d] = plane
+    kx = q_x[COFF - 4] + q_x[COFF - 3]
+    for s in range(-3, 1):
+        k = at(q_x, kc, s, 0, inward, COFF)
+        before, kx = kx, k + at(q_x, kc, s + 1, 0, inward, COFF)
+        if s < 0:
+            cy_x[COFF + s], cz_x[COFF + s], diag = faces_yz(k, 2)
+            diag = diag + before + kx
+        else:
+            diag = cinv[inward(0)] + before
+        scale = inverse(k, diag, 0.8)
+        cinv_x[COFF + s] = scale
+        e0_x[COFF + s] = s_x[COFF + s] * scale
+
+
+def sweep(first, last, e_at, q_at, rc_at, cy_at, cz_at, cinv_at, emit):
+    flux_x = (q_at(first - 1) + q_at(first)) * (e_at(first - 1) - e_at(first))
+    for c in range(first, last + 1):
+        e = e_at(c)
+        out = flux_yz(e, cy_at(c), cz_at(c), 2) - flux_x
+        flux_x = (q_at(c) + q_at(c + 1)) * (e - e_at(c + 1))
+        emit(c, e + cinv_at(c) * (rc_at(c) - (out + flux_x)))
+
+
+def mid_kernel(
+    u_ref, k_ref, r_ref, rc_ref, kc_ref,
     ky_ref, kz_ref, inv_ref, d0_ref, r1_ref, d1_ref, sum_ref, smooth_ref,
-    q_ref, s_ref, cy_ref, cz_ref, cinv_ref, e0_ref, e1_ref, e2_ref,
-    kx_ref, rx_ref, tmp_ref,
+    cy_ref, cz_ref, cinv_ref, e0_ref,
 ):
     core = lax.rem(lax.axis_index("pencil"), 2)
-    r_end, ks, rs, rc_end, kcs, rcs = open_message(
-        msg_ref, uo_ref[1], ko_ref[1], r_ref[NX - 1], rc_ref[CX - 1], tmp_ref
-    )
-    for d, k in enumerate(ks):
-        kx_ref[d] = k
-    for d, r in enumerate([r_end] + rs):
-        rx_ref[d] = r
-    for c in range(CX):
-        q_ref[c], q_ref[CX + c] = kc_ref[c], kcs[c]
-        s_ref[c] = rc_ref[c] if c < CX - 1 else rc_end
-        if c < 3:
-            s_ref[CX + c] = rcs[c]
-
-    def k_at(p):
-        return k_ref[p] if p < NX else kx_ref[p - NX]
-
-    def r_at(p):
-        return r_ref[p] if p < NX - 1 else rx_ref[p - NX + 1]
-
     kx = None
-    for p in range(NX + 2):
-        k = k_at(p)
+    for p in range(NX):
+        k = k_ref[p]
         ky_ref[p], kz_ref[p], diag = faces_yz(k)
-        before, kx = kx, k + k_at(p + 1)
-        if p == 0:
-            inv_ref[p] = diag + kx
+        if kx is not None:
+            diag = diag + kx
+        if p < NX - 1:
+            kx = k + k_ref[p + 1]
+            diag = diag + kx
+        if 0 < p < NX - 1:
+            inv = inverse(k, diag)
+            inv_ref[p] = inv
+            d0_ref[p] = r_ref[p] * inv * (1.0 / THETA)
         else:
-            inv = inverse(k, diag + before + kx)
-            inv_ref[p] = inv
-            d0_ref[p] = r_at(p) * inv * (1.0 / THETA)
-    flux_x = (k_at(1) + k_at(2)) * (d0_ref[1] - d0_ref[2])
-    for p in range(2, NX + 1):
+            inv_ref[p] = diag
+    flux_x = (k_ref[1] + k_ref[2]) * (d0_ref[1] - d0_ref[2])
+    for p in range(2, NX - 2):
         d0 = d0_ref[p]
         out = flux_yz(d0, ky_ref[p], kz_ref[p]) - flux_x
-        flux_x = (k_at(p) + k_at(p + 1)) * (d0 - d0_ref[p + 1])
-        r1 = r_at(p) - (out + flux_x)
+        flux_x = (k_ref[p] + k_ref[p + 1]) * (d0 - d0_ref[p + 1])
+        r1 = r_ref[p] - (out + flux_x)
         d1 = step_d1(r1, d0, inv_ref[p])
         r1_ref[p], d1_ref[p] = r1, d1
-        if p < NX:
-            sum_ref[p] = u_ref[place(core, p, NX)] + main(d0) + main(d1)
-    flux_x = main((k_at(2) + k_at(3)) * (d1_ref[2] - d1_ref[3]))
-    for p in range(3, NX):
+        sum_ref[p] = u_ref[place(core, p, NX)] + main(d0) + main(d1)
+    flux_x = main((k_ref[2] + k_ref[3]) * (d1_ref[2] - d1_ref[3]))
+    for p in range(3, NX - 3):
         d1 = d1_ref[p]
         out = main(flux_yz(d1, ky_ref[p], kz_ref[p])) - flux_x
-        flux_x = main((k_at(p) + k_at(p + 1)) * (d1 - d1_ref[p + 1]))
+        flux_x = main((k_ref[p] + k_ref[p + 1]) * (d1 - d1_ref[p + 1]))
         smooth_ref[p] = main(r1_ref[p]) - (out + flux_x)
-
     kx = None
-    for c in range(CX + 3):
-        k = q_ref[c]
+    for c in range(CX):
+        k = kc_ref[c]
         cy_ref[c], cz_ref[c], diag = faces_yz(k, 2)
-        before, kx = kx, k + q_ref[c + 1]
-        if c == 0:
-            cinv_ref[c] = diag + kx
+        if kx is not None:
+            diag = diag + kx
+        if c < CX - 1:
+            kx = k + kc_ref[c + 1]
+            diag = diag + kx
+        if 0 < c < CX - 1:
+            inv = inverse(k, diag, 0.8)
+            cinv_ref[c] = inv
+            e0_ref[c] = rc_ref[c] * inv
         else:
-            inv = inverse(k, diag + before + kx, 0.8)
-            cinv_ref[c] = inv
-            e0_ref[c] = s_ref[c] * inv
-    for now, then, first, last in ((e0_ref, e1_ref, 2, CX + 1), (e1_ref, e2_ref, 3, CX)):
-        flux_x = (q_ref[first - 1] + q_ref[first]) * (now[first - 1] - now[first])
-        for c in range(first, last + 1):
-            e = now[c]
-            out = flux_yz(e, cy_ref[c], cz_ref[c], 2) - flux_x
-            flux_x = (q_ref[c] + q_ref[c + 1]) * (e - now[c + 1])
-            then[c] = e + cinv_ref[c] * (s_ref[c] - (out + flux_x))
+            cinv_ref[c] = diag
+
+
+def chip_kernel(
+    u_ref, uo_ref, ko_ref, k_ref, r_ref, rc_ref, kc_ref,
+    ky_ref, kz_ref, inv_ref, d0_ref, r1_ref, d1_ref,
+    cy_ref, cz_ref, cinv_ref, e0_ref, msg_ref,
+    sum_ref, smooth_ref, q_x, s_x, cinv_x, e1_x, e2_x,
+    k_x, r_x, ky_x, kz_x, inv_x, d0_x, d1_x, cy_x, cz_x, e0_x, tmp_ref,
+):
+    core = lax.rem(lax.axis_index("pencil"), 2)
+    opened = open_message(msg_ref, uo_ref[1], ko_ref[1], r_ref[NX - 1], rc_ref[CX - 1], tmp_ref)
+
+    def emit(s, rest, step):
+        smooth_ref[s] = rest
+        if s < 2:
+            sum_ref[s] = u_ref[place(core, NX - 1 - s, NX)] + step
+
+    fine_side(
+        opened, lambda s: NX - 1 - s,
+        (k_ref, r_ref, ky_ref, kz_ref, inv_ref, d0_ref, r1_ref, d1_ref),
+        (k_x, r_x, ky_x, kz_x, inv_x, d0_x, d1_x), emit,
+    )
+
+    def inward(s):
+        return CX - 1 - s
+
+    coarse_side(opened, inward, kc_ref, cinv_ref, (q_x, s_x, cy_x, cz_x, cinv_x, e0_x))
+
+    def pick(near, own, first):
+        return lambda s: at(near, own, s, first, inward, COFF)
+
+    rest = (
+        pick(q_x, kc_ref, 0), pick(s_x, rc_ref, 1), pick(cy_x, cy_ref, 0), pick(cz_x, cz_ref, 0),
+        pick(cinv_x, cinv_ref, 1),
+    )
+
+    def keep(ref):
+        def store(s, e):
+            ref[COFF + s] = e
+
+        return store
+
+    sweep(-2, 1, pick(e0_x, e0_ref, 1), *rest, keep(e1_x))
+    sweep(-1, 0, lambda s: e1_x[COFF + s], *rest, keep(e2_x))
 
 
 def final_kernel(
-    u_ref, uo_ref, ko_ref, k_ref, r_ref,
+    u_ref, uo_ref, ko_ref, k_ref, r_ref, rc_ref, kc_ref,
     ky_ref, kz_ref, inv_ref, d0_ref, r1_ref, d1_ref, sum_ref, smooth_ref,
-    q_ref, s_ref, cy_ref, cz_ref, cinv_ref, e0_ref, e1_ref, e2_ref, msg_ref,
+    cy_ref, cz_ref, cinv_ref, e0_ref,
+    sum_c, smooth_c, q_c, s_c, cinv_c, e1_c, e2_c, msg_ref,
     new_hbm, smooth_hbm,
     k_x, r_x, ky_x, kz_x, inv_x, d0_x, d1_x, q_x, s_x, cy_x, cz_x, cinv_x, e0_x, e1_x, e2_x,
     tmp_ref, lift_ref, new_ref, out_ref, new_sem, smooth_sem,
@@ -344,107 +455,61 @@
         copies[-1].start()
 
     for p in range(3, NX):
-        put(smooth_ref.at[p], smooth_hbm, smooth_sem, p)
-    OFF, COFF = 3, 4
-    r_end, ks, rs, rc_end, kcs, rcs = open_message(
-        msg_ref, uo_ref[0], ko_ref[0], r_ref[0], s_ref[0], tmp_ref
-    )
-    for d, k in enumerate(ks):
-        k_x[OFF - 1 - d] = k
-    for d, r in enumerate([r_end] + rs):
-        r_x[OFF - d] = r
-    for d, k in enumerate(kcs):
-        q_x[COFF - 1 - d] = k
-    for d, r in enumerate([rc_end] + rcs):
-        s_x[COFF - d] = r
-
-    def at(near, own, p, first=0, off=OFF):
-        return own[p] if p >= first else near[off + p]
-
-    def k_at(p):
-        return at(k_x, k_ref, p)
-
-    def d0_at(p):
-        return at(d0_x, d0_ref, p, 1)
-
-    def d1_at(p):
-        return at(d1_x, d1_ref, p, 2)
-
-    kx = k_at(-3) + k_at(-2)
-    for p in range(-2, 1):
-        k = k_at(p)
-        before, kx = kx, k + k_at(p + 1)
-        if p < 0:
-            ky_x[OFF + p], kz_x[OFF + p], diag = faces_yz(k)
-            diag = diag + before + kx
-        else:
-            diag = inv_ref[p] + before
-        inv = inverse(k, diag)
-        inv_x[OFF + p] = inv
-        d0_x[OFF + p] = r_x[OFF + p] * inv * (1.0 / THETA)
-    flux_x = (k_at(-2) + k_at(-1)) * (d0_at(-2) - d0_at(-1))
-    for p in range(-1, 2):
-        d0 = d0_at(p)
-        out = flux_yz(d0, at(ky_x, ky_ref, p), at(kz_x, kz_ref, p)) - flux_x
-        flux_x = (k_at(p) + k_at(p + 1)) * (d0 - d0_at(p + 1))
-        r1 = at(r_x, r_ref, p, 1) - (out + flux_x)
-        r_x[OFF + p] = r1
-        d1_x[OFF + p] = step_d1(r1, d0, at(inv_x, inv_ref, p, 1))
-    flux_x = main((k_at(-1) + k_at(0)) * (d1_at(-1) - d1_at(0)))
-    for p in range(3):
-        d1 = d1_at(p)
-        out = main(flux_yz(d1, ky_ref[p], kz_ref[p])) - flux_x
-        flux_x = main((k_at(p) + k_at(p + 1)) * (d1 - d1_at(p + 1)))
-        out_ref[p] = main(at(r_x, r1_ref, p, 2)) - (out + flux_x)
+        put(smooth_ref.at[p] if p < NX - 3 else smooth_c.at[NX - 1 - p], smooth_hbm, smooth_sem, p)
+    opened = open_message(msg_ref, uo_ref[0], ko_ref[0], r_ref[0], rc_ref[0], tmp_ref)
+
+    def emit(p, rest, step):
+        out_ref[p] = rest
         put(out_ref.at[p], smooth_hbm, smooth_sem, p)
-
-    def q_at(c):
-        return at(q_x, q_ref, c, 0, COFF)
-
-    kx = q_at(-4) + q_at(-3)
-    for c in range(-3, 1):
-        k = q_at(c)
-        before, kx = kx, k + q_at(c + 1)
-        if c < 0:
-            cy_x[COFF + c], cz_x[COFF + c], diag = faces_yz(k, 2)
-            diag = diag + before + kx
-        else:
-            diag = cinv_ref[c] + before
-        inv = inverse(k, diag, 0.8)
-        cinv_x[COFF + c] = inv
-        e0_x[COFF + c] = s_x[COFF + c] * inv
-    for (near, own, known), store, first in (
-        ((e0_x, e0_ref, 1), e1_x, -2), ((e1_x, e1_ref, 2), e2_x, -1), ((e2_x, e2_ref, 3), None, 0)
-    ):
-        def e_at(c):
-            return at(near, own, c, known, COFF)
-
-        flux_x = (q_at(first - 1) + q_at(first)) * (e_at(first - 1) - e_at(first))
-        for c in range(first, first + 4):
-            e = e_at(c)
-            cy, cz = at(cy_x, cy_ref, c, 0, COFF), at(cz_x, cz_ref, c, 0, COFF)
-            out = flux_yz(e, cy, cz, 2) - flux_x
-            flux_x = (q_at(c) + q_at(c + 1)) * (e - e_at(c + 1))
-            rest = at(s_x, s_ref, c, 1, COFF) - (out + flux_x)
-            e = e + at(cinv_x, cinv_ref, c, 1, COFF) * rest
-            if store is not None:
-                store[COFF + c] = e
-                continue
-            cols = []
-            for t in range(NZ // 128):
-                part = e[:CY, t * 128 : (t + 1) * 128]
-                tile = lift_ref.at[t]
-                tile[pl.ds(0, CY, stride=2), :] = part
-                tile[pl.ds(1, CY, stride=2), :] = part
-                cols.append(tile[...])
-            lifted = jnp.concatenate(cols, axis=1)
-            for p in (2 * c, 2 * c + 1):
-                if p < 2:
-                    done = u_ref[place(core, p, NX)] + main(d0_at(p)) + main(d1_at(p))
-                else:
-                    done = sum_ref[p]
-                new_ref[p] = done + lifted
-                put(new_ref.at[p], new_hbm, new_sem, p)
+        if p < 2:
+            new_ref[p] = u_ref[place(core, p, NX)] + step
+
+    fine_side(
+        opened, lambda s: s,
+        (k_ref, r_ref, ky_ref, kz_ref, inv_ref, d0_ref, r1_ref, d1_ref),
+        (k_x, r_x, ky_x, kz_x, inv_x, d0_x, d1_x), emit,
+    )
+    coarse_side(opened, lambda s: s, kc_ref, cinv_ref, (q_x, s_x, cy_x, cz_x, cinv_x, e0_x))
+
+    def pick(near, own, first, far=None, beyond=CX):
+        def read(c):
+            if c < first:
+                return near[COFF + c]
+            return own[c] if c < beyond else far[COFF + CX - 1 - c]
+
+        return read
+
+    rest = (
+        pick(q_x, kc_ref, 0, q_c), pick(s_x, rc_ref, 1, s_c, 3), pick(cy_x, cy_ref, 0),
+        pick(cz_x, cz_ref, 0), pick(cinv_x, cinv_ref, 1, cinv_c, 3),
+    )
+
+    def keep(ref):
+        def store(c, e):
+            ref[COFF + c] = e
+
+        return store
+
+    def lift(c, e):
+        cols = []
+        for t in range(NZ // 128):
+            part = e[:CY, t * 128 : (t + 1) * 128]
+            tile = lift_ref.at[2 * c + t]
+            tile[pl.ds(0, CY, stride=2), :] = part
+            tile[pl.ds(1, CY, stride=2), :] = part
+            cols.append(tile[...])
+        lifted = jnp.concatenate(cols, axis=1)
+        for p in (2 * c, 2 * c + 1):
+            if p < 2:
+                done = new_ref[p]
+            else:
+                done = sum_ref[p] if p < NX - 2 else sum_c[NX - 1 - p]
+            new_ref[p] = done + lifted
+            put(new_ref.at[p], new_hbm, new_sem, p)
+
+    sweep(-2, 1, pick(e0_x, e0_ref, 1), *rest, keep(e1_x))
+    sweep(-1, 2, pick(e1_x, None, 2, e1_c, 2), *rest, keep(e2_x))
+    sweep(0, 3, pick(e2_x, None, 3, e2_c, 3), *rest, lift)
     for copy in copies:
         copy.wait()
 
@@ -499,23 +564,27 @@
     uo, ko, k_in, r_in, rc, kc, chip, link = call(
         block_kernel,
         [(2, RE, ZE), (2, RE, ZE), fine(NX), fine(NX), coarse(CX), coarse(CX), message, message],
-        "vvvvvv", [(NX, RE, ZE)] * 3 + [(ZE // 128, RE, 128)], 3 << 20, 1 << 22,
+        "vvvvvv", [(NX, RE, ZE)] * 3 + [(NX, ZE // 128, RE, 128)], 3 << 20, 1 << 22,
     )(u, k, f, upward, downward, ends)
     chip = swapped(chip, "pencil", 0)
     link = swapped(link, "pencil", 1)
+    edges = (ZE // 128, RE, 128)
+    *fine_own, sums, smooth, cy, cz, cinv, e0 = call(
+        mid_kernel, [fine(NX)] * 6 + [own, own] + [coarse(CX)] * 4, "v" * 5, [],
+        4 << 20, 1 << 22,
+    )(u, k_in, r_in, rc, kc)
     half = call(
         chip_kernel,
-        [fine(NX + 2)] * 4 + [fine(NX + 1)] * 2 + [own, own]
-        + [coarse(2 * CX)] + [coarse(CX + 3)] * 7,
-        "vvvvvvvv", [fine(3), fine(3), (ZE // 128, RE, 128)], 4 << 20, 1 << 22,
-    )(u, uo, ko, k_in, r_in, rc, kc, chip)
+        [(2, NY, NZ), (3, NY, NZ)] + [coarse(5)] * 3 + [coarse(6)] * 2, "v" * 18,
+        [fine(3), fine(5)] + [fine(5)] * 5 + [coarse(5)] * 3 + [edges], 4 << 20, 1 << 22,
+    )(u, uo, ko, k_in, r_in, rc, kc, *fine_own, cy, cz, cinv, e0, chip)
     return tuple(
         call(
-            final_kernel, [list(own), list(own)], "v" * 22,
-            [fine(3), fine(5)] + [fine(5)] * 5 + [coarse(4)] + [coarse(8)] * 7
-            + [(ZE // 128, RE, 128), (NZ // 128, NY, 128), own, (3, NY, NZ), dma((NX,)), dma((NX,))],
+            final_kernel, [list(own), list(own)], "v" * 27,
+            [fine(3), fine(5)] + [fine(5)] * 5 + [coarse(5)] * 6 + [coarse(6), coarse(7)]
+            + [edges, (NX, NY, 128), own, (3, NY, NZ), dma((NX,)), dma((NX,))],
             4 << 20, 1 << 22,
-        )(u, uo, ko, k_in, r_in, *half, link)
+        )(u, uo, ko, k_in, r_in, rc, kc, *fine_own, sums, smooth, cy, cz, cinv, e0, *half, link)
     )
 
 

time: 37 us -> 37 us (level)
  Pallas kernels: 7.6 us -> 6.98 us
  waiting for transfers between devices: 9.08 us -> 9.65 us
    pallas_call x2 -> x3, Pallas kernels: 4.07 us -> 3.46 us  [the longest x1 1.69 us: on_device(): call(final_kernel, [list(own), list(own)], 'v' * 27, [fine(3), fine(5)] +...]
    ppermute x2, waiting for transfers between devices: 2.95 us -> 3.53 us  [swapped(): return lax.ppermute(cells, axis, pairs)]
  transfers between devices with their start and end apart: 5 -> 5, of which waited for: 3 -> 3; matrix products, arithmetic and copies ran while one was open for 0% -> 0% of each run, Pallas kernels for 6% -> 5%
where the time goes in v3:
time: 37 us; the launch traced here: 36.7 us
  starting transfers between devices  19.4 us (52%)
  waiting for transfers between devices  9.65 us (26%)
  Pallas kernels  6.98 us (19%)
  between operations  0.71 us (2%)
    all_to_all x1, starting transfers between devices, on_device(): ends = lax.all_to_all(ends, ('gz', 'coarse'), 0, 0)  7.59 us
    ppermute x2, starting transfers between devices, swapped(): return lax.ppermute(cells, axis, pairs)  7.2 us
    ppermute x2, waiting for transfers between devices, shifted(): lax.ppermute(cells, axis, [(i, i + by) for i in range(count) if 0 <= i +...  6.12 us
    ppermute x2, starting transfers between devices, shifted(): lax.ppermute(cells, axis, [(i, i + by) for i in range(count) if 0 <= i +...  4.56 us
    ppermute x2, waiting for transfers between devices, swapped(): return lax.ppermute(cells, axis, pairs)  3.53 us
    pallas_call x1, Pallas kernels, on_device(): call(pack_kernel, [own, own, own, (GROUPS, H, NZ), (GROUPS, H, NZ), [16,...  1.88 us
    pallas_call x1, Pallas kernels, on_device(): call(final_kernel, [list(own), list(own)], 'v' * 27, [fine(3), fine(5)] +...  1.69 us
    pallas_call x1, Pallas kernels, on_device(): call(block_kernel, [(2, RE, ZE), (2, RE, ZE), fine(NX), fine(NX), coarse(...  1.64 us
  transfers between devices with their start and end apart: 5, of which 3 were waited for; matrix products, arithmetic and copies ran while one was open for 0% of the time, Pallas kernels for 5%

profile of v3, /device:TPU:1, one launch (start us, length us, event | category | flops | bytes accessed | tf_op | source)
XLA Modules:
  0.0 36.7 jit_solution(14864637481806657413)
XLA Ops:
  0.6 1.9 %shard_map.50 = (f32[8,16,256]{2,1,0:T(8,128)S(1)}, f32[8,16,256]{2,1,0:T(8,128)S(1)}, f32[8,16,256]{2,1,0:T(8,128)S(1)}, f32[24,8,256]{2,1,0:T(8,128)S(1)}, f32...) custom-call(f32[8,16,256]{2,1,0:T(8,128)} %u_hbm.1, f32[8,16,256]{2,1,0:T(8,128)} %k_hbm.1, f32[8,16,256]{2,1,0:T(8,128)} %f_hbm.1), custom_call_target="tpu_custom_call" | custom-call | flops 262144 | bytes 1048576 | tf_op jit(solution)/shard_map/pallas_call | solution.py:548
  2.5 7.6 %all-to-all-start = ((f32[16,16,256]{2,1,0:T(8,128)}), f32[16,16,256]{2,1,0:T(8,128)S(1)}, u32[]{:S(2)}, u32[]{:S(2)}) async-start(f32[16,16,256]{2,1,0:T(8,128)} %get-tuple-element.40), calls=%async_computation | async-start | bytes 524288 | tf_op jit(solution)/shard_map/all_to_all | solution.py:555
  10.1 3.3 %collective-permute-start = (f32[24,8,256]{2,1,0:T(8,128)S(1)}, f32[24,8,256]{2,1,0:T(8,128)S(1)}, u32[]{:S(2)}, u32[]{:S(2)}) collective-permute-start(f32[24,8,256]{2,1,0:T(8,128)S(1)} %get-tuple-element.38), channel_id=1, source_target_pairs={{0,1},{1,2},{2,3},{4,5},{5,6},{6,7},{8,9},{9,10},{10,11},{12,13},{... | collective-permute-start | bytes 589832 | tf_op jit(solution)/shard_map/ppermute | solution.py:534
  13.4 1.3 %collective-permute-start.1 = (f32[24,8,256]{2,1,0:T(8,128)S(1)}, f32[24,8,256]{2,1,0:T(8,128)S(1)}, u32[]{:S(2)}, u32[]{:S(2)}) collective-permute-start(f32[24,8,256]{2,1,0:T(8,128)S(1)} %get-tuple-element.39), channel_id=1, source_target_pairs={{1,0},{2,1},{3,2},{5,4},{6,5},{7,6},{9,8},{10,9},{11,10},{13,12},{... | collective-permute-start | bytes 589832 | tf_op jit(solution)/shard_map/ppermute | solution.py:534
  14.7 2.6 %collective-permute-done.up_ref = f32[24,8,256]{2,1,0:T(8,128)S(1)} collective-permute-done((f32[24,8,256]{2,1,0:T(8,128)S(1)}, f32[24,8,256]{2,1,0:T(8,128)S(1)}, u32[]{:S(2)}, u32[]{:S(2)}) %collective-permute-start) | collective-permute-done | bytes 196640 | tf_op jit(solution)/shard_map/ppermute | solution.py:534
  17.3 3.6 %collective-permute-done.1.down_ref = f32[24,8,256]{2,1,0:T(8,128)S(1)} collective-permute-done((f32[24,8,256]{2,1,0:T(8,128)S(1)}, f32[24,8,256]{2,1,0:T(8,128)S(1)}, u32[]{:S(2)}, u32[]{:S(2)}) %collective-permute-start.1) | collective-permute-done | bytes 196640 | tf_op jit(solution)/shard_map/ppermute | solution.py:534
  20.8 0.0 all-to-all-done.z_ref
  20.8 1.6 %shard_map.51 = (f32[2,32,384]{2,1,0:T(8,128)S(1)}, f32[2,32,384]{2,1,0:T(8,128)S(1)}, f32[8,24,384]{2,1,0:T(8,128)S(1)}, f32[8,24,384]{2,1,0:T(8,128)S(1)}, f32...) custom-call(f32[8,16,256]{2,1,0:T(8,128)S(1)} %get-tuple-element.35.u, ...), custom_call_target="tpu_custom_call" | custom-call | flops 4194304 | bytes 3145728 | tf_op jit(solution)/shard_map/pallas_call | solution.py:564
  22.5 5.3 %collective-permute-start.2 = (f32[27,8,256]{2,1,0:T(8,128)S(1)}, f32[27,8,256]{2,1,0:T(8,128)S(1)}, u32[]{:S(2)}, u32[]{:S(2)}) collective-permute-start(f32[27,8,256]{2,1,0:T(8,128)S(1)} %get-tuple-element.59), channel_id=1, source_target_pairs={{0,16},{16,0},{32,48},{48,32},{64,80},{80,64},{96,112},{112,96},{1... | collective-permute-start | bytes 663560 | tf_op jit(solution)/shard_map/ppermute | solution.py:542
  27.8 1.9 %collective-permute-start.3 = (f32[27,8,256]{2,1,0:T(8,128)S(1)}, f32[27,8,256]{2,1,0:T(8,128)S(1)}, u32[]{:S(2)}, u32[]{:S(2)}) collective-permute-start(f32[27,8,256]{2,1,0:T(8,128)S(1)} %get-tuple-element.67), channel_id=1, source_target_pairs={{16,32},{32,16},{48,64},{64,48},{80,96},{96,80},{112,128},{128,112... | collective-permute-start | bytes 663560 | tf_op jit(solution)/shard_map/ppermute | solution.py:542
  29.7 0.9 %shard_map.52 = (f32[8,24,384]{2,1,0:T(8,128)S(1)}, f32[8,24,384]{2,1,0:T(8,128)S(1)}, f32[8,24,384]{2,1,0:T(8,128)S(1)}, f32[8,24,384]{2,1,0:T(8,128)S(1)}, f32...) custom-call(f32[8,16,256]{2,1,0:T(8,128)S(1)} %get-tuple-element.35., ...), custom_call_target="tpu_custom_call" | custom-call | flops 4194304 | bytes 4194304 | tf_op jit(solution)/shard_map/pallas_call | solution.py:572
  30.5 0.0 collective-permute-done.2.msg_ref
  30.6 0.9 %shard_map.53 = (f32[2,16,256]{2,1,0:T(8,128)S(1)}, f32[3,16,256]{2,1,0:T(8,128)S(1)}, f32[5,16,384]{2,1,0:T(8,128)S(1)}, f32[5,16,384]{2,1,0:T(8,128)S(1)}, f32...) custom-call(f32[8,16,256]{2,1,0:T(8,128)S(1)} %get-tuple-element.35.u_ref, ...), custom_call_target="tpu_custom_call" | custom-call | flops 4194304 | bytes 4194304 | tf_op jit(solution)/shard_map/pallas_call | solution.py:576
  31.5 3.5 %collective-permute-done.3.msg_ref = f32[27,8,256]{2,1,0:T(8,128)S(1)} collective-permute-done((f32[27,8,256]{2,1,0:T(8,128)S(1)}, f32[27,8,256]{2,1,0:T(8,128)S(1)}, u32[]{:S(2)}, u32[]{:S(2)}) %collective-permute-start.3) | collective-permute-done | bytes 221216 | tf_op jit(solution)/shard_map/ppermute | solution.py:542
  35.0 1.7 %shard_map.54 = (f32[8,16,256]{2,1,0:T(8,128)}, f32[8,16,256]{2,1,0:T(8,128)}) custom-call(f32[8,16,256]{2,1,0:T(8,128)S(1)} %get-tuple-element.35.u_ref, f32[2,32,384]{2,1,0:T(8,128)S(1)} %get-tuple-element.41.uo_ref, f32[2,32,384]{2,1,0:T(8,128)S(1)} %get-tuple-element.42.ko_ref, f32[8,24,384]{2,1,0:T(8,128)S(1)} %get-tuple-element.43.k_ref, ...), custom_call_target="tpu_custom_call" | custom-call | flops 4194304 | bytes 4194304 | tf_op jit(solution)/shard_map/pallas_call | solution.py:582
Async XLA Ops:
  2.5 18.3 %all-to-all-start = ((f32[16,16,256]{2,1,0:T(8,128)}), f32[16,16,256]{2,1,0:T(8,128)S(1)}, u32[]{:S(2)}, u32[]{:S(2)}) async-start(f32[16,16,256]{2,1,0:T(8,128)} %get-tuple-element.40), calls=%async_computation | async-start | bytes 524288 | tf_op jit(solution)/shard_map/all_to_all | solution.py:555
  10.1 7.1 %collective-permute-start = (f32[24,8,256]{2,1,0:T(8,128)S(1)}, f32[24,8,256]{2,1,0:T(8,128)S(1)}, u32[]{:S(2)}, u32[]{:S(2)}) collective-permute-start(f32[24,8,256]{2,1,0:T(8,128)S(1)} %get-tuple-element.38), channel_id=1, source_target_pairs={{0,1},{1,2},{2,3},{4,5},{5,6},{6,7},{8,9},{9,10},{10,11},{12,13},{... | collective-permute-start | bytes 589832 | tf_op jit(solution)/shard_map/ppermute | solution.py:534
  13.4 7.4 %collective-permute-start.1 = (f32[24,8,256]{2,1,0:T(8,128)S(1)}, f32[24,8,256]{2,1,0:T(8,128)S(1)}, u32[]{:S(2)}, u32[]{:S(2)}) collective-permute-start(f32[24,8,256]{2,1,0:T(8,128)S(1)} %get-tuple-element.39), channel_id=1, source_target_pairs={{1,0},{2,1},{3,2},{5,4},{6,5},{7,6},{9,8},{10,9},{11,10},{13,12},{... | collective-permute-start | bytes 589832 | tf_op jit(solution)/shard_map/ppermute | solution.py:534
  22.5 8.1 %collective-permute-start.2 = (f32[27,8,256]{2,1,0:T(8,128)S(1)}, f32[27,8,256]{2,1,0:T(8,128)S(1)}, u32[]{:S(2)}, u32[]{:S(2)}) collective-permute-start(f32[27,8,256]{2,1,0:T(8,128)S(1)} %get-tuple-element.59), channel_id=1, source_target_pairs={{0,16},{16,0},{32,48},{48,32},{64,80},{80,64},{96,112},{112,96},{1... | collective-permute-start | bytes 663560 | tf_op jit(solution)/shard_map/ppermute | solution.py:542
  27.8 7.3 %collective-permute-start.3 = (f32[27,8,256]{2,1,0:T(8,128)S(1)}, f32[27,8,256]{2,1,0:T(8,128)S(1)}, u32[]{:S(2)}, u32[]{:S(2)}) collective-permute-start(f32[27,8,256]{2,1,0:T(8,128)S(1)} %get-tuple-element.67), channel_id=1, source_target_pairs={{16,32},{32,16},{48,64},{64,48},{80,96},{96,80},{112,128},{128,112... | collective-permute-start | bytes 663560 | tf_op jit(solution)/shard_map/ppermute | solution.py:542

commit v4 on v3

--- a/solution.py
+++ b/solution.py
@@ -80,14 +80,17 @@
         copy.wait()
 
 
+def lane_pairs(plane, even):
+    return plane + jnp.where(even, up(plane, 1), down(plane, 1))
+
+
 def restrict_plane(plane, scratch_ref, even, scale):
-    pairs = plane + jnp.where(even, up(plane, 1), down(plane, 1))
-    cols = []
+    rows, cols = plane.shape[0], []
     for t in range(ZE // 128):
-        scratch_ref[t] = pairs[:, t * 128 : (t + 1) * 128]
         tile = scratch_ref.at[t]
-        cols.append(tile[pl.ds(0, CE, stride=2), :] + tile[pl.ds(1, CE, stride=2), :])
-    return scale * jnp.concatenate(cols, axis=1)
+        tile[:rows] = plane[:, t * 128 : (t + 1) * 128]
+        cols.append(tile[pl.ds(0, rows // 2, stride=2), :] + tile[pl.ds(1, rows // 2, stride=2), :])
+    return scale * lane_pairs(jnp.concatenate(cols, axis=1), even)
 
 
 def place(core, p, count):
@@ -134,12 +137,12 @@
     return jnp.concatenate(rows, axis=0)
 
 
-def block_kernel(
-    u_ref, k_ref, f_ref, up_ref, down_ref, z_ref,
-    uo_ref, ko_ref, k_in_ref, r_in_ref, rc_ref, kc_ref, chip_ref, link_ref,
-    ue_ref, ke_ref, fe_ref, tmp_ref,
+def own_kernel(
+    u_ref, k_ref, f_ref, z_ref,
+    uo_ref, ko_ref, ro_ref, rc_ref, kc_ref, zu_ref, zk_ref, zf_ref,
+    tmp_ref,
 ):
-    gz, cy, core = lax.axis_index("gz"), lax.axis_index("coarse"), lax.rem(lax.axis_index("pencil"), 2)
+    gz, cy = lax.axis_index("gz"), lax.axis_index("coarse")
     lane = lanes((RE, 128))
     sides = []
     for from_z, inside in ((3, gz > 0), (1, gz < 3)):
@@ -150,47 +153,108 @@
             jnp.where(cy > 0, z_ref[z + lax.rem(cy + 3, 4), :H], 0.0),
         ]
         sides.append(jnp.where(inside, jnp.concatenate(rows, axis=0), 0.0))
-    for i, (own, ext) in enumerate(((u_ref, ue_ref), (k_ref, ke_ref), (f_ref, fe_ref))):
-        scale = (lambda v: 0.5 * v) if i == 1 else (lambda v: v)
-        for p in range(NX):
-            g = i * NX + p
-            t, q = divmod(g, 16)
-            before, after = (side[:, t * 128 : t * 128 + 128] for side in sides)
-            if (120 - H * q) % 128:
-                before = pltpu.roll(before, (120 - H * q) % 128, 1)
-            if q:
-                after = pltpu.roll(after, 128 - H * q, 1)
-            ext[p, :NY, :NZ] = scale(own[p])
-            ext[p, NY : NY + H, :NZ] = scale(down_ref[g])
-            ext[p, NY + H :, :NZ] = scale(up_ref[g])
-            ext[p, :, NZ:] = scale(jnp.where(lane < H, after, jnp.where(lane >= 120, before, 0.0)))
-    even = lanes((RE, ZE)) % 2 == 0
-    flux_x = None
-    r_pair = k_pair = None
+
+    def extended(i, p, own, halo):
+        t, q = divmod(i * NX + p, 16)
+        before, after = (side[:, t * 128 : t * 128 + 128] for side in sides)
+        if (120 - H * q) % 128:
+            before = pltpu.roll(before, (120 - H * q) % 128, 1)
+        if q:
+            after = pltpu.roll(after, 128 - H * q, 1)
+        beyond = jnp.where(lane < H, after, jnp.where(lane >= 120, before, 0.0))
+        cells = own[p]
+        if i == 1:
+            beyond, cells = 0.5 * beyond, 0.5 * cells
+        halo[p] = beyond[NY:]
+        return jnp.concatenate([cells, beyond[:NY]], axis=1)
+
+    even = lanes((CY, ZE)) % 2 == 0
+    inner = lax.broadcasted_iota(jnp.int32, (NY, ZE), 0) < NY - 1
+    flux_x = r_pair = k_pair = None
+    u, k = extended(0, 0, u_ref, zu_ref), extended(1, 0, k_ref, zk_ref)
     for p in range(NX):
-        k, u = ke_ref[p], ue_ref[p]
+        uo_ref[p], ko_ref[p] = u, k
         flux = (k + up(k, 1)) * (u - up(u, 1))
         out = flux - down(flux, 1)
-        flux = (k + up(k, 0)) * (u - up(u, 0))
+        flux = jnp.where(inner, (k + up(k, 0)) * (u - up(u, 0)), 0.0)
         out = out + (flux - down(flux, 0))
         if flux_x is not None:
             out = out - flux_x
+        r, k_now = extended(2, p, f_ref, zf_ref), k
         if p < NX - 1:
-            flux_x = (k + ke_ref[p + 1]) * (u - ue_ref[p + 1])
+            un, kn = extended(0, p + 1, u_ref, zu_ref), extended(1, p + 1, k_ref, zk_ref)
+            flux_x = (k + kn) * (u - un)
             out = out + flux_x
-        r = fe_ref[p] - out
+            u, k = un, kn
+        r = r - out
+        ro_ref[p] = r
+        if p % 2 == 0:
+            r_pair, k_pair = r, k_now
+        else:
+            rc_ref[p // 2] = restrict_plane(r_pair + r, tmp_ref.at[p - 1], even, 0.125)
+            kc_ref[p // 2] = restrict_plane(k_pair + k_now, tmp_ref.at[p], even, 0.03125)
+
+
+def edge_kernel(
+    u_ref, k_ref, r_ref, rcl_ref, kcl_ref, zu_ref, zk_ref, zf_ref, up_ref, down_ref,
+    uo_ref, ko_ref, k_in_ref, r_in_ref, rc_ref, kc_ref, chip_ref, link_ref,
+    tmp_ref,
+):
+    core = lax.rem(lax.axis_index("pencil"), 2)
+    row = lax.broadcasted_iota(jnp.int32, (H, ZE), 0)
+    even = lanes((CY, ZE)) % 2 == 0
+
+    def halo(i, p, beyond):
+        g = i * NX + p
+        scale = (lambda v: 0.5 * v) if i == 1 else (lambda v: v)
+        cells = jnp.concatenate([scale(down_ref[g]), scale(up_ref[g])], axis=0)
+        return jnp.concatenate([cells, beyond[p]], axis=1)
+
+    flux_x = r_pair = k_pair = d_pair = None
+    u, k = halo(0, 0, zu_ref), halo(1, 0, zk_ref)
+    for p in range(NX):
+        own_u, own_k, own_r = u_ref[p], k_ref[p], r_ref[p]
+        flux = (k + up(k, 1)) * (u - up(u, 1))
+        out = flux - down(flux, 1)
+        kl, ul, kv, uv = k[:H], u[:H], k[H:], u[H:]
+        low = (down(own_k[H:], 0) + kl) * (down(own_u[H:], 0) - ul)
+        high = (kv + up(own_k[:H], 0)) * (uv - up(own_u[:H], 0))
+        flux = (kl + up(kl, 0)) * (ul - up(ul, 0))
+        below = flux - jnp.where(row == 0, low, down(flux, 0))
+        flux = jnp.where(row == H - 1, high, (kv + up(kv, 0)) * (uv - up(uv, 0)))
+        out = out + jnp.concatenate([below, flux - down(flux, 0)], axis=0)
+        first = jnp.where(row == 0, down(high, 0), 0.0)
+        last = jnp.where(row == H - 1, up(low, 0), 0.0)
+        if flux_x is not None:
+            out = out - flux_x
+        r, k_now, u_now = halo(2, p, zf_ref), k, u
+        if p < NX - 1:
+            un, kn = halo(0, p + 1, zu_ref), halo(1, p + 1, zk_ref)
+            flux_x = (k + kn) * (u - un)
+            out = out + flux_x
+            u, k = un, kn
+        r = r - out
         q = place(core, p, NX)
-        r_in_ref[q] = inner_rows(r)
-        k_in_ref[q] = inner_rows(k)
+        near = row < H // 2
+        r_in_ref[q] = jnp.concatenate(
+            [own_r[:H] + first, own_r[H:] - last, jnp.where(near, r[:H], r[H:])], axis=0
+        )
+        k_in_ref[q] = jnp.concatenate([own_k, jnp.where(near, k_now[:H], k_now[H:])], axis=0)
+        if p in (0, NX - 1):
+            end = place(core, p // (NX - 1), 2)
+            uo_ref[end] = jnp.concatenate([own_u, u_now], axis=0)
+            ko_ref[end] = jnp.concatenate([own_k, k_now], axis=0)
         if p % 2 == 0:
-            r_pair, k_pair = r, k
+            r_pair, k_pair, d_pair = r, k_now, first - last
         else:
             c = place(core, p // 2, CX)
-            rc_ref[c] = restrict_plane(r_pair + r, tmp_ref.at[p - 1], even, 0.125)
-            kc_ref[c] = restrict_plane(k_pair + k, tmp_ref.at[p], even, 0.03125)
-    for i in range(2):
-        end = place(core, i * (NX - 1), NX)
-        uo_ref[i], ko_ref[i] = ue_ref[end], ke_ref[end]
+            rc_ref[c] = jnp.concatenate([
+                rcl_ref[p // 2] + 0.125 * lane_pairs(d_pair + (first - last), even),
+                restrict_plane(r_pair + r, tmp_ref.at[p - 1], even, 0.125),
+            ], axis=0)
+            kc_ref[c] = jnp.concatenate(
+                [kcl_ref[p // 2], restrict_plane(k_pair + k_now, tmp_ref.at[p], even, 0.03125)], axis=0
+            )
     even_c = lanes((CE, ZE)) % 2 == 0
     for i, ref in enumerate((link_ref, chip_ref)):
         at, step, c = i * (NX - 1), 1 - 2 * i, i * (CX - 1)
@@ -232,12 +296,12 @@
 
 
 def open_message(msg, u_end, k_end, r_end, rc_end, tmp_ref):
-    even, even_c = lanes((RE, ZE)) % 2 == 0, lanes((CE, ZE)) % 2 == 0
+    even_c = lanes((CE, ZE)) % 2 == 0
     none = jnp.zeros((RF - NY, ZE), f32)
     un, kn = received_rows(msg, X_U, 4), received_rows(msg, X_K, 4)
     flux = (k_end + kn) * (u_end - un)
     inner = inner_rows(flux)
-    coarse = restrict_plane(flux, tmp_ref, even, 0.125)
+    coarse = restrict_plane(flux, tmp_ref, even_c, 0.125)
     ks = [inner_rows(kn), received_rows(msg, X_K2, 3)]
     ks.append(jnp.concatenate([received_rows(msg, X_K3, 2), none], axis=0))
     rs = [received_rows(msg, X_R1, 3) + inner]
@@ -561,14 +625,19 @@
         return (n, CE, ZE)
 
     message = (X_GROUPS + 2, 8, NZ)
+    edges = (ZE // 128, RE, 128)
+    rows = [(NX, NY, ZE)] * 3 + [(CX, CY, ZE)] * 2
+    tiles = [(NX, 2 * H, 128)] * 3
+    parts = call(
+        own_kernel, rows + tiles, "v" * 4, [(NX, ZE // 128, NY, 128)], 3 << 20, 1 << 22,
+    )(u, k, f, ends)
     uo, ko, k_in, r_in, rc, kc, chip, link = call(
-        block_kernel,
+        edge_kernel,
         [(2, RE, ZE), (2, RE, ZE), fine(NX), fine(NX), coarse(CX), coarse(CX), message, message],
-        "vvvvvv", [(NX, RE, ZE)] * 3 + [(NX, ZE // 128, RE, 128)], 3 << 20, 1 << 22,
-    )(u, k, f, upward, downward, ends)
+        "v" * 10, [(NX, ZE // 128, NY, 128)], 3 << 20, 1 << 22,
+    )(*parts, upward, downward)
     chip = swapped(chip, "pencil", 0)
     link = swapped(link, "pencil", 1)
-    edges = (ZE // 128, RE, 128)
     *fine_own, sums, smooth, cy, cz, cinv, e0 = call(
         mid_kernel, [fine(NX)] * 6 + [own, own] + [coarse(CX)] * 4, "v" * 5, [],
         4 << 20, 1 << 22,

time: 37 us -> 36 us (0.973)
  waiting for transfers between devices: 9.65 us -> 8.69 us
    ppermute x2, waiting for transfers between devices: 6.12 us -> 2.34 us  [shifted(): lax.ppermute(cells, axis, [(i, i + by) for i in range(count) if 0 <= i +...]
    all_to_all x1, waiting for transfers between devices: 0.01 us -> 2.74 us  [on_device(): ends = lax.all_to_all(ends, ('gz', 'coarse'), 0, 0)]
    pallas_call x1 -> x2, Pallas kernels: 1.64 us -> 1.7 us  [the longest x1 1.03 us: on_device(): call(own_kernel, rows + tiles, 'v' * 4, [(NX, ZE // 128, NY, 128)], 3 <<...]
  transfers between devices with their start and end apart: 5 -> 5, of which waited for: 3 -> 3; matrix products, arithmetic and copies ran while one was open for 0% -> 0% of each run, Pallas kernels for 5% -> 8%
where the time goes in v4:
time: 36 us; the launch traced here: 35.7 us
  starting transfers between devices  19.3 us (54%)
  waiting for transfers between devices  8.69 us (24%)
  Pallas kernels  6.89 us (19%)
  between operations  0.72 us (2%)
    all_to_all x1, starting transfers between devices, on_device(): ends = lax.all_to_all(ends, ('gz', 'coarse'), 0, 0)  7.58 us
    ppermute x2, starting transfers between devices, swapped(): return lax.ppermute(cells, axis, pairs)  7.2 us
    ppermute x2, starting transfers between devices, shifted(): lax.ppermute(cells, axis, [(i, i + by) for i in range(count) if 0 <= i +...  4.56 us
    ppermute x2, waiting for transfers between devices, swapped(): return lax.ppermute(cells, axis, pairs)  3.61 us
    all_to_all x1, waiting for transfers between devices, on_device(): ends = lax.all_to_all(ends, ('gz', 'coarse'), 0, 0)  2.74 us
    ppermute x2, waiting for transfers between devices, shifted(): lax.ppermute(cells, axis, [(i, i + by) for i in range(count) if 0 <= i +...  2.34 us
    pallas_call x1, Pallas kernels, on_device(): call(pack_kernel, [own, own, own, (GROUPS, H, NZ), (GROUPS, H, NZ), [16,...  1.89 us
    pallas_call x1, Pallas kernels, on_device(): call(final_kernel, [list(own), list(own)], 'v' * 27, [fine(3), fine(5)] +...  1.61 us
  transfers between devices with their start and end apart: 5, of which 3 were waited for; matrix products, arithmetic and copies ran while one was open for 0% of the time, Pallas kernels for 8%

profile of v4, /device:TPU:1, one launch (start us, length us, event | category | flops | bytes accessed | tf_op | source)
XLA Modules:
  0.0 35.7 jit_solution(17138712413925586845)
XLA Ops:
  0.6 1.9 %shard_map.50 = (f32[8,16,256]{2,1,0:T(8,128)S(1)}, f32[8,16,256]{2,1,0:T(8,128)S(1)}, f32[8,16,256]{2,1,0:T(8,128)S(1)}, f32[24,8,256]{2,1,0:T(8,128)S(1)}, f32...) custom-call(f32[8,16,256]{2,1,0:T(8,128)} %u_hbm.1, f32[8,16,256]{2,1,0:T(8,128)} %k_hbm.1, f32[8,16,256]{2,1,0:T(8,128)} %f_hbm.1), custom_call_target="tpu_custom_call" | custom-call | flops 262144 | bytes 1048576 | tf_op jit(solution)/shard_map/pallas_call | solution.py:612
  2.5 7.6 %all-to-all-start = ((f32[16,16,256]{2,1,0:T(8,128)}), f32[16,16,256]{2,1,0:T(8,128)S(1)}, u32[]{:S(2)}, u32[]{:S(2)}) async-start(f32[16,16,256]{2,1,0:T(8,128)} %get-tuple-element.46), calls=%async_computation | async-start | bytes 524288 | tf_op jit(solution)/shard_map/all_to_all | solution.py:619
  10.1 3.3 %collective-permute-start = (f32[24,8,256]{2,1,0:T(8,128)S(1)}, f32[24,8,256]{2,1,0:T(8,128)S(1)}, u32[]{:S(2)}, u32[]{:S(2)}) collective-permute-start(f32[24,8,256]{2,1,0:T(8,128)S(1)} %get-tuple-element.55), channel_id=1, source_target_pairs={{0,1},{1,2},{2,3},{4,5},{5,6},{6,7},{8,9},{9,10},{10,11},{12,13},{... | collective-permute-start | bytes 589832 | tf_op jit(solution)/shard_map/ppermute | solution.py:598
  13.4 1.3 %collective-permute-start.1 = (f32[24,8,256]{2,1,0:T(8,128)S(1)}, f32[24,8,256]{2,1,0:T(8,128)S(1)}, u32[]{:S(2)}, u32[]{:S(2)}) collective-permute-start(f32[24,8,256]{2,1,0:T(8,128)S(1)} %get-tuple-element.56), channel_id=1, source_target_pairs={{1,0},{2,1},{3,2},{5,4},{6,5},{7,6},{9,8},{10,9},{11,10},{13,12},{... | collective-permute-start | bytes 589832 | tf_op jit(solution)/shard_map/ppermute | solution.py:598
  14.7 2.7 %all-to-all-done.z_ref = f32[16,16,256]{2,1,0:T(8,128)S(1)} async-done(((f32[16,16,256]{2,1,0:T(8,128)}), f32[16,16,256]{2,1,0:T(8,128)S(1)}, u32[]{:S(2)}, u32[]{:S(2)}) %all-to-all-start) | async-done | bytes 262176 | tf_op jit(solution)/shard_map/all_to_all | solution.py:619
  17.4 1.0 %shard_map.51 = (f32[8,16,384]{2,1,0:T(8,128)S(1)}, f32[8,16,384]{2,1,0:T(8,128)S(1)}, f32[8,16,384]{2,1,0:T(8,128)S(1)}, f32[4,8,384]{2,1,0:T(8,128)S(1)}, f32[...) custom-call(f32[8,16,256]{2,1,0:T(8,128)S(1)} %get-tuple-element.43.u_r, ...), custom_call_target="tpu_custom_call" | custom-call | flops 4194304 | bytes 3145728 | tf_op jit(solution)/shard_map/pallas_call | solution.py:631
  18.5 0.0 collective-permute-done.up_ref
  18.5 2.3 %collective-permute-done.1.down_ref = f32[24,8,256]{2,1,0:T(8,128)S(1)} collective-permute-done((f32[24,8,256]{2,1,0:T(8,128)S(1)}, f32[24,8,256]{2,1,0:T(8,128)S(1)}, u32[]{:S(2)}, u32[]{:S(2)}) %collective-permute-start.1) | collective-permute-done | bytes 196640 | tf_op jit(solution)/shard_map/ppermute | solution.py:598
  20.8 0.7 %shard_map.52 = (f32[2,32,384]{2,1,0:T(8,128)S(1)}, f32[2,32,384]{2,1,0:T(8,128)S(1)}, f32[8,24,384]{2,1,0:T(8,128)S(1)}, f32[8,24,384]{2,1,0:T(8,128)S(1)}, f32...) custom-call(f32[8,16,384]{2,1,0:T(8,128)S(1)} %get-tuple-element.47.u, ...), custom_call_target="tpu_custom_call" | custom-call | flops 4194304 | bytes 3145728 | tf_op jit(solution)/shard_map/pallas_call | solution.py:634
  21.5 5.3 %collective-permute-start.2 = (f32[27,8,256]{2,1,0:T(8,128)S(1)}, f32[27,8,256]{2,1,0:T(8,128)S(1)}, u32[]{:S(2)}, u32[]{:S(2)}) collective-permute-start(f32[27,8,256]{2,1,0:T(8,128)S(1)} %get-tuple-element.75), channel_id=1, source_target_pairs={{0,16},{16,0},{32,48},{48,32},{64,80},{80,64},{96,112},{112,96},{1... | collective-permute-start | bytes 663560 | tf_op jit(solution)/shard_map/ppermute | solution.py:606
  26.8 1.9 %collective-permute-start.3 = (f32[27,8,256]{2,1,0:T(8,128)S(1)}, f32[27,8,256]{2,1,0:T(8,128)S(1)}, u32[]{:S(2)}, u32[]{:S(2)}) collective-permute-start(f32[27,8,256]{2,1,0:T(8,128)S(1)} %get-tuple-element.83), channel_id=1, source_target_pairs={{16,32},{32,16},{48,64},{64,48},{80,96},{96,80},{112,128},{128,112... | collective-permute-start | bytes 663560 | tf_op jit(solution)/shard_map/ppermute | solution.py:606
  28.7 0.9 %shard_map.53 = (f32[8,24,384]{2,1,0:T(8,128)S(1)}, f32[8,24,384]{2,1,0:T(8,128)S(1)}, f32[8,24,384]{2,1,0:T(8,128)S(1)}, f32[8,24,384]{2,1,0:T(8,128)S(1)}, f32...) custom-call(f32[8,16,256]{2,1,0:T(8,128)S(1)} %get-tuple-element.43., ...), custom_call_target="tpu_custom_call" | custom-call | flops 4194304 | bytes 4194304 | tf_op jit(solution)/shard_map/pallas_call | solution.py:641
  29.6 0.0 collective-permute-done.2.msg_ref
  29.6 0.8 %shard_map.54 = (f32[2,16,256]{2,1,0:T(8,128)S(1)}, f32[3,16,256]{2,1,0:T(8,128)S(1)}, f32[5,16,384]{2,1,0:T(8,128)S(1)}, f32[5,16,384]{2,1,0:T(8,128)S(1)}, f32...) custom-call(f32[8,16,256]{2,1,0:T(8,128)S(1)} %get-tuple-element.43.u_ref, ...), custom_call_target="tpu_custom_call" | custom-call | flops 4194304 | bytes 4194304 | tf_op jit(solution)/shard_map/pallas_call | solution.py:645
  30.4 3.6 %collective-permute-done.3.msg_ref = f32[27,8,256]{2,1,0:T(8,128)S(1)} collective-permute-done((f32[27,8,256]{2,1,0:T(8,128)S(1)}, f32[27,8,256]{2,1,0:T(8,128)S(1)}, u32[]{:S(2)}, u32[]{:S(2)}) %collective-permute-start.3) | collective-permute-done | bytes 221216 | tf_op jit(solution)/shard_map/ppermute | solution.py:606
  34.0 1.6 %shard_map.55 = (f32[8,16,256]{2,1,0:T(8,128)}, f32[8,16,256]{2,1,0:T(8,128)}) custom-call(f32[8,16,256]{2,1,0:T(8,128)S(1)} %get-tuple-element.43.u_ref, f32[2,32,384]{2,1,0:T(8,128)S(1)} %get-tuple-element.57.uo_ref, f32[2,32,384]{2,1,0:T(8,128)S(1)} %get-tuple-element.58.ko_ref, f32[8,24,384]{2,1,0:T(8,128)S(1)} %get-tuple-element.59.k_ref, ...), custom_call_target="tpu_custom_call" | custom-call | flops 4194304 | bytes 4194304 | tf_op jit(solution)/shard_map/pallas_call | solution.py:651
Async XLA Ops:
  2.5 14.9 %all-to-all-start = ((f32[16,16,256]{2,1,0:T(8,128)}), f32[16,16,256]{2,1,0:T(8,128)S(1)}, u32[]{:S(2)}, u32[]{:S(2)}) async-start(f32[16,16,256]{2,1,0:T(8,128)} %get-tuple-element.46), calls=%async_computation | async-start | bytes 524288 | tf_op jit(solution)/shard_map/all_to_all | solution.py:619
  10.1 8.4 %collective-permute-start = (f32[24,8,256]{2,1,0:T(8,128)S(1)}, f32[24,8,256]{2,1,0:T(8,128)S(1)}, u32[]{:S(2)}, u32[]{:S(2)}) collective-permute-start(f32[24,8,256]{2,1,0:T(8,128)S(1)} %get-tuple-element.55), channel_id=1, source_target_pairs={{0,1},{1,2},{2,3},{4,5},{5,6},{6,7},{8,9},{9,10},{10,11},{12,13},{... | collective-permute-start | bytes 589832 | tf_op jit(solution)/shard_map/ppermute | solution.py:598
  13.4 7.4 %collective-permute-start.1 = (f32[24,8,256]{2,1,0:T(8,128)S(1)}, f32[24,8,256]{2,1,0:T(8,128)S(1)}, u32[]{:S(2)}, u32[]{:S(2)}) collective-permute-start(f32[24,8,256]{2,1,0:T(8,128)S(1)} %get-tuple-element.56), channel_id=1, source_target_pairs={{1,0},{2,1},{3,2},{5,4},{6,5},{7,6},{9,8},{10,9},{11,10},{13,12},{... | collective-permute-start | bytes 589832 | tf_op jit(solution)/shard_map/ppermute | solution.py:598
  21.5 8.1 %collective-permute-start.2 = (f32[27,8,256]{2,1,0:T(8,128)S(1)}, f32[27,8,256]{2,1,0:T(8,128)S(1)}, u32[]{:S(2)}, u32[]{:S(2)}) collective-permute-start(f32[27,8,256]{2,1,0:T(8,128)S(1)} %get-tuple-element.75), channel_id=1, source_target_pairs={{0,16},{16,0},{32,48},{48,32},{64,80},{80,64},{96,112},{112,96},{1... | collective-permute-start | bytes 663560 | tf_op jit(solution)/shard_map/ppermute | solution.py:606
  26.8 7.3 %collective-permute-start.3 = (f32[27,8,256]{2,1,0:T(8,128)S(1)}, f32[27,8,256]{2,1,0:T(8,128)S(1)}, u32[]{:S(2)}, u32[]{:S(2)}) collective-permute-start(f32[27,8,256]{2,1,0:T(8,128)S(1)} %get-tuple-element.83), channel_id=1, source_target_pairs={{16,32},{32,16},{48,64},{64,48},{80,96},{96,80},{112,128},{128,112... | collective-permute-start | bytes 663560 | tf_op jit(solution)/shard_map/ppermute | solution.py:606

commit v5 on v4

--- a/solution.py
+++ b/solution.py
@@ -37,10 +37,11 @@
 
 def pack_kernel(
     u_hbm, k_hbm, f_hbm,
-    u_ref, k_ref, f_ref, up_ref, down_ref, z_hbm,
+    u_ref, k_ref, f_ref, one_ref, two_ref, z_hbm,
     end_ref, own_sem, end_sem,
 ):
     gz, cy = lax.axis_index("gz"), lax.axis_index("coarse")
+    core = lax.rem(lax.axis_index("pencil"), 2)
     fields = (u_ref, k_ref, f_ref)
     copies = []
     for i, (far, near) in enumerate(zip((u_hbm, k_hbm, f_hbm), fields)):
@@ -72,10 +73,11 @@
         )):
             sends.append(pltpu.make_async_copy(src, dst, end_sem.at[3 * side + j]))
             sends[-1].start()
-    for i, field in enumerate(fields):
-        for p in range(NX):
-            up_ref[i * NX + p] = field[p, NY - H :, :]
-            down_ref[i * NX + p] = field[p, :H, :]
+    for ref, start in ((one_ref, (1 - core) * (NY - H)), (two_ref, core * (NY - H))):
+        rows = pl.ds(pl.multiple_of(start, 8), H)
+        for i, field in enumerate(fields):
+            for p in range(NX):
+                ref[i * NX + p] = field[p, rows, :]
     for copy in sends:
         copy.wait()
 
@@ -196,7 +198,7 @@
 
 
 def edge_kernel(
-    u_ref, k_ref, r_ref, rcl_ref, kcl_ref, zu_ref, zk_ref, zf_ref, up_ref, down_ref,
+    u_ref, k_ref, r_ref, rcl_ref, kcl_ref, zu_ref, zk_ref, zf_ref, one_ref, two_ref,
     uo_ref, ko_ref, k_in_ref, r_in_ref, rc_ref, kc_ref, chip_ref, link_ref,
     tmp_ref,
 ):
@@ -207,7 +209,9 @@
     def halo(i, p, beyond):
         g = i * NX + p
         scale = (lambda v: 0.5 * v) if i == 1 else (lambda v: v)
-        cells = jnp.concatenate([scale(down_ref[g]), scale(up_ref[g])], axis=0)
+        one, two = scale(one_ref[g]), scale(two_ref[g])
+        after, before = jnp.where(core == 1, one, two), jnp.where(core == 1, two, one)
+        cells = jnp.concatenate([after, before], axis=0)
         return jnp.concatenate([cells, beyond[p]], axis=1)
 
     flux_x = r_pair = k_pair = d_pair = None
@@ -593,9 +597,15 @@
     )
 
 
-def shifted(cells, axis, by):
-    count = lax.axis_size(axis)
-    return lax.ppermute(cells, axis, [(i, i + by) for i in range(count) if 0 <= i + by < count])
+def parted(cells, by):
+    count = lax.axis_size("coarse")
+    pairs = []
+    for p in range(lax.axis_size("pencil")):
+        step = by if p % 2 == 0 else -by
+        pairs += [
+            (p * count + i, p * count + i + step) for i in range(count) if 0 <= i + step < count
+        ]
+    return lax.ppermute(cells, ("pencil", "coarse"), pairs)
 
 
 def swapped(cells, axis, first):
@@ -609,13 +619,13 @@
 def on_device(right_side, conductivity, guess):
     own = (NX, NY, NZ)
     dma = pltpu.SemaphoreType.DMA
-    u, k, f, upward, downward, ends = call(
+    u, k, f, one, two, ends = call(
         pack_kernel,
         [own, own, own, (GROUPS, H, NZ), (GROUPS, H, NZ), [16, NY, 256]],
         "hhh", [(2, NY, 256), dma((6,)), dma((6,))], 1 << 20, 1 << 18,
     )(*(pltpu.with_memory_space_constraint(a, pltpu.HBM) for a in (guess, conductivity, right_side)))
-    upward = shifted(upward, "coarse", 1)
-    downward = shifted(downward, "coarse", -1)
+    one = parted(one, 1)
+    two = parted(two, -1)
     ends = lax.all_to_all(ends, ("gz", "coarse"), 0, 0)
 
     def fine(n):
@@ -635,7 +645,7 @@
         edge_kernel,
         [(2, RE, ZE), (2, RE, ZE), fine(NX), fine(NX), coarse(CX), coarse(CX), message, message],
         "v" * 10, [(NX, ZE // 128, NY, 128)], 3 << 20, 1 << 22,
-    )(*parts, upward, downward)
+    )(*parts, one, two)
     chip = swapped(chip, "pencil", 0)
     link = swapped(link, "pencil", 1)
     *fine_own, sums, smooth, cy, cz, cinv, e0 = call(

time: 36 us -> 35.9 us (level)
  starting transfers between devices: 19.3 us -> 20.7 us
  waiting for transfers between devices: 8.69 us -> 7.35 us
    ppermute x2, starting transfers between devices: 4.56 us -> 5.29 us  [parted(): return lax.ppermute(cells, ('pencil', 'coarse'), pairs)]
    all_to_all x1, waiting for transfers between devices: 2.74 us -> 2.06 us  [on_device(): ends = lax.all_to_all(ends, ('gz', 'coarse'), 0, 0)]
    ppermute x2, waiting for transfers between devices: 2.34 us -> 1.68 us  [parted(): return lax.ppermute(cells, ('pencil', 'coarse'), pairs)]
    ppermute x2, starting transfers between devices: 7.2 us -> 7.81 us  [swapped(): return lax.ppermute(cells, axis, pairs)]
where the time goes in v5:
time: 35.9 us; the launch traced here: 35.6 us
  starting transfers between devices  20.7 us (58%)
  waiting for transfers between devices  7.35 us (20%)
  Pallas kernels  6.82 us (19%)
  between operations  0.72 us (2%)
    ppermute x2, starting transfers between devices, swapped(): return lax.ppermute(cells, axis, pairs)  7.81 us
    all_to_all x1, starting transfers between devices, on_device(): ends = lax.all_to_all(ends, ('gz', 'coarse'), 0, 0)  7.58 us
    ppermute x2, starting transfers between devices, parted(): return lax.ppermute(cells, ('pencil', 'coarse'), pairs)  5.29 us
    ppermute x2, waiting for transfers between devices, swapped(): return lax.ppermute(cells, axis, pairs)  3.61 us
    all_to_all x1, waiting for transfers between devices, on_device(): ends = lax.all_to_all(ends, ('gz', 'coarse'), 0, 0)  2.06 us
    pallas_call x1, Pallas kernels, on_device(): call(pack_kernel, [own, own, own, (GROUPS, H, NZ), (GROUPS, H, NZ), [16,...  1.9 us
    ppermute x2, waiting for transfers between devices, parted(): return lax.ppermute(cells, ('pencil', 'coarse'), pairs)  1.68 us
    pallas_call x1, Pallas kernels, on_device(): call(final_kernel, [list(own), list(own)], 'v' * 27, [fine(3), fine(5)] +...  1.61 us
  transfers between devices with their start and end apart: 5, of which 3 were waited for; matrix products, arithmetic and copies ran while one was open for 0% of the time, Pallas kernels for 8%

profile of v5, /device:TPU:1, one launch (start us, length us, event | category | flops | bytes accessed | tf_op | source)
XLA Modules:
  0.0 35.6 jit_solution(3731657470678361873)
XLA Ops:
  0.6 1.9 %shard_map.50 = (f32[8,16,256]{2,1,0:T(8,128)S(1)}, f32[8,16,256]{2,1,0:T(8,128)S(1)}, f32[8,16,256]{2,1,0:T(8,128)S(1)}, f32[24,8,256]{2,1,0:T(8,128)S(1)}, f32...) custom-call(f32[8,16,256]{2,1,0:T(8,128)} %u_hbm.1, f32[8,16,256]{2,1,0:T(8,128)} %k_hbm.1, f32[8,16,256]{2,1,0:T(8,128)} %f_hbm.1), custom_call_target="tpu_custom_call" | custom-call | flops 262144 | bytes 1048576 | tf_op jit(solution)/shard_map/pallas_call | solution.py:622
  2.5 7.6 %all-to-all-start = ((f32[16,16,256]{2,1,0:T(8,128)}), f32[16,16,256]{2,1,0:T(8,128)S(1)}, u32[]{:S(2)}, u32[]{:S(2)}) async-start(f32[16,16,256]{2,1,0:T(8,128)} %get-tuple-element.46), calls=%async_computation | async-start | bytes 524288 | tf_op jit(solution)/shard_map/all_to_all | solution.py:629
  10.1 1.3 %collective-permute-start = (f32[24,8,256]{2,1,0:T(8,128)S(1)}, f32[24,8,256]{2,1,0:T(8,128)S(1)}, u32[]{:S(2)}, u32[]{:S(2)}) collective-permute-start(f32[24,8,256]{2,1,0:T(8,128)S(1)} %get-tuple-element.55), channel_id=1, source_target_pairs={{0,1},{1,2},{2,3},{17,16},{18,17},{19,18},{32,33},{33,34},{34,35},... | collective-permute-start | bytes 589832 | tf_op jit(solution)/shard_map/ppermute | solution.py:608
  11.4 4.0 %collective-permute-start.1 = (f32[24,8,256]{2,1,0:T(8,128)S(1)}, f32[24,8,256]{2,1,0:T(8,128)S(1)}, u32[]{:S(2)}, u32[]{:S(2)}) collective-permute-start(f32[24,8,256]{2,1,0:T(8,128)S(1)} %get-tuple-element.56), channel_id=1, source_target_pairs={{1,0},{2,1},{3,2},{16,17},{17,18},{18,19},{33,32},{34,33},{35,34},... | collective-permute-start | bytes 589832 | tf_op jit(solution)/shard_map/ppermute | solution.py:608
  15.4 2.1 %all-to-all-done.z_ref = f32[16,16,256]{2,1,0:T(8,128)S(1)} async-done(((f32[16,16,256]{2,1,0:T(8,128)}), f32[16,16,256]{2,1,0:T(8,128)S(1)}, u32[]{:S(2)}, u32[]{:S(2)}) %all-to-all-start) | async-done | bytes 262176 | tf_op jit(solution)/shard_map/all_to_all | solution.py:629
  17.5 1.0 %shard_map.51 = (f32[8,16,384]{2,1,0:T(8,128)S(1)}, f32[8,16,384]{2,1,0:T(8,128)S(1)}, f32[8,16,384]{2,1,0:T(8,128)S(1)}, f32[4,8,384]{2,1,0:T(8,128)S(1)}, f32[...) custom-call(f32[8,16,256]{2,1,0:T(8,128)S(1)} %get-tuple-element.43.u_r, ...), custom_call_target="tpu_custom_call" | custom-call | flops 4194304 | bytes 3145728 | tf_op jit(solution)/shard_map/pallas_call | solution.py:641
  18.5 0.0 collective-permute-done.one_ref
  18.5 1.7 %collective-permute-done.1.two_ref = f32[24,8,256]{2,1,0:T(8,128)S(1)} collective-permute-done((f32[24,8,256]{2,1,0:T(8,128)S(1)}, f32[24,8,256]{2,1,0:T(8,128)S(1)}, u32[]{:S(2)}, u32[]{:S(2)}) %collective-permute-start.1) | collective-permute-done | bytes 196640 | tf_op jit(solution)/shard_map/ppermute | solution.py:608
  20.2 0.6 %shard_map.52 = (f32[2,32,384]{2,1,0:T(8,128)S(1)}, f32[2,32,384]{2,1,0:T(8,128)S(1)}, f32[8,24,384]{2,1,0:T(8,128)S(1)}, f32[8,24,384]{2,1,0:T(8,128)S(1)}, f32...) custom-call(f32[8,16,384]{2,1,0:T(8,128)S(1)} %get-tuple-element.47.u, ...), custom_call_target="tpu_custom_call" | custom-call | flops 4194304 | bytes 3145728 | tf_op jit(solution)/shard_map/pallas_call | solution.py:644
  20.8 5.9 %collective-permute-start.2 = (f32[27,8,256]{2,1,0:T(8,128)S(1)}, f32[27,8,256]{2,1,0:T(8,128)S(1)}, u32[]{:S(2)}, u32[]{:S(2)}) collective-permute-start(f32[27,8,256]{2,1,0:T(8,128)S(1)} %get-tuple-element.75), channel_id=1, source_target_pairs={{0,16},{16,0},{32,48},{48,32},{64,80},{80,64},{96,112},{112,96},{1... | collective-permute-start | bytes 663560 | tf_op jit(solution)/shard_map/ppermute | solution.py:616
  26.7 1.9 %collective-permute-start.3 = (f32[27,8,256]{2,1,0:T(8,128)S(1)}, f32[27,8,256]{2,1,0:T(8,128)S(1)}, u32[]{:S(2)}, u32[]{:S(2)}) collective-permute-start(f32[27,8,256]{2,1,0:T(8,128)S(1)} %get-tuple-element.83), channel_id=1, source_target_pairs={{16,32},{32,16},{48,64},{64,48},{80,96},{96,80},{112,128},{128,112... | collective-permute-start | bytes 663560 | tf_op jit(solution)/shard_map/ppermute | solution.py:616
  28.6 0.9 %shard_map.53 = (f32[8,24,384]{2,1,0:T(8,128)S(1)}, f32[8,24,384]{2,1,0:T(8,128)S(1)}, f32[8,24,384]{2,1,0:T(8,128)S(1)}, f32[8,24,384]{2,1,0:T(8,128)S(1)}, f32...) custom-call(f32[8,16,256]{2,1,0:T(8,128)S(1)} %get-tuple-element.43., ...), custom_call_target="tpu_custom_call" | custom-call | flops 4194304 | bytes 4194304 | tf_op jit(solution)/shard_map/pallas_call | solution.py:651
  29.5 0.0 collective-permute-done.2.msg_ref
  29.5 0.8 %shard_map.54 = (f32[2,16,256]{2,1,0:T(8,128)S(1)}, f32[3,16,256]{2,1,0:T(8,128)S(1)}, f32[5,16,384]{2,1,0:T(8,128)S(1)}, f32[5,16,384]{2,1,0:T(8,128)S(1)}, f32...) custom-call(f32[8,16,256]{2,1,0:T(8,128)S(1)} %get-tuple-element.43.u_ref, ...), custom_call_target="tpu_custom_call" | custom-call | flops 4194304 | bytes 4194304 | tf_op jit(solution)/shard_map/pallas_call | solution.py:655
  30.4 3.6 %collective-permute-done.3.msg_ref = f32[27,8,256]{2,1,0:T(8,128)S(1)} collective-permute-done((f32[27,8,256]{2,1,0:T(8,128)S(1)}, f32[27,8,256]{2,1,0:T(8,128)S(1)}, u32[]{:S(2)}, u32[]{:S(2)}) %collective-permute-start.3) | collective-permute-done | bytes 221216 | tf_op jit(solution)/shard_map/ppermute | solution.py:616
  34.0 1.6 %shard_map.55 = (f32[8,16,256]{2,1,0:T(8,128)}, f32[8,16,256]{2,1,0:T(8,128)}) custom-call(f32[8,16,256]{2,1,0:T(8,128)S(1)} %get-tuple-element.43.u_ref, f32[2,32,384]{2,1,0:T(8,128)S(1)} %get-tuple-element.57.uo_ref, f32[2,32,384]{2,1,0:T(8,128)S(1)} %get-tuple-element.58.ko_ref, f32[8,24,384]{2,1,0:T(8,128)S(1)} %get-tuple-element.59.k_ref, ...), custom_call_target="tpu_custom_call" | custom-call | flops 4194304 | bytes 4194304 | tf_op jit(solution)/shard_map/pallas_call | solution.py:661
Async XLA Ops:
  2.5 15.0 %all-to-all-start = ((f32[16,16,256]{2,1,0:T(8,128)}), f32[16,16,256]{2,1,0:T(8,128)S(1)}, u32[]{:S(2)}, u32[]{:S(2)}) async-start(f32[16,16,256]{2,1,0:T(8,128)} %get-tuple-element.46), calls=%async_computation | async-start | bytes 524288 | tf_op jit(solution)/shard_map/all_to_all | solution.py:629
  10.1 8.4 %collective-permute-start = (f32[24,8,256]{2,1,0:T(8,128)S(1)}, f32[24,8,256]{2,1,0:T(8,128)S(1)}, u32[]{:S(2)}, u32[]{:S(2)}) collective-permute-start(f32[24,8,256]{2,1,0:T(8,128)S(1)} %get-tuple-element.55), channel_id=1, source_target_pairs={{0,1},{1,2},{2,3},{17,16},{18,17},{19,18},{32,33},{33,34},{34,35},... | collective-permute-start | bytes 589832 | tf_op jit(solution)/shard_map/ppermute | solution.py:608
  11.4 8.8 %collective-permute-start.1 = (f32[24,8,256]{2,1,0:T(8,128)S(1)}, f32[24,8,256]{2,1,0:T(8,128)S(1)}, u32[]{:S(2)}, u32[]{:S(2)}) collective-permute-start(f32[24,8,256]{2,1,0:T(8,128)S(1)} %get-tuple-element.56), channel_id=1, source_target_pairs={{1,0},{2,1},{3,2},{16,17},{17,18},{18,19},{33,32},{34,33},{35,34},... | collective-permute-start | bytes 589832 | tf_op jit(solution)/shard_map/ppermute | solution.py:608
  20.8 8.7 %collective-permute-start.2 = (f32[27,8,256]{2,1,0:T(8,128)S(1)}, f32[27,8,256]{2,1,0:T(8,128)S(1)}, u32[]{:S(2)}, u32[]{:S(2)}) collective-permute-start(f32[27,8,256]{2,1,0:T(8,128)S(1)} %get-tuple-element.75), channel_id=1, source_target_pairs={{0,16},{16,0},{32,48},{48,32},{64,80},{80,64},{96,112},{112,96},{1... | collective-permute-start | bytes 663560 | tf_op jit(solution)/shard_map/ppermute | solution.py:616
  26.7 7.3 %collective-permute-start.3 = (f32[27,8,256]{2,1,0:T(8,128)S(1)}, f32[27,8,256]{2,1,0:T(8,128)S(1)}, u32[]{:S(2)}, u32[]{:S(2)}) collective-permute-start(f32[27,8,256]{2,1,0:T(8,128)S(1)} %get-tuple-element.83), channel_id=1, source_target_pairs={{16,32},{32,16},{48,64},{64,48},{80,96},{96,80},{112,128},{128,112... | collective-permute-start | bytes 663560 | tf_op jit(solution)/shard_map/ppermute | solution.py:616

commit v6 on v5

--- a/solution.py
+++ b/solution.py
@@ -19,7 +19,7 @@
 ZE = NZ + 128
 CX, CY = NX // 2, NY // 2
 CE = RE // 2
-GROUPS = 3 * NX
+GROUPS = 3 * NX - 2
 f32 = jnp.float32
 
 
@@ -51,33 +51,40 @@
             copies[-1].start()
     for copy in copies:
         copy.wait()
-    group = lanes((NY, 128)) // H
+    group = lanes((H, 128)) // H
     sends = []
     for side, (first, start, to_z) in enumerate(((NZ - 128, H, 1), (0, 0, 3))):
-        for t in range(2):
-            tile = jnp.zeros((NY, 128), f32)
+        for tile in range(3):
+            packed = jnp.zeros((H, 128), f32)
             for q in range(16):
-                g = t * 16 + q
-                if g < GROUPS:
-                    cells = fields[g // NX][g % NX, :, first : first + 128]
-                    shift = (H * q + start) % 128
-                    moved = pltpu.roll(cells, shift, 1) if shift else cells
-                    tile = jnp.where(group == q, moved, tile)
-            end_ref[side, :, t * 128 : (t + 1) * 128] = tile
+                if tile == 1:
+                    field, rows = f_ref, (0, NY - H)[q // NX]
+                else:
+                    field, rows = fields[q // NX], (0, NY - H)[tile // 2]
+                cells = field[q % NX, rows : rows + H, first : first + 128]
+                shift = (H * q + start) % 128
+                moved = pltpu.roll(cells, shift, 1) if shift else cells
+                packed = jnp.where(group == q, moved, packed)
+            end_ref[side, tile] = packed
         z = lax.rem(gz + to_z, 4) * 4
         end = end_ref.at[side]
         for j, (src, dst) in enumerate((
             (end, z_hbm.at[z + cy]),
-            (end.at[pl.ds(NY - H, H)], z_hbm.at[z + lax.rem(cy + 1, 4), pl.ds(0, H)]),
-            (end.at[pl.ds(0, H)], z_hbm.at[z + lax.rem(cy + 3, 4), pl.ds(0, H)]),
+            (end.at[pl.ds(1, 2)], z_hbm.at[z + lax.rem(cy + 1, 4), pl.ds(1, 2)]),
+            (end.at[pl.ds(0, 2)], z_hbm.at[z + lax.rem(cy + 3, 4), pl.ds(0, 2)]),
         )):
             sends.append(pltpu.make_async_copy(src, dst, end_sem.at[3 * side + j]))
             sends[-1].start()
     for ref, start in ((one_ref, (1 - core) * (NY - H)), (two_ref, core * (NY - H))):
         rows = pl.ds(pl.multiple_of(start, 8), H)
         for i, field in enumerate(fields):
-            for p in range(NX):
+            for p in range(NX if i < 2 else 0):
                 ref[i * NX + p] = field[p, rows, :]
+        row = lax.broadcasted_iota(jnp.int32, (H, NZ), 0)
+        spare = (row + jnp.where(start > 0, 0, 2)) % H < 2
+        for p in range(NX - 2):
+            moved = pltpu.roll(f_ref[NX - 2 + p // 3, rows, :], 6 - 2 * (p % 3), 0)
+            ref[2 * NX + p] = jnp.where(spare, moved, f_ref[p, rows, :])
     for copy in sends:
         copy.wait()
 
@@ -149,16 +156,21 @@
     sides = []
     for from_z, inside in ((3, gz > 0), (1, gz < 3)):
         z = lax.rem(gz + from_z, 4) * 4
-        rows = [
-            z_ref[z + cy],
-            jnp.where(cy < 3, z_ref[z + lax.rem(cy + 1, 4), :H], 0.0),
-            jnp.where(cy > 0, z_ref[z + lax.rem(cy + 3, 4), :H], 0.0),
+        same, after, before = (z + lax.rem(cy + d, 4) for d in (0, 1, 3))
+        uk = [
+            z_ref[same, 0], z_ref[same, 2],
+            jnp.where(cy < 3, z_ref[after, 0], 0.0), jnp.where(cy > 0, z_ref[before, 2], 0.0),
         ]
-        sides.append(jnp.where(inside, jnp.concatenate(rows, axis=0), 0.0))
+        f = [
+            z_ref[same, 1], pltpu.roll(z_ref[same, 1], 64, 1),
+            jnp.where(cy < 3, z_ref[after, 1], 0.0),
+            jnp.where(cy > 0, pltpu.roll(z_ref[before, 1], 64, 1), 0.0),
+        ]
+        sides.append(tuple(jnp.where(inside, jnp.concatenate(v, axis=0), 0.0) for v in (uk, f)))
 
     def extended(i, p, own, halo):
         t, q = divmod(i * NX + p, 16)
-        before, after = (side[:, t * 128 : t * 128 + 128] for side in sides)
+        before, after = (side[t] for side in sides)
         if (120 - H * q) % 128:
             before = pltpu.roll(before, (120 - H * q) % 128, 1)
         if q:
@@ -206,13 +218,23 @@
     row = lax.broadcasted_iota(jnp.int32, (H, ZE), 0)
     even = lanes((CY, ZE)) % 2 == 0
 
+    pair = lax.broadcasted_iota(jnp.int32, (H, NZ), 0) // 2
+
+    def tiles(g):
+        one, two = one_ref[g], two_ref[g]
+        return jnp.where(core == 1, one, two), jnp.where(core == 1, two, one)
+
     def halo(i, p, beyond):
-        g = i * NX + p
-        scale = (lambda v: 0.5 * v) if i == 1 else (lambda v: v)
-        one, two = scale(one_ref[g]), scale(two_ref[g])
-        after, before = jnp.where(core == 1, one, two), jnp.where(core == 1, two, one)
+        if i < 2 or p < NX - 2:
+            after, before = tiles(i * NX + p)
+        else:
+            after = before = jnp.zeros((H, NZ), f32)
+            for j in range(3):
+                a, b = tiles(2 * NX + 3 * (p - NX + 2) + j)
+                after = jnp.where(pair == j, pltpu.roll(a, 2 + 2 * j, 0), after)
+                before = jnp.where(pair == j + 1, pltpu.roll(b, 2 + 2 * j, 0), before)
         cells = jnp.concatenate([after, before], axis=0)
-        return jnp.concatenate([cells, beyond[p]], axis=1)
+        return jnp.concatenate([0.5 * cells if i == 1 else cells, beyond[p]], axis=1)
 
     flux_x = r_pair = k_pair = d_pair = None
     u, k = halo(0, 0, zu_ref), halo(1, 0, zk_ref)
@@ -621,8 +643,8 @@
     dma = pltpu.SemaphoreType.DMA
     u, k, f, one, two, ends = call(
         pack_kernel,
-        [own, own, own, (GROUPS, H, NZ), (GROUPS, H, NZ), [16, NY, 256]],
-        "hhh", [(2, NY, 256), dma((6,)), dma((6,))], 1 << 20, 1 << 18,
+        [own, own, own, (GROUPS, H, NZ), (GROUPS, H, NZ), [16, 3, H, 128]],
+        "hhh", [(2, 3, H, 128), dma((6,)), dma((6,))], 1 << 20, 1 << 18,
     )(*(pltpu.with_memory_space_constraint(a, pltpu.HBM) for a in (guess, conductivity, right_side)))
     one = parted(one, 1)
     two = parted(two, -1)

time: 35.9 us -> 35.7 us (level)
  waiting for transfers between devices: 7.35 us -> 6.58 us
  starting transfers between devices: 20.7 us -> 21.2 us
    ppermute x2, starting transfers between devices: 7.81 us -> 8.37 us  [swapped(): return lax.ppermute(cells, axis, pairs)]
    all_to_all x1, waiting for transfers between devices: 2.06 us -> 1.62 us  [on_device(): ends = lax.all_to_all(ends, ('gz', 'coarse'), 0, 0)]
where the time goes in v6:
time: 35.7 us; the launch traced here: 35.4 us
  starting transfers between devices  21.2 us (59%)
  Pallas kernels  6.82 us (19%)
  waiting for transfers between devices  6.58 us (18%)
  between operations  0.72 us (2%)
    ppermute x2, starting transfers between devices, swapped(): return lax.ppermute(cells, axis, pairs)  8.37 us
    all_to_all x1, starting transfers between devices, on_device(): ends = lax.all_to_all(ends, ('gz', 'coarse'), 0, 0)  7.59 us
    ppermute x2, starting transfers between devices, parted(): return lax.ppermute(cells, ('pencil', 'coarse'), pairs)  5.29 us
    ppermute x2, waiting for transfers between devices, swapped(): return lax.ppermute(cells, axis, pairs)  3.61 us
    pallas_call x1, Pallas kernels, on_device(): call(pack_kernel, [own, own, own, (GROUPS, H, NZ), (GROUPS, H, NZ), [16,...  1.89 us
    all_to_all x1, waiting for transfers between devices, on_device(): ends = lax.all_to_all(ends, ('gz', 'coarse'), 0, 0)  1.62 us
    pallas_call x1, Pallas kernels, on_device(): call(final_kernel, [list(own), list(own)], 'v' * 27, [fine(3), fine(5)] +...  1.61 us
    ppermute x2, waiting for transfers between devices, parted(): return lax.ppermute(cells, ('pencil', 'coarse'), pairs)  1.35 us
  transfers between devices with their start and end apart: 5, of which 3 were waited for; matrix products, arithmetic and copies ran while one was open for 0% of the time, Pallas kernels for 8%

profile of v6, /device:TPU:1, one launch (start us, length us, event | category | flops | bytes accessed | tf_op | source)
XLA Modules:
  0.0 35.4 jit_solution(4499360002540283369)
XLA Ops:
  0.6 1.9 %shard_map.50 = (f32[8,16,256]{2,1,0:T(8,128)S(1)}, f32[8,16,256]{2,1,0:T(8,128)S(1)}, f32[8,16,256]{2,1,0:T(8,128)S(1)}, f32[22,8,256]{2,1,0:T(8,128)S(1)}, f32...) custom-call(f32[8,16,256]{2,1,0:T(8,128)} %u_hbm.1, f32[8,16,256]{2,1,0:T(8,128)} %k_hbm.1, f32[8,16,256]{2,1,0:T(8,128)} %f_hbm.1), custom_call_target="tpu_custom_call" | custom-call | flops 262144 | bytes 1048576 | tf_op jit(solution)/shard_map/pallas_call | solution.py:644
  2.5 7.6 %all-to-all-start = ((f32[16,3,8,128]{3,2,1,0:T(8,128)}), f32[16,3,8,128]{3,2,1,0:T(8,128)S(1)}, u32[]{:S(2)}, u32[]{:S(2)}) async-start(f32[16,3,8,128]{3,2,1,0:T(8,128)} %get-tuple-element.46), calls=%async_computation | async-start | bytes 393216 | tf_op jit(solution)/shard_map/all_to_all | solution.py:651
  10.1 1.3 %collective-permute-start = (f32[22,8,256]{2,1,0:T(8,128)S(1)}, f32[22,8,256]{2,1,0:T(8,128)S(1)}, u32[]{:S(2)}, u32[]{:S(2)}) collective-permute-start(f32[22,8,256]{2,1,0:T(8,128)S(1)} %get-tuple-element.55), channel_id=1, source_target_pairs={{0,1},{1,2},{2,3},{17,16},{18,17},{19,18},{32,33},{33,34},{34,35},... | collective-permute-start | bytes 540680 | tf_op jit(solution)/shard_map/ppermute | solution.py:630
  11.4 4.0 %collective-permute-start.1 = (f32[22,8,256]{2,1,0:T(8,128)S(1)}, f32[22,8,256]{2,1,0:T(8,128)S(1)}, u32[]{:S(2)}, u32[]{:S(2)}) collective-permute-start(f32[22,8,256]{2,1,0:T(8,128)S(1)} %get-tuple-element.56), channel_id=1, source_target_pairs={{1,0},{2,1},{3,2},{16,17},{17,18},{18,19},{33,32},{34,33},{35,34},... | collective-permute-start | bytes 540680 | tf_op jit(solution)/shard_map/ppermute | solution.py:630
  15.4 1.6 %all-to-all-done.z_ref = f32[16,3,8,128]{3,2,1,0:T(8,128)S(1)} async-done(((f32[16,3,8,128]{3,2,1,0:T(8,128)}), f32[16,3,8,128]{3,2,1,0:T(8,128)S(1)}, u32[]{:S(2)}, u32[]{:S(2)}) %all-to-all-start) | async-done | bytes 196640 | tf_op jit(solution)/shard_map/all_to_all | solution.py:651
  17.0 1.1 %shard_map.51 = (f32[8,16,384]{2,1,0:T(8,128)S(1)}, f32[8,16,384]{2,1,0:T(8,128)S(1)}, f32[8,16,384]{2,1,0:T(8,128)S(1)}, f32[4,8,384]{2,1,0:T(8,128)S(1)}, f32[...) custom-call(f32[8,16,256]{2,1,0:T(8,128)S(1)} %get-tuple-element.43.u_r, ...), custom_call_target="tpu_custom_call" | custom-call | flops 4194304 | bytes 3145728 | tf_op jit(solution)/shard_map/pallas_call | solution.py:663
  18.1 0.0 collective-permute-done.one_ref
  18.1 1.3 %collective-permute-done.1.two_ref = f32[22,8,256]{2,1,0:T(8,128)S(1)} collective-permute-done((f32[22,8,256]{2,1,0:T(8,128)S(1)}, f32[22,8,256]{2,1,0:T(8,128)S(1)}, u32[]{:S(2)}, u32[]{:S(2)}) %collective-permute-start.1) | collective-permute-done | bytes 180256 | tf_op jit(solution)/shard_map/ppermute | solution.py:630
  19.5 0.6 %shard_map.52 = (f32[2,32,384]{2,1,0:T(8,128)S(1)}, f32[2,32,384]{2,1,0:T(8,128)S(1)}, f32[8,24,384]{2,1,0:T(8,128)S(1)}, f32[8,24,384]{2,1,0:T(8,128)S(1)}, f32...) custom-call(f32[8,16,384]{2,1,0:T(8,128)S(1)} %get-tuple-element.47.u, ...), custom_call_target="tpu_custom_call" | custom-call | flops 4194304 | bytes 3145728 | tf_op jit(solution)/shard_map/pallas_call | solution.py:666
  20.0 6.4 %collective-permute-start.2 = (f32[27,8,256]{2,1,0:T(8,128)S(1)}, f32[27,8,256]{2,1,0:T(8,128)S(1)}, u32[]{:S(2)}, u32[]{:S(2)}) collective-permute-start(f32[27,8,256]{2,1,0:T(8,128)S(1)} %get-tuple-element.75), channel_id=1, source_target_pairs={{0,16},{16,0},{32,48},{48,32},{64,80},{80,64},{96,112},{112,96},{1... | collective-permute-start | bytes 663560 | tf_op jit(solution)/shard_map/ppermute | solution.py:638
  26.5 1.9 %collective-permute-start.3 = (f32[27,8,256]{2,1,0:T(8,128)S(1)}, f32[27,8,256]{2,1,0:T(8,128)S(1)}, u32[]{:S(2)}, u32[]{:S(2)}) collective-permute-start(f32[27,8,256]{2,1,0:T(8,128)S(1)} %get-tuple-element.83), channel_id=1, source_target_pairs={{16,32},{32,16},{48,64},{64,48},{80,96},{96,80},{112,128},{128,112... | collective-permute-start | bytes 663560 | tf_op jit(solution)/shard_map/ppermute | solution.py:638
  28.4 0.9 %shard_map.53 = (f32[8,24,384]{2,1,0:T(8,128)S(1)}, f32[8,24,384]{2,1,0:T(8,128)S(1)}, f32[8,24,384]{2,1,0:T(8,128)S(1)}, f32[8,24,384]{2,1,0:T(8,128)S(1)}, f32...) custom-call(f32[8,16,256]{2,1,0:T(8,128)S(1)} %get-tuple-element.43., ...), custom_call_target="tpu_custom_call" | custom-call | flops 4194304 | bytes 4194304 | tf_op jit(solution)/shard_map/pallas_call | solution.py:673
  29.3 0.0 collective-permute-done.2.msg_ref
  29.3 0.8 %shard_map.54 = (f32[2,16,256]{2,1,0:T(8,128)S(1)}, f32[3,16,256]{2,1,0:T(8,128)S(1)}, f32[5,16,384]{2,1,0:T(8,128)S(1)}, f32[5,16,384]{2,1,0:T(8,128)S(1)}, f32...) custom-call(f32[8,16,256]{2,1,0:T(8,128)S(1)} %get-tuple-element.43.u_ref, ...), custom_call_target="tpu_custom_call" | custom-call | flops 4194304 | bytes 4194304 | tf_op jit(solution)/shard_map/pallas_call | solution.py:677
  30.1 3.6 %collective-permute-done.3.msg_ref = f32[27,8,256]{2,1,0:T(8,128)S(1)} collective-permute-done((f32[27,8,256]{2,1,0:T(8,128)S(1)}, f32[27,8,256]{2,1,0:T(8,128)S(1)}, u32[]{:S(2)}, u32[]{:S(2)}) %collective-permute-start.3) | collective-permute-done | bytes 221216 | tf_op jit(solution)/shard_map/ppermute | solution.py:638
  33.8 1.6 %shard_map.55 = (f32[8,16,256]{2,1,0:T(8,128)}, f32[8,16,256]{2,1,0:T(8,128)}) custom-call(f32[8,16,256]{2,1,0:T(8,128)S(1)} %get-tuple-element.43.u_ref, f32[2,32,384]{2,1,0:T(8,128)S(1)} %get-tuple-element.57.uo_ref, f32[2,32,384]{2,1,0:T(8,128)S(1)} %get-tuple-element.58.ko_ref, f32[8,24,384]{2,1,0:T(8,128)S(1)} %get-tuple-element.59.k_ref, ...), custom_call_target="tpu_custom_call" | custom-call | flops 4194304 | bytes 4194304 | tf_op jit(solution)/shard_map/pallas_call | solution.py:683
Async XLA Ops:
  2.5 14.5 %all-to-all-start = ((f32[16,3,8,128]{3,2,1,0:T(8,128)}), f32[16,3,8,128]{3,2,1,0:T(8,128)S(1)}, u32[]{:S(2)}, u32[]{:S(2)}) async-start(f32[16,3,8,128]{3,2,1,0:T(8,128)} %get-tuple-element.46), calls=%async_computation | async-start | bytes 393216 | tf_op jit(solution)/shard_map/all_to_all | solution.py:651
  10.1 8.0 %collective-permute-start = (f32[22,8,256]{2,1,0:T(8,128)S(1)}, f32[22,8,256]{2,1,0:T(8,128)S(1)}, u32[]{:S(2)}, u32[]{:S(2)}) collective-permute-start(f32[22,8,256]{2,1,0:T(8,128)S(1)} %get-tuple-element.55), channel_id=1, source_target_pairs={{0,1},{1,2},{2,3},{17,16},{18,17},{19,18},{32,33},{33,34},{34,35},... | collective-permute-start | bytes 540680 | tf_op jit(solution)/shard_map/ppermute | solution.py:630
  11.4 8.0 %collective-permute-start.1 = (f32[22,8,256]{2,1,0:T(8,128)S(1)}, f32[22,8,256]{2,1,0:T(8,128)S(1)}, u32[]{:S(2)}, u32[]{:S(2)}) collective-permute-start(f32[22,8,256]{2,1,0:T(8,128)S(1)} %get-tuple-element.56), channel_id=1, source_target_pairs={{1,0},{2,1},{3,2},{16,17},{17,18},{18,19},{33,32},{34,33},{35,34},... | collective-permute-start | bytes 540680 | tf_op jit(solution)/shard_map/ppermute | solution.py:630
  20.0 9.2 %collective-permute-start.2 = (f32[27,8,256]{2,1,0:T(8,128)S(1)}, f32[27,8,256]{2,1,0:T(8,128)S(1)}, u32[]{:S(2)}, u32[]{:S(2)}) collective-permute-start(f32[27,8,256]{2,1,0:T(8,128)S(1)} %get-tuple-element.75), channel_id=1, source_target_pairs={{0,16},{16,0},{32,48},{48,32},{64,80},{80,64},{96,112},{112,96},{1... | collective-permute-start | bytes 663560 | tf_op jit(solution)/shard_map/ppermute | solution.py:638
  26.5 7.3 %collective-permute-start.3 = (f32[27,8,256]{2,1,0:T(8,128)S(1)}, f32[27,8,256]{2,1,0:T(8,128)S(1)}, u32[]{:S(2)}, u32[]{:S(2)}) collective-permute-start(f32[27,8,256]{2,1,0:T(8,128)S(1)} %get-tuple-element.83), channel_id=1, source_target_pairs={{16,32},{32,16},{48,64},{64,48},{80,96},{96,80},{112,128},{128,112... | collective-permute-start | bytes 663560 | tf_op jit(solution)/shard_map/ppermute | solution.py:638

commit v7 on v6

--- a/solution.py
+++ b/solution.py
@@ -49,12 +49,16 @@
             at = pl.ds(half * NX // 2, NX // 2)
             copies.append(pltpu.make_async_copy(far.at[at], near.at[at], own_sem.at[2 * i + half]))
             copies[-1].start()
-    for copy in copies:
-        copy.wait()
     group = lanes((H, 128)) // H
     sends = []
-    for side, (first, start, to_z) in enumerate(((NZ - 128, H, 1), (0, 0, 3))):
-        for tile in range(3):
+    faces = ((NZ - 128, H, 1), (0, 0, 3))
+    for copy in copies[:4]:
+        copy.wait()
+    for tile in (0, 2, 1):
+        if tile == 1:
+            for copy in copies[4:]:
+                copy.wait()
+        for side, (first, start, to_z) in enumerate(faces):
             packed = jnp.zeros((H, 128), f32)
             for q in range(16):
                 if tile == 1:
@@ -66,6 +70,7 @@
                 moved = pltpu.roll(cells, shift, 1) if shift else cells
                 packed = jnp.where(group == q, moved, packed)
             end_ref[side, tile] = packed
+    for side, (first, start, to_z) in enumerate(faces):
         z = lax.rem(gz + to_z, 4) * 4
         end = end_ref.at[side]
         for j, (src, dst) in enumerate((

time: 35.7 us -> 35.7 us (level)
  no operation moved by 1% of the time
where the time goes in v7:
time: 35.7 us; the launch traced here: 35.4 us
  starting transfers between devices  21.3 us (60%)
  Pallas kernels  6.86 us (19%)
  waiting for transfers between devices  6.57 us (18%)
  between operations  0.72 us (2%)
    ppermute x2, starting transfers between devices, swapped(): return lax.ppermute(cells, axis, pairs)  8.37 us
    all_to_all x1, starting transfers between devices, on_device(): ends = lax.all_to_all(ends, ('gz', 'coarse'), 0, 0)  7.6 us
    ppermute x2, starting transfers between devices, parted(): return lax.ppermute(cells, ('pencil', 'coarse'), pairs)  5.29 us
    ppermute x2, waiting for transfers between devices, swapped(): return lax.ppermute(cells, axis, pairs)  3.61 us
    pallas_call x1, Pallas kernels, on_device(): call(pack_kernel, [own, own, own, (GROUPS, H, NZ), (GROUPS, H, NZ), [16,...  1.93 us
    all_to_all x1, waiting for transfers between devices, on_device(): ends = lax.all_to_all(ends, ('gz', 'coarse'), 0, 0)  1.63 us
    pallas_call x1, Pallas kernels, on_device(): call(final_kernel, [list(own), list(own)], 'v' * 27, [fine(3), fine(5)] +...  1.61 us
    ppermute x2, waiting for transfers between devices, parted(): return lax.ppermute(cells, ('pencil', 'coarse'), pairs)  1.34 us
  transfers between devices with their start and end apart: 5, of which 3 were waited for; matrix products, arithmetic and copies ran while one was open for 0% of the time, Pallas kernels for 8%

profile of v7, /device:TPU:1, one launch (start us, length us, event | category | flops | bytes accessed | tf_op | source)
XLA Modules:
  0.0 35.4 jit_solution(488148589628737409)
XLA Ops:
  0.6 1.9 %shard_map.50 = (f32[8,16,256]{2,1,0:T(8,128)S(1)}, f32[8,16,256]{2,1,0:T(8,128)S(1)}, f32[8,16,256]{2,1,0:T(8,128)S(1)}, f32[22,8,256]{2,1,0:T(8,128)S(1)}, f32...) custom-call(f32[8,16,256]{2,1,0:T(8,128)} %u_hbm.1, f32[8,16,256]{2,1,0:T(8,128)} %k_hbm.1, f32[8,16,256]{2,1,0:T(8,128)} %f_hbm.1), custom_call_target="tpu_custom_call" | custom-call | flops 262144 | bytes 1048576 | tf_op jit(solution)/shard_map/pallas_call | solution.py:649
  2.6 7.6 %all-to-all-start = ((f32[16,3,8,128]{3,2,1,0:T(8,128)}), f32[16,3,8,128]{3,2,1,0:T(8,128)S(1)}, u32[]{:S(2)}, u32[]{:S(2)}) async-start(f32[16,3,8,128]{3,2,1,0:T(8,128)} %get-tuple-element.46), calls=%async_computation | async-start | bytes 393216 | tf_op jit(solution)/shard_map/all_to_all | solution.py:656
  10.2 1.3 %collective-permute-start = (f32[22,8,256]{2,1,0:T(8,128)S(1)}, f32[22,8,256]{2,1,0:T(8,128)S(1)}, u32[]{:S(2)}, u32[]{:S(2)}) collective-permute-start(f32[22,8,256]{2,1,0:T(8,128)S(1)} %get-tuple-element.55), channel_id=1, source_target_pairs={{0,1},{1,2},{2,3},{17,16},{18,17},{19,18},{32,33},{33,34},{34,35},... | collective-permute-start | bytes 540680 | tf_op jit(solution)/shard_map/ppermute | solution.py:635
  11.5 4.0 %collective-permute-start.1 = (f32[22,8,256]{2,1,0:T(8,128)S(1)}, f32[22,8,256]{2,1,0:T(8,128)S(1)}, u32[]{:S(2)}, u32[]{:S(2)}) collective-permute-start(f32[22,8,256]{2,1,0:T(8,128)S(1)} %get-tuple-element.56), channel_id=1, source_target_pairs={{1,0},{2,1},{3,2},{16,17},{17,18},{18,19},{33,32},{34,33},{35,34},... | collective-permute-start | bytes 540680 | tf_op jit(solution)/shard_map/ppermute | solution.py:635
  15.5 1.6 %all-to-all-done.z_ref = f32[16,3,8,128]{3,2,1,0:T(8,128)S(1)} async-done(((f32[16,3,8,128]{3,2,1,0:T(8,128)}), f32[16,3,8,128]{3,2,1,0:T(8,128)S(1)}, u32[]{:S(2)}, u32[]{:S(2)}) %all-to-all-start) | async-done | bytes 196640 | tf_op jit(solution)/shard_map/all_to_all | solution.py:656
  17.1 1.1 %shard_map.51 = (f32[8,16,384]{2,1,0:T(8,128)S(1)}, f32[8,16,384]{2,1,0:T(8,128)S(1)}, f32[8,16,384]{2,1,0:T(8,128)S(1)}, f32[4,8,384]{2,1,0:T(8,128)S(1)}, f32[...) custom-call(f32[8,16,256]{2,1,0:T(8,128)S(1)} %get-tuple-element.43.u_r, ...), custom_call_target="tpu_custom_call" | custom-call | flops 4194304 | bytes 3145728 | tf_op jit(solution)/shard_map/pallas_call | solution.py:668
  18.2 0.0 collective-permute-done.one_ref
  18.2 1.3 %collective-permute-done.1.two_ref = f32[22,8,256]{2,1,0:T(8,128)S(1)} collective-permute-done((f32[22,8,256]{2,1,0:T(8,128)S(1)}, f32[22,8,256]{2,1,0:T(8,128)S(1)}, u32[]{:S(2)}, u32[]{:S(2)}) %collective-permute-start.1) | collective-permute-done | bytes 180256 | tf_op jit(solution)/shard_map/ppermute | solution.py:635
  19.5 0.6 %shard_map.52 = (f32[2,32,384]{2,1,0:T(8,128)S(1)}, f32[2,32,384]{2,1,0:T(8,128)S(1)}, f32[8,24,384]{2,1,0:T(8,128)S(1)}, f32[8,24,384]{2,1,0:T(8,128)S(1)}, f32...) custom-call(f32[8,16,384]{2,1,0:T(8,128)S(1)} %get-tuple-element.47.u, ...), custom_call_target="tpu_custom_call" | custom-call | flops 4194304 | bytes 3145728 | tf_op jit(solution)/shard_map/pallas_call | solution.py:671
  20.1 6.4 %collective-permute-start.2 = (f32[27,8,256]{2,1,0:T(8,128)S(1)}, f32[27,8,256]{2,1,0:T(8,128)S(1)}, u32[]{:S(2)}, u32[]{:S(2)}) collective-permute-start(f32[27,8,256]{2,1,0:T(8,128)S(1)} %get-tuple-element.75), channel_id=1, source_target_pairs={{0,16},{16,0},{32,48},{48,32},{64,80},{80,64},{96,112},{112,96},{1... | collective-permute-start | bytes 663560 | tf_op jit(solution)/shard_map/ppermute | solution.py:643
  26.5 1.9 %collective-permute-start.3 = (f32[27,8,256]{2,1,0:T(8,128)S(1)}, f32[27,8,256]{2,1,0:T(8,128)S(1)}, u32[]{:S(2)}, u32[]{:S(2)}) collective-permute-start(f32[27,8,256]{2,1,0:T(8,128)S(1)} %get-tuple-element.83), channel_id=1, source_target_pairs={{16,32},{32,16},{48,64},{64,48},{80,96},{96,80},{112,128},{128,112... | collective-permute-start | bytes 663560 | tf_op jit(solution)/shard_map/ppermute | solution.py:643
  28.5 0.9 %shard_map.53 = (f32[8,24,384]{2,1,0:T(8,128)S(1)}, f32[8,24,384]{2,1,0:T(8,128)S(1)}, f32[8,24,384]{2,1,0:T(8,128)S(1)}, f32[8,24,384]{2,1,0:T(8,128)S(1)}, f32...) custom-call(f32[8,16,256]{2,1,0:T(8,128)S(1)} %get-tuple-element.43., ...), custom_call_target="tpu_custom_call" | custom-call | flops 4194304 | bytes 4194304 | tf_op jit(solution)/shard_map/pallas_call | solution.py:678
  29.3 0.0 collective-permute-done.2.msg_ref
  29.3 0.8 %shard_map.54 = (f32[2,16,256]{2,1,0:T(8,128)S(1)}, f32[3,16,256]{2,1,0:T(8,128)S(1)}, f32[5,16,384]{2,1,0:T(8,128)S(1)}, f32[5,16,384]{2,1,0:T(8,128)S(1)}, f32...) custom-call(f32[8,16,256]{2,1,0:T(8,128)S(1)} %get-tuple-element.43.u_ref, ...), custom_call_target="tpu_custom_call" | custom-call | flops 4194304 | bytes 4194304 | tf_op jit(solution)/shard_map/pallas_call | solution.py:682
  30.2 3.6 %collective-permute-done.3.msg_ref = f32[27,8,256]{2,1,0:T(8,128)S(1)} collective-permute-done((f32[27,8,256]{2,1,0:T(8,128)S(1)}, f32[27,8,256]{2,1,0:T(8,128)S(1)}, u32[]{:S(2)}, u32[]{:S(2)}) %collective-permute-start.3) | collective-permute-done | bytes 221216 | tf_op jit(solution)/shard_map/ppermute | solution.py:643
  33.8 1.6 %shard_map.55 = (f32[8,16,256]{2,1,0:T(8,128)}, f32[8,16,256]{2,1,0:T(8,128)}) custom-call(f32[8,16,256]{2,1,0:T(8,128)S(1)} %get-tuple-element.43.u_ref, f32[2,32,384]{2,1,0:T(8,128)S(1)} %get-tuple-element.57.uo_ref, f32[2,32,384]{2,1,0:T(8,128)S(1)} %get-tuple-element.58.ko_ref, f32[8,24,384]{2,1,0:T(8,128)S(1)} %get-tuple-element.59.k_ref, ...), custom_call_target="tpu_custom_call" | custom-call | flops 4194304 | bytes 4194304 | tf_op jit(solution)/shard_map/pallas_call | solution.py:688
Async XLA Ops:
  2.6 14.5 %all-to-all-start = ((f32[16,3,8,128]{3,2,1,0:T(8,128)}), f32[16,3,8,128]{3,2,1,0:T(8,128)S(1)}, u32[]{:S(2)}, u32[]{:S(2)}) async-start(f32[16,3,8,128]{3,2,1,0:T(8,128)} %get-tuple-element.46), calls=%async_computation | async-start | bytes 393216 | tf_op jit(solution)/shard_map/all_to_all | solution.py:656
  10.2 8.0 %collective-permute-start = (f32[22,8,256]{2,1,0:T(8,128)S(1)}, f32[22,8,256]{2,1,0:T(8,128)S(1)}, u32[]{:S(2)}, u32[]{:S(2)}) collective-permute-start(f32[22,8,256]{2,1,0:T(8,128)S(1)} %get-tuple-element.55), channel_id=1, source_target_pairs={{0,1},{1,2},{2,3},{17,16},{18,17},{19,18},{32,33},{33,34},{34,35},... | collective-permute-start | bytes 540680 | tf_op jit(solution)/shard_map/ppermute | solution.py:635
  11.5 8.0 %collective-permute-start.1 = (f32[22,8,256]{2,1,0:T(8,128)S(1)}, f32[22,8,256]{2,1,0:T(8,128)S(1)}, u32[]{:S(2)}, u32[]{:S(2)}) collective-permute-start(f32[22,8,256]{2,1,0:T(8,128)S(1)} %get-tuple-element.56), channel_id=1, source_target_pairs={{1,0},{2,1},{3,2},{16,17},{17,18},{18,19},{33,32},{34,33},{35,34},... | collective-permute-start | bytes 540680 | tf_op jit(solution)/shard_map/ppermute | solution.py:635
  20.1 9.2 %collective-permute-start.2 = (f32[27,8,256]{2,1,0:T(8,128)S(1)}, f32[27,8,256]{2,1,0:T(8,128)S(1)}, u32[]{:S(2)}, u32[]{:S(2)}) collective-permute-start(f32[27,8,256]{2,1,0:T(8,128)S(1)} %get-tuple-element.75), channel_id=1, source_target_pairs={{0,16},{16,0},{32,48},{48,32},{64,80},{80,64},{96,112},{112,96},{1... | collective-permute-start | bytes 663560 | tf_op jit(solution)/shard_map/ppermute | solution.py:643
  26.5 7.3 %collective-permute-start.3 = (f32[27,8,256]{2,1,0:T(8,128)S(1)}, f32[27,8,256]{2,1,0:T(8,128)S(1)}, u32[]{:S(2)}, u32[]{:S(2)}) collective-permute-start(f32[27,8,256]{2,1,0:T(8,128)S(1)} %get-tuple-element.83), channel_id=1, source_target_pairs={{16,32},{32,16},{48,64},{64,48},{80,96},{96,80},{112,128},{128,112... | collective-permute-start | bytes 663560 | tf_op jit(solution)/shard_map/ppermute | solution.py:643
